TPU v7x, 256 devices: a whole 4x4x8 slice. The times are simulated.
256 devices in a mesh: dom: 32 (over y, z), band: 8 (over x, core).
Axes of the slice: x: 4, y: 4, z: 8, core: 2. Of those that a mesh axis runs over, the one named last changes fastest.
Arguments:
- orbitals: float32 [32, 128, 24, 576], P('dom', 'band'), may hold values from -6 to 6
- potential: float32 [32, 24, 576], P('dom'), may hold values from 0 to 3
- density_in: float32 [32, 24, 576], P('dom', 'band'), may hold values from 0.3 to 3
- occupation: float32 [128], replicated, may hold values from 0.5 to 2
- position: int32 [32], replicated, may hold values from 0 to 31, each once
- mixing: int32 [2], replicated, may hold values from 1 to 8
- correlation_weight: int32 [6], replicated, may hold values from 1 to 15
Outputs:
- orbitals_out: float32 [32, 128, 24, 576], P('dom', None, 'band')
- density: float32 [32, 24, 576], P('dom', 'band')
- hartree: float32 [32, 8, 8, 6], P('dom', 'band')
Inputs may be any that keep to these rules, and one draw needn't show every extreme that they name: position is a permutation: every place along the chain holds exactly one domain.
All inputs are finite; a program needn't handle non-finite values.
Results may differ from a plain program's by a relative error of at most 0.0001.
Values sent between devices are 32-bit elements; how exact they have to be, the bound alone decides.
No kernel may reach another device: no remote copies, remote signals or barrier semaphores. Data moves between devices by JAX's collectives and lax.ppermute only.
A program may use at most 64 MiB of HBM per device.

v0:
```python
import jax
import jax.numpy as jnp
from jax import lax
from jax.sharding import PartitionSpec as P

G = 24
BUFFER = 6
COARSEN = 3
NS_STEPS = 2
CG = 8
CZ = 6


HIGHEST = lax.Precision.HIGHEST
filter_low = 1.0
filter_high = 9.5
blend_total = 16.0


def total_of_pieces(x, axis):
    tiles = lax.all_gather(x, axis)
    return tiles.sum(axis=0)


def from_everyone(x, axis):
    copies = jnp.broadcast_to(x, (lax.axis_size(axis), *x.shape))
    return lax.all_to_all(copies, axis, split_axis=0, concat_axis=0, tiled=True)


def joined_along(tiles, dim):
    tiles = jnp.moveaxis(tiles, 0, dim)
    dims = tiles.shape
    return tiles.reshape(*dims[:dim], dims[dim] * dims[dim + 1], *dims[dim + 2 :])


def gathered_copies(x, axis, dim):
    tiles = from_everyone(x, axis)
    return joined_along(tiles, dim)


def split_up(x, dim, size):
    dims = x.shape
    tiles = x.reshape(*dims[:dim], size, dims[dim] // size, *dims[dim + 1 :])
    return jnp.moveaxis(tiles, dim, 0)


def summed_on_arrival(x, axis, dim):
    tiles = split_up(x, dim, lax.axis_size(axis))
    arrived = lax.all_to_all(tiles, axis, split_axis=0, concat_axis=0, tiled=True)
    return arrived.sum(axis=0)


def sine_entries(row_values, col_values, extent):
    products = (row_values[:, None] + 1.0) * (col_values[None, :] + 1.0)
    return jnp.sqrt(2.0 / (extent + 1.0)) * jnp.sin(jnp.pi * products / (extent + 1.0))


def sine_table(extent):
    indices = jnp.arange(extent, dtype=jnp.float32)
    return sine_entries(indices, indices, extent)


def cosine_table(extent):
    indices = jnp.arange(extent, dtype=jnp.float32)
    entries = jnp.sqrt(2.0 / extent) * jnp.cos(
        jnp.pi * indices[:, None] * (indices[None, :] + 0.5) / extent
    )
    return entries * jnp.where(indices == 0.0, jnp.sqrt(0.5), 1.0)[:, None]


def lap_eigen(indices, extent, shift_by):
    half_angle = 0.5 * jnp.pi * (indices + shift_by) / (extent + shift_by)
    return 4.0 * jnp.sin(half_angle) ** 2


def kinetic_table(extent):
    indices = jnp.arange(extent, dtype=jnp.float32)
    single = 0.5 * lap_eigen(indices, extent, 1.0)
    plane_values = single[:, None] + single[None, :]
    return single[:, None] + plane_values.reshape(1, extent * extent)


def transform(values, sine_matrix, plane_matrix):
    values = jnp.einsum("bxc,xk->bkc", values, sine_matrix, precision=HIGHEST)
    return jnp.einsum("bxc,cd->bxd", values, plane_matrix, precision=HIGHEST)


def apply_hamil(values, potential_grid, sine_matrix, plane_matrix, kinetic):
    spectral = kinetic * transform(values, sine_matrix, plane_matrix)
    return transform(spectral, sine_matrix, plane_matrix) + potential_grid * values


def chebyshev(orbital_block, potential_grid, sine_matrix, plane_matrix, kinetic):
    center = 0.5 * (filter_high + filter_low)
    half_width = 0.5 * (filter_high - filter_low)

    def shifted(values):
        return (
            apply_hamil(values, potential_grid, sine_matrix, plane_matrix, kinetic)
            - center * values
        ) / half_width

    before = orbital_block
    current = shifted(orbital_block)
    newest = 2.0 * shifted(current) - before
    before, current = (current, newest)
    return current


def body(orbitals, potential, density_in, occupation, position, mixing, correlation_weight):
    nbands = occupation.shape[0]
    dom_count = lax.axis_size("dom")
    planes_local = density_in.shape[1]
    sine_matrix = sine_table(G)
    plane_matrix = jnp.kron(sine_matrix, sine_matrix)
    kinetic = kinetic_table(G)
    potential_grid = potential[0]
    points = float(G * G * G)
    filtered = chebyshev(orbitals[0], potential_grid, sine_matrix, plane_matrix, kinetic)
    regrouped = lax.all_to_all(filtered, "band", split_axis=1, concat_axis=0, tiled=True)
    flat_orbitals = regrouped.reshape(nbands, planes_local * G * G)
    local_raw = jnp.dot(flat_orbitals, flat_orbitals.T, precision=HIGHEST)
    correlation_raw = total_of_pieces(local_raw, "band")
    norm_fro = jnp.sqrt(jnp.sum(correlation_raw * correlation_raw))
    scaling = jnp.sqrt(points / norm_fro)
    poly_matrix = scaling * jnp.eye(nbands, dtype=jnp.float32)
    correlation = correlation_raw / norm_fro
    for iteration in range(NS_STEPS):
        if iteration > 0:
            inner_product = jnp.dot(poly_matrix, correlation_raw, precision=HIGHEST)
            correlation = jnp.dot(inner_product, poly_matrix.T, precision=HIGHEST) / points
        poly_matrix = 1.5 * poly_matrix - 0.5 * jnp.dot(correlation, poly_matrix, precision=HIGHEST)
    current = jnp.dot(poly_matrix, flat_orbitals, precision=HIGHEST)
    density_local = jnp.dot(occupation, current * current, precision=HIGHEST) / nbands
    orbitals_out = current.reshape(1, nbands, planes_local, G * G)
    fresh_cube = density_local.reshape(planes_local, G, G)
    own_low = fresh_cube[:, :, :BUFFER]
    own_high = fresh_cube[:, :, G - BUFFER :]
    edge_slabs = jnp.stack([own_low, own_high], 0)
    everyone = gathered_copies(edge_slabs, "dom", 0).reshape(dom_count, 2, planes_local, G, BUFFER)
    dom_index = lax.axis_index("dom")
    own_place = position[dom_index]
    left_pick = (position == own_place - 1).astype(jnp.float32)
    right_pick = (position == own_place + 1).astype(jnp.float32)
    left_high = jnp.einsum("d,dxyb->xyb", left_pick, everyone[:, 1], precision=HIGHEST)
    right_low = jnp.einsum("d,dxyb->xyb", right_pick, everyone[:, 0], precision=HIGHEST)
    weight_left = correlation_weight.astype(jnp.float32)
    blend_low = jnp.where(
        own_place > 0,
        (weight_left * left_high + (blend_total - weight_left) * own_low) / blend_total,
        own_low,
    )
    blend_high = jnp.where(
        own_place < dom_count - 1,
        (weight_left * own_high + (blend_total - weight_left) * right_low) / blend_total,
        own_high,
    )
    blended = jnp.concatenate([blend_low, fresh_cube[:, :, BUFFER : G - BUFFER], blend_high], 2)
    mix_weights = mixing.astype(jnp.float32)
    inflow = density_in[0].reshape(planes_local, G, G)
    mixed_density = (mix_weights[0] * blended + mix_weights[1] * inflow) / (
        mix_weights[0] + mix_weights[1]
    )
    density_out = mixed_density.reshape(1, planes_local, G * G)
    coarse_x = planes_local // COARSEN
    core_cells = mixed_density[:, :, : G - BUFFER].reshape(
        coarse_x, COARSEN, CG, COARSEN, CZ, COARSEN
    )
    coarse = jnp.sum(core_cells, axis=(1, 3, 5)) / float(COARSEN**3)
    chain_length = dom_count * CZ
    cross_table = jnp.kron(cosine_table(CG), cosine_table(CG))
    level_x = lap_eigen(jnp.arange(CG, dtype=jnp.float32), CG, 0.0)
    level_xy = (level_x[:, None] + level_x[None, :]).reshape(CG * CG)
    source_scale = 8.0 / float(chain_length * chain_length)
    band_index = lax.axis_index("band")
    whole_domain = gathered_copies(coarse, "band", 0)
    transformed = jnp.dot(cross_table, whole_domain.reshape(CG * CG, CZ), precision=HIGHEST)
    rows_mine = (own_place * CZ + jnp.arange(CZ, dtype=jnp.int32)).astype(jnp.float32)
    all_kz = jnp.arange(chain_length, dtype=jnp.float32)
    sine_mine = sine_entries(rows_mine, all_kz, chain_length)
    spectrum = summed_on_arrival(jnp.dot(sine_mine.T, transformed.T, precision=HIGHEST), "dom", 0)
    kz_mine = (dom_index * CZ + jnp.arange(CZ, dtype=jnp.int32)).astype(jnp.float32)
    level_z = lap_eigen(kz_mine, chain_length, 1.0)
    spectrum = spectrum / (level_z[:, None] + level_xy[None, :])
    row_ids = jnp.arange(chain_length, dtype=jnp.int32)
    owners = row_ids // CZ
    placed = jnp.sum(
        jnp.where(
            owners[:, None] == jnp.arange(dom_count, dtype=jnp.int32)[None, :], position[None, :], 0
        ),
        axis=1,
    )
    chain_rows = (placed * CZ + row_ids % CZ).astype(jnp.float32)
    field_rows = summed_on_arrival(
        jnp.dot(sine_entries(chain_rows, kz_mine, chain_length), spectrum, precision=HIGHEST),
        "dom",
        0,
    )
    own_block = jnp.dot(cross_table.T, field_rows.T, precision=HIGHEST) * source_scale
    own_block = own_block.reshape(CG, CG, CZ)
    hartree = lax.dynamic_slice_in_dim(own_block, band_index * coarse_x, coarse_x, 0).reshape(
        1, coarse_x, CG, CZ
    )
    return (orbitals_out, density_out, hartree)


def solution(mesh):
    return jax.shard_map(
        body,
        mesh=mesh,
        in_specs=(
            P("dom", "band", None, None),
            P("dom", None, None),
            P("dom", "band", None),
            P(),
            P(),
            P(),
            P(),
        ),
        out_specs=(
            P("dom", None, "band", None),
            P("dom", "band", None),
            P("dom", "band", None, None),
        ),
        check_vma=False,
    )
```

profile of v0, /device:TPU:1, one launch (start us, length us, event | category | flops | bytes accessed | tf_op | source)
XLA Modules:
  0.0 137.5 jit_solution(5844069615576071497)
XLA Ops:
  0.9 3.8 %broadcast_multiply_fusion = f32[24,24,24,24]{3,2,1,0:T(8,128)} fusion(f32[24,24]{1,0:T(8,128)S(1)} %copy.56), kind=kLoop, calls=%fused_computation | loop fusion | flops 331776 | bytes 1329408 | tf_op jit(solution)/shard_map/jit(kron)/mul | solution.py:115
  4.7 4.8 %reshape.392 = f32[576,576,1]{1,0,2:T(8,128)S(1)} reshape(f32[24,24,24,24]{3,2,1,0:T(8,128)} %broadcast_multiply_fusion) | data formatting | bytes 2654208 | tf_op jit(solution)/shard_map/jit(kron)/mul | solution.py:115
  9.4 1.0 convolution_bitcast_fusion.3
  10.7 2.9 %convolution_multiply_fusion.1 = f32[16,24,576]{2,1,0:T(8,128)S(1)} fusion(f32[16,24,576]{2,1,0:T(8,128)S(1)} %convolution_bitcast_fusion.3, f32[576,576,1]{1,0,2:T(8,128)S(1)} %reshape.392, f32[24,576]{1,0:T(8,128)S(1)} %broadcast_add_fusion), kind=kOutput, calls=%fused_computation.12 | convolution fusion | flops 1529044992 | bytes 3151872 | tf_op jit(solution)/shard_map/bxc,cd->bxd/dot_general | solution.py:85
  13.6 1.0 convolution_bitcast_fusion.2
  14.7 2.9 %fusion.3 = f32[16,24,576]{2,1,0:T(8,128)S(1)} fusion(f32[16,24,576]{2,1,0:T(8,128)S(1)} %convolution_bitcast_fusion.2, f32[576,576,1]{1,0,2:T(8,128)S(1)} %reshape.392, f32[1,16,24,576]{3,2,1,0:T(8,128)S(1)} %copy-done.1, f32[24,576]{1,0:T(8,128)S(1)} %bitcast.128), kind=kOutput, calls=%fused_computation.11 | convolution fusion | flops 1529708544 | bytes 4036608 | tf_op jit(solution)/shard_map/bxc,cd->bxd/dot_general | solution.py:85
  17.6 1.0 convolution_bitcast_fusion.1
  18.6 2.9 %convolution_multiply_fusion = f32[16,24,576]{2,1,0:T(8,128)S(1)} fusion(f32[16,24,576]{2,1,0:T(8,128)S(1)} %convolution_bitcast_fusion.1, f32[576,576,1]{1,0,2:T(8,128)S(1)} %reshape.392, f32[24,576]{1,0:T(8,128)S(1)} %broadcast_add_fusion), kind=kOutput, calls=%fused_computation.9 | convolution fusion | flops 1529044992 | bytes 3151872 | tf_op jit(solution)/shard_map/bxc,cd->bxd/dot_general | solution.py:85
  21.5 1.0 convolution_bitcast_fusion
  22.6 3.1 %fusion.2 = f32[16,24,576]{2,1,0:T(8,128)S(1)} fusion(f32[16,24,576]{2,1,0:T(8,128)S(1)} %convolution_bitcast_fusion, f32[576,576,1]{1,0,2:T(8,128)S(1)} %reshape.392, f32[1,16,24,576]{3,2,1,0:T(8,128)S(1)} %copy-done.1, f32[16,24,576]{2,1,0:T(8,128)S(1)} %fusion.3, f32[24,576]{1,0:T(8,128)S(1)} %broadcast_multiply_fusion.2), kind=kOutput, calls=%fused_computation.8 | convolution fusion | flops 1530150912 | bytes 4921344 | tf_op jit(solution)/shard_map/bxc,cd->bxd/dot_general | solution.py:85
  25.6 1.1 copy.58
  26.8 6.8 %all-to-all-start = ((f32[16,24,576]{2,0,1:T(8,128)}), f32[16,24,576]{2,0,1:T(8,128)S(1)}, u32[]{:S(2)}, u32[]{:S(2)}) async-start(f32[16,24,576]{2,0,1:T(8,128)} %copy.58), calls=%async_computation | async-start | bytes 1966080 | tf_op jit(solution)/shard_map/all_to_all | solution.py:120
  33.6 0.6 dynamic_slice.6
  36.9 0.6 fusion.97
  39.7 8.1 %all-to-all-done = f32[16,24,576]{2,0,1:T(8,128)S(1)} async-done(((f32[16,24,576]{2,0,1:T(8,128)}), f32[16,24,576]{2,0,1:T(8,128)S(1)}, u32[]{:S(2)}, u32[]{:S(2)}) %all-to-all-start) | async-done | bytes 884768 | tf_op jit(solution)/shard_map/all_to_all | solution.py:120
  47.9 0.5 copy.59
  48.4 0.7 reshape.383
  49.1 0.9 fusion.98
  50.0 13.9 %all-gather = f32[1024,128]{1,0:T(8,128)S(1)} all-gather(f32[128,128]{1,0:T(8,128)S(1)} %fusion.98), channel_id=2, replica_groups=mesh['dom'=32,'band'=8] {'band'}, dimensions={0}, use_global_device_ids=true | all-gather | bytes 589824 | tf_op jit(solution)/shard_map/all_gather | solution.py:21
  63.9 0.6 multiply_reduce_fusion
  66.2 1.6 %fusion.100 = f32[128,1728]{0,1:T(8,128)S(1)} fusion(f32[128,128]{1,0:T(8,128)S(1)} %fusion.4, f32[128,1728]{1,0:T(8,128)S(1)} %reshape.383), kind=kOutput, calls=%fused_computation.157 | convolution fusion | flops 339738624 | bytes 1835008 | tf_op jit(solution)/shard_map/dot_general | solution.py:133
  67.9 1.0 convolution_reduce_fusion
  69.4 1.3 reshape.401
  70.7 10.5 %all-to-all-start.1 = ((f32[32,1,864]{2,1,0:T(1,128)}), f32[32,1,864]{2,1,0:T(1,128)S(1)}, u32[]{:S(2)}, u32[]{:S(2)}) async-start(f32[32,1,864]{2,1,0:T(1,128)} %reshape.401), calls=%async_computation.1 | async-start | bytes 229376 | tf_op jit(solution)/shard_map/all_to_all | solution.py:27
  81.3 8.8 %all-to-all-done.1 = f32[32,1,864]{2,1,0:T(1,128)S(1)} async-done(((f32[32,1,864]{2,1,0:T(1,128)}), f32[32,1,864]{2,1,0:T(1,128)S(1)}, u32[]{:S(2)}, u32[]{:S(2)}) %all-to-all-start.1) | async-done | bytes 110624 | tf_op jit(solution)/shard_map/all_to_all | solution.py:27
  90.1 0.5 broadcast.479
  90.6 0.9 reduce.5
  91.6 0.5 reshape.402
  92.1 0.5 fusion.96
  92.7 0.7 fusion.10
  93.7 0.7 fusion.12
  94.6 0.6 maximum_multiply_fusion
  95.3 0.7 copy_multiply_fusion
  96.4 0.6 broadcast_in_dim.35
  97.0 5.2 %all-to-all-start.2 = ((f32[8,1,8,6]{2,1,3,0:T(1,128)}), f32[8,1,8,6]{2,1,3,0:T(1,128)S(1)}, u32[]{:S(2)}, u32[]{:S(2)}) async-start(f32[8,1,8,6]{2,1,3,0:T(1,128)} %broadcast_in_dim.35), calls=%async_computation.2 | async-start | bytes 49152 | tf_op jit(solution)/shard_map/all_to_all | solution.py:27
  102.3 4.5 %all-to-all-done.2 = f32[8,1,8,6]{2,1,3,0:T(1,128)S(1)} async-done(((f32[8,1,8,6]{2,1,3,0:T(1,128)}), f32[8,1,8,6]{2,1,3,0:T(1,128)S(1)}, u32[]{:S(2)}, u32[]{:S(2)}) %all-to-all-start.2) | async-done | bytes 1568 | tf_op jit(solution)/shard_map/all_to_all | solution.py:27
  107.1 0.5 fusion.31
  107.6 0.7 reshape.403
  108.3 3.9 %all-to-all-start.3 = ((f32[32,1,384]{2,1,0:T(1,128)}), f32[32,1,384]{2,1,0:T(1,128)S(1)}, u32[]{:S(2)}, u32[]{:S(2)}) async-start(f32[32,1,384]{2,1,0:T(1,128)} %reshape.403), calls=%async_computation.3 | async-start | bytes 98304 | tf_op jit(solution)/shard_map/all_to_all | solution.py:49
  112.2 8.7 %all-to-all-done.3 = f32[32,1,384]{2,1,0:T(1,128)S(1)} async-done(((f32[32,1,384]{2,1,0:T(1,128)}), f32[32,1,384]{2,1,0:T(1,128)S(1)}, u32[]{:S(2)}, u32[]{:S(2)}) %all-to-all-start.3) | async-done | bytes 49184 | tf_op jit(solution)/shard_map/all_to_all | solution.py:49
  121.0 0.8 reduce.6
  121.9 0.5 fusion.36
  122.4 0.7 reshape.405
  123.1 3.9 %all-to-all-start.4 = ((f32[32,1,384]{2,1,0:T(1,128)}), f32[32,1,384]{2,1,0:T(1,128)S(1)}, u32[]{:S(2)}, u32[]{:S(2)}) async-start(f32[32,1,384]{2,1,0:T(1,128)} %reshape.405), calls=%async_computation.4 | async-start | bytes 98304 | tf_op jit(solution)/shard_map/all_to_all | solution.py:49
  127.0 0.6 copy.69
  127.6 8.2 %all-to-all-done.4 = f32[32,1,384]{2,1,0:T(1,128)S(1)} async-done(((f32[32,1,384]{2,1,0:T(1,128)}), f32[32,1,384]{2,1,0:T(1,128)S(1)}, u32[]{:S(2)}, u32[]{:S(2)}) %all-to-all-start.4) | async-done | bytes 49184 | tf_op jit(solution)/shard_map/all_to_all | solution.py:49
  135.8 0.8 reduce.7
  136.9 0.6 dynamic-slice_bitcast_fusion
  (77 shorter events, 4.6 us)
Async XLA Ops:
  0.6 67.2 %copy-start = (f32[128]{0:T(128)S(1)}, f32[128]{0:T(128)}, u32[]{:S(2)}) copy-start(f32[128]{0:T(128)} %param.10) | copy-start | bytes 1540
  4.7 4.8 %copy-start.1 = (f32[1,16,24,576]{3,2,1,0:T(8,128)S(1)}, f32[1,16,24,576]{3,2,1,0:T(8,128)}, u32[]{:S(2)}) copy-start(f32[1,16,24,576]{3,2,1,0:T(8,128)} %param.7) | copy-start | bytes 2654212
  13.6 1.1 copy-start.3
  26.8 6.9 %copy-start.5 = (s32[32]{0:T(128)S(1)}, s32[32]{0:T(128)}, u32[]{:S(2)}) copy-start(s32[32]{0:T(128)} %param.11) | copy-start | bytes 388
  26.8 10.0 %copy-start.7 = (s32[6]{0:T(128)S(1)}, s32[6]{0:T(128)}, u32[]{:S(2)}) copy-start(s32[6]{0:T(128)} %param.13) | copy-start | bytes 76
  26.8 10.1 %copy-start.6 = (s32[2]{0:T(128)S(1)}, s32[2]{0:T(128)}, u32[]{:S(2)}) copy-start(s32[2]{0:T(128)} %param.12) | copy-start | bytes 28
  26.8 21.1 %all-to-all-start = ((f32[16,24,576]{2,0,1:T(8,128)}), f32[16,24,576]{2,0,1:T(8,128)S(1)}, u32[]{:S(2)}, u32[]{:S(2)}) async-start(f32[16,24,576]{2,0,1:T(8,128)} %copy.58), calls=%async_computation | async-start | bytes 1966080 | tf_op jit(solution)/shard_map/all_to_all | solution.py:120
  67.9 23.7 %copy-start.2 = (f32[128,1728]{0,1:T(8,128)}, f32[128,1728]{0,1:T(8,128)S(1)}, u32[]{:S(2)}) copy-start(f32[128,1728]{0,1:T(8,128)S(1)} %fusion.100) | copy-start | bytes 2654212
  70.7 19.4 %all-to-all-start.1 = ((f32[32,1,864]{2,1,0:T(1,128)}), f32[32,1,864]{2,1,0:T(1,128)S(1)}, u32[]{:S(2)}, u32[]{:S(2)}) async-start(f32[32,1,864]{2,1,0:T(1,128)} %reshape.401), calls=%async_computation.1 | async-start | bytes 229376 | tf_op jit(solution)/shard_map/all_to_all | solution.py:27
  92.1 3.2 %copy-start.4 = (f32[1,3,576]{2,0,1:T(1,128)S(1)}, f32[1,3,576]{2,0,1:T(1,128)}, u32[]{:S(2)}) copy-start(f32[1,3,576]{2,0,1:T(1,128)} %param.9) | copy-start | bytes 20740
  97.0 9.9 %all-to-all-start.2 = ((f32[8,1,8,6]{2,1,3,0:T(1,128)}), f32[8,1,8,6]{2,1,3,0:T(1,128)S(1)}, u32[]{:S(2)}, u32[]{:S(2)}) async-start(f32[8,1,8,6]{2,1,3,0:T(1,128)} %broadcast_in_dim.35), calls=%async_computation.2 | async-start | bytes 49152 | tf_op jit(solution)/shard_map/all_to_all | solution.py:27
  108.3 12.7 %all-to-all-start.3 = ((f32[32,1,384]{2,1,0:T(1,128)}), f32[32,1,384]{2,1,0:T(1,128)S(1)}, u32[]{:S(2)}, u32[]{:S(2)}) async-start(f32[32,1,384]{2,1,0:T(1,128)} %reshape.403), calls=%async_computation.3 | async-start | bytes 98304 | tf_op jit(solution)/shard_map/all_to_all | solution.py:49
  123.1 12.7 %all-to-all-start.4 = ((f32[32,1,384]{2,1,0:T(1,128)}), f32[32,1,384]{2,1,0:T(1,128)S(1)}, u32[]{:S(2)}, u32[]{:S(2)}) async-start(f32[32,1,384]{2,1,0:T(1,128)} %reshape.405), calls=%async_computation.4 | async-start | bytes 98304 | tf_op jit(solution)/shard_map/all_to_all | solution.py:49
where the time goes:
time: 139 us; the launch traced here: 137 us
  waiting for transfers between devices  38.3 us (28%)
  starting transfers between devices  30.2 us (22%)
  matrix products  22.8 us (16%)
  local copies, waits for them, and re-layouts  16.6 us (12%)
  blocking collectives  13.9 us (10%)
  other arithmetic  9.34 us (7%)
  between operations  6.34 us (5%)
    all_to_all x2, waiting for transfers between devices, summed_on_arrival(): lax.all_to_all(tiles, axis, split_axis=0, concat_axis=0, tiled=True)  16.9 us
    all_to_all x2, starting transfers between devices, from_everyone(): return lax.all_to_all(copies, axis, split_axis=0, concat_axis=0, tiled=True)  15.7 us
    all_gather x1, blocking collectives, total_of_pieces(): tiles = lax.all_gather(x, axis)  13.9 us
    all_to_all x2, waiting for transfers between devices, from_everyone(): return lax.all_to_all(copies, axis, split_axis=0, concat_axis=0, tiled=True)  13.3 us
    dot_general x4, matrix products, transform(): return jnp.einsum('bxc,cd->bxd', values, plane_matrix, precision=HIGHEST)  11.7 us
    all_to_all x1, waiting for transfers between devices, body(): lax.all_to_all(filtered, 'band', split_axis=1, concat_axis=0, tiled=True)  8.13 us
    all_to_all x2, starting transfers between devices, summed_on_arrival(): lax.all_to_all(tiles, axis, split_axis=0, concat_axis=0, tiled=True)  7.71 us
    all_to_all x1, starting transfers between devices, body(): lax.all_to_all(filtered, 'band', split_axis=1, concat_axis=0, tiled=True)  6.79 us
  transfers between devices with their start and end apart: 5, of which 5 were waited for; matrix products, arithmetic and copies ran while one was open for 2% of the time, Pallas kernels for 0%

commit v1 on v0

v1 whole, which is shorter than its diff:
```python
import functools
import numpy as np
import jax
import jax.numpy as jnp
from jax import lax
from jax.experimental import pallas as pl
from jax.experimental.pallas import tpu as pltpu
from jax.sharding import PartitionSpec as P

NB = 128
G = 24
GG = G * G
BUFFER = 6
CG = 8
CZ = 6
NZC = 192
DOMS = 32
BANDS = 8
LOCAL = NB // BANDS
PLANES = G // BANDS
ROW = 640
SHARE = 1792
PACKED = 72
HALF_ROW = GG // 2
EDGE = GG + HALF_ROW
POINTS = float(G * G * G)
FILTER_LOW = 1.0
FILTER_HIGH = 9.5
CENTER = 0.5 * (FILTER_HIGH + FILTER_LOW)
HALF = 0.5 * (FILTER_HIGH - FILTER_LOW)
HIGHEST = lax.Precision.HIGHEST
F32 = jnp.float32
INTERPRET = False
LIMIT = pltpu.CompilerParams(vmem_limit_bytes=16 << 20)


def tables():
    k = np.arange(CG)
    cosine = np.sqrt(2.0 / CG) * np.cos(np.pi * k[:, None] * (k[None, :] + 0.5) / CG)
    cosine[0] *= np.sqrt(0.5)
    r = np.arange(NZC)
    sine = np.zeros((NZC + 8, NZC))
    sine[:NZC] = np.sqrt(2.0 / (NZC + 1)) * np.sin(np.pi * (r[:, None] + 1) * (r[None, :] + 1) / (NZC + 1))
    level_xy = 4.0 * np.sin(0.5 * np.pi * k / CG) ** 2
    level_z = 4.0 * np.sin(0.5 * np.pi * (r + 1) / (NZC + 1)) ** 2
    inverse = 1.0 / (level_xy[:, None, None] + level_xy[None, :, None] + level_z[None, None, :])
    scale = 8.0 / float(NZC * NZC)
    onto_x = np.broadcast_to((scale * cosine.T)[:, :, None], (CG, CG, NZC))
    lane = np.arange(GG)
    gather = np.zeros((ROW, 128))
    for ky in range(CG):
        gather[lane, ky * 8 + (lane % G) // 3] = cosine[ky, (lane // G) // 3]
    over_x = np.broadcast_to(cosine.T[:, :, None], (CG, CG, 128))
    over_y = np.broadcast_to(cosine[:, :, None], (CG, CG, 256))
    sine = np.stack([sine[CZ * place : CZ * place + 8] for place in range(DOMS)])
    as_f32 = lambda a: np.ascontiguousarray(a, dtype=np.float32)
    return tuple(as_f32(a) for a in (sine, inverse.reshape(CG * CG, NZC), onto_x, gather, over_x, over_y))


def halves(x):
    high = x.astype(jnp.bfloat16)
    return high, (x - high.astype(F32)).astype(jnp.bfloat16)


def dot3(x, y, dims=(((1,), (0,)), ((), ()))):
    x_high, x_low = halves(x)
    y_high, y_low = halves(y)
    dot = functools.partial(lax.dot_general, dimension_numbers=dims, preferred_element_type=F32)
    return dot(x_high, y_high) + (dot(x_high, y_low) + dot(x_low, y_high))


def rolled(x, shift):
    return pltpu.roll(x, shift % ROW, 1)


def lane_index(shape):
    lane = lax.broadcasted_iota(jnp.int32, shape, 1).astype(F32)
    return lane, lane - G * jnp.floor((lane + 0.5) * (1.0 / G))


def filter_kernel(orb_ref, pot_ref, out_ref, plane_ref, diag_ref):
    rows = orb_ref.shape[0]
    lane, z = lane_index((rows, ROW))
    inside = lane < GG
    not_first = jnp.where(z > 0.5, 1.0, 0.0)
    not_last = jnp.where(z < G - 1.5, 1.0, 0.0)
    step = jnp.where(inside, 0.5 / HALF, 0.0)
    plane_ref[...] = jnp.zeros_like(plane_ref)
    diag_ref[...] = jnp.zeros_like(diag_ref)
    diag_ref[:, :GG] = (pot_ref[...] + (3.0 - CENTER)) * (1.0 / HALF)
    zeros = jnp.zeros((rows, ROW), F32)

    def load(x):
        plane_ref[x, :, :GG] = orb_ref[:, x, :]
        return plane_ref[x]

    def near(v, below, above):
        sides = rolled(v, 1) * not_first + rolled(v, -1) * not_last
        return (sides + (rolled(v, G) + rolled(v, -G))) + (below + above)

    first = {-1: zeros, G: zeros}
    start = {-1: zeros, 0: load(0), G: zeros}
    for x in range(G + 1):
        if x < G:
            if x + 1 < G:
                start[x + 1] = load(x + 1)
            v = start[x]
            first[x] = diag_ref[x : x + 1, :] * v - step * near(v, start[x - 1], start[x + 1])
        w = x - 1
        if w >= 0:
            v = first[w]
            twice = diag_ref[w : w + 1, :] * v - step * near(v, first[w - 1], first[w + 1])
            second = 2.0 * twice - start[w]
            p = w % PLANES
            out_ref[w // PLANES, :, p * GG : (p + 1) * GG] = second[:, :GG]
            if p == PLANES - 1:
                out_ref[w // PLANES, :, PLANES * GG :] = jnp.zeros((rows, SHARE - PLANES * GG), F32)


def filtered_shares(orbitals, potential):
    rows = 8
    return pl.pallas_call(
        filter_kernel,
        out_shape=jax.ShapeDtypeStruct((BANDS, LOCAL, SHARE), F32),
        grid=(LOCAL // rows,),
        in_specs=[
            pl.BlockSpec((rows, G, GG), lambda i: (i, 0, 0)),
            pl.BlockSpec((G, GG), lambda i: (0, 0)),
        ],
        out_specs=pl.BlockSpec((BANDS, rows, SHARE), lambda i: (0, i, 0)),
        scratch_shapes=[pltpu.VMEM((G, rows, ROW), F32), pltpu.VMEM((G, ROW), F32)],
        compiler_params=LIMIT,
        interpret=INTERPRET,
        name="filter",
    )(orbitals, potential)


def gram_kernel(f_ref, out_ref):
    high, low = halves(f_ref[...])
    both = lax.dot_general(
        high, jnp.concatenate([high, low], 0), (((1,), (1,)), ((), ())), preferred_element_type=F32
    )
    cross = both[:, NB:]
    raw = both[:, :NB] + (cross + cross.T)
    row = lax.broadcasted_iota(jnp.int32, (64, NB), 0)
    col = lax.broadcasted_iota(jnp.int32, (64, NB), 1)
    lower = pltpu.roll(raw[64:], 64, 1)
    packed = jnp.where(col >= row, raw[:64], lower)
    diag = jnp.sum(jnp.where(col == row + 64, raw[64:], 0.0), axis=0, keepdims=True)
    diag = jnp.broadcast_to(diag, (8, NB))
    for k in range(BANDS):
        out_ref[k, :64] = packed
        out_ref[k, 64:] = diag


def packed_grams(flat):
    return pl.pallas_call(
        gram_kernel,
        out_shape=jax.ShapeDtypeStruct((BANDS, PACKED, NB), F32),
        compiler_params=LIMIT,
        interpret=INTERPRET,
        name="gram",
    )(flat)


def density_kernel(g_ref, f_ref, occ_ref, vec_ref, gather_ref, poly_ref, fresh_ref, coarse_ref):
    total = g_ref[0]
    for k in range(1, BANDS):
        total = total + g_ref[k]
    packed = total[:64]
    row = lax.broadcasted_iota(jnp.int32, (64, NB), 0)
    col = lax.broadcasted_iota(jnp.int32, (64, NB), 1)
    top = jnp.where(col > row, packed, jnp.where(col == row, 0.5 * packed, 0.0))
    low = pltpu.roll(jnp.where(col < row, packed, 0.0), 64, 1)
    low = low + jnp.where(col == row + 64, 0.5 * total[64:65], 0.0)
    half = jnp.concatenate([top, low], 0)
    raw = half + half.T
    norm = jnp.sqrt(jnp.sum(jnp.sum(raw * raw, axis=0, keepdims=True), axis=1, keepdims=True))
    a = raw / norm
    scaling = jnp.sqrt(POINTS / norm)
    eye = jnp.where(
        lax.broadcasted_iota(jnp.int32, (NB, NB), 0) == lax.broadcasted_iota(jnp.int32, (NB, NB), 1), 1.0, 0.0
    )
    square = dot3(a, a)
    tail = dot3(square, 0.0625 * square - 0.5625 * a)
    poly = scaling * (2.25 * eye + (1.6875 * square - 2.4375 * a) + tail)
    poly_ref[...] = poly
    poly_high, poly_low = halves(poly)
    both = jnp.concatenate([poly_high, poly_low], 1)
    dot = functools.partial(jnp.dot, preferred_element_type=F32)
    weight = jnp.broadcast_to(occ_ref[...] * (1.0 / NB), (NB, 256))
    for c in range(SHARE // 256):
        cols = slice(256 * c, 256 * (c + 1))
        high, low = halves(f_ref[:, cols])
        current = dot(both, jnp.concatenate([high, high], 0)) + dot(poly_high, low)
        line = jnp.sum(current * current * weight, axis=0, keepdims=True)
        fresh_ref[:, cols] = jnp.broadcast_to(line, (8, 256))
    planes = fresh_ref[:, :ROW] + fresh_ref[:, GG : GG + ROW] + fresh_ref[:, 2 * GG : 2 * GG + ROW]
    inside = lax.broadcasted_iota(jnp.int32, (8, ROW), 1) < GG
    cells = jnp.where(inside, vec_ref[0:1] * planes + vec_ref[1:2], 0.0)
    coarse_ref[...] = jnp.dot(cells, gather_ref[...], precision=HIGHEST, preferred_element_type=F32)


def density_rows(grams, flat, occupation, vectors, gather):
    return pl.pallas_call(
        density_kernel,
        out_shape=(
            jax.ShapeDtypeStruct((NB, NB), F32),
            jax.ShapeDtypeStruct((8, SHARE), F32),
            jax.ShapeDtypeStruct((8, 128), F32),
        ),
        compiler_params=LIMIT,
        interpret=INTERPRET,
        name="density",
    )(grams, flat, occupation, vectors, gather)


def output_kernel(poly_ref, f_ref, fresh_ref, vec_ref, out_ref, own_ref, edge_ref):
    poly_high, poly_low = halves(poly_ref[...])
    dot = functools.partial(jnp.dot, preferred_element_type=F32)
    for c in range(SHARE // 128):
        turned = f_ref[:, 128 * c : 128 * (c + 1)].T
        high, low = halves(turned)
        value = dot(high, poly_high) + (dot(high, poly_low) + dot(low, poly_high))
        count = min(128, PLANES * GG - 128 * c)
        out_ref[128 * c : 128 * c + count] = value[:count]
    lane, z = lane_index((8, ROW))
    low_edge = (z < BUFFER - 0.5) & (lane < GG)
    high_edge = (z > G - BUFFER - 0.5) & (lane < GG)
    middle = (z > BUFFER - 0.5) & (z < G - BUFFER - 0.5)
    edges = []
    for p in range(PLANES):
        plane = fresh_ref[:, p * GG : p * GG + ROW]
        own_ref[p] = (vec_ref[7:8] * plane + vec_ref[2 + p : 3 + p])[0:1]
        edges.append((jnp.where(low_edge, plane, 0.0), jnp.where(high_edge, plane, 0.0)))
    first = (edges[0][0] + edges[0][1]) + (rolled(edges[1][0], 12) + rolled(edges[1][1], -12))
    last = edges[2][0] + edges[2][1]
    lower = last + (rolled(edges[2][0], 12 - HALF_ROW) + rolled(edges[2][1], -12 - HALF_ROW))
    lower = jnp.where(lane < HALF_ROW, jnp.where(middle, 0.0, last) + jnp.where(middle, lower, 0.0), 0.0)
    first = first + rolled(jnp.where(lane < 64, lower, 0.0), GG)
    rest = rolled(lower, -64)
    edge_ref[0:1] = jnp.zeros((1, 128), F32)
    for t in range(7):
        source, at = (first, 128 * t) if t < 5 else (rest, 128 * (t - 5))
        edge_ref[t + 1 : t + 2] = source[0:1, at : at + 128]


def output_parts(poly, flat, fresh, vectors):
    return pl.pallas_call(
        output_kernel,
        out_shape=(
            jax.ShapeDtypeStruct((PLANES * GG, NB), F32),
            jax.ShapeDtypeStruct((PLANES, 1, ROW), F32),
            jax.ShapeDtypeStruct((8, 128), F32),
        ),
        cost_estimate=pl.CostEstimate(flops=200_000_000, bytes_accessed=2_000_000, transcendentals=0),
        compiler_params=LIMIT,
        interpret=INTERPRET,
        name="output",
    )(poly, flat, fresh, vectors)


def prepare_kernel(
    where_ref, pos_ref, mix_ref, corr_ref, din_ref, sine_ref, inverse_ref, onto_ref, vec_ref, side_ref, green_ref, left_ref, right_ref, din_row
):
    dom, band = where_ref[0], where_ref[1]
    own = pos_ref[dom]
    shape = (1, ROW)
    lane, z = lane_index(shape)
    corr = jnp.zeros(shape, F32)
    for j in range(BUFFER):
        here = (jnp.abs(z - j) < 0.5) | (jnp.abs(z - (G - BUFFER + j)) < 0.5)
        corr = jnp.where(here, corr_ref[j].astype(F32), corr)
    corr = corr * (1.0 / 16.0)
    fresh_weight = jnp.full(shape, mix_ref[0].astype(F32))
    input_weight = jnp.full(shape, mix_ref[1].astype(F32))
    both = fresh_weight + input_weight
    fresh_weight = fresh_weight / both
    input_weight = input_weight / both
    has_left = jnp.where(jnp.full(shape, own) > 0, 1.0, 0.0)
    has_right = jnp.where(jnp.full(shape, own) < DOMS - 1, 1.0, 0.0)
    low = z < BUFFER - 0.5
    high = z > G - BUFFER - 0.5
    from_left = jnp.where(low, corr * has_left, 0.0)
    from_right = jnp.where(high, (1.0 - corr) * has_right, 0.0)
    keep = 1.0 - from_left - from_right
    cell = 1.0 / 27.0
    vec_ref[0:1] = cell * fresh_weight * jnp.where(high, corr * has_right, keep)
    din_row[...] = jnp.zeros_like(din_row)
    for p in range(PLANES):
        din_row[p : p + 1, :GG] = din_ref[p]
    din_sum = din_row[0:1] + din_row[1:2] + din_row[2:3]
    vec_ref[1:2] = jnp.where(high, 0.0, cell * input_weight * din_sum)
    for p in range(PLANES):
        vec_ref[2 + p : 3 + p] = input_weight * din_row[p : p + 1]
    vec_ref[5:6] = fresh_weight * from_left
    vec_ref[6:7] = fresh_weight * from_right
    vec_ref[7:8] = fresh_weight * keep
    left, right = jnp.int32(0), jnp.int32(0)
    for d in range(DOMS):
        left = jnp.where(pos_ref[d] == own - 1, d, left)
        right = jnp.where(pos_ref[d] == own + 1, d, right)
        right_ref[8 * d : 8 * d + 8] = sine_ref[pos_ref[d]]
    side_ref[0] = left
    side_ref[1] = right
    mine = sine_ref[own]
    onto = onto_ref[band]
    for ky in range(CG):
        part = inverse_ref[8 * ky : 8 * ky + 8] * onto
        for j in range(8):
            at = ky * 64 + j * 8
            left_ref[at : at + 8] = part * mine[j : j + 1]
    green_ref[...] = lax.dot_general(
        left_ref[...], right_ref[...], (((1,), (1,)), ((), ())), precision=HIGHEST, preferred_element_type=F32
    )


def prepared(where, position, mixing, corr, din, sine, inverse, onto):
    smem = pl.BlockSpec(memory_space=pltpu.SMEM)
    vmem = pl.BlockSpec(memory_space=pltpu.VMEM)
    return pl.pallas_call(
        prepare_kernel,
        out_shape=(
            jax.ShapeDtypeStruct((8, ROW), F32),
            jax.ShapeDtypeStruct((2,), jnp.int32),
            jax.ShapeDtypeStruct((512, 256), F32),
        ),
        in_specs=[smem] * 4 + [vmem] * 4,
        out_specs=(vmem, smem, vmem),
        scratch_shapes=[pltpu.VMEM((512, NZC), F32), pltpu.VMEM((256, NZC), F32), pltpu.VMEM((8, ROW), F32)],
        cost_estimate=pl.CostEstimate(flops=400_000_000, bytes_accessed=2_000_000, transcendentals=0),
        compiler_params=LIMIT,
        interpret=INTERPRET,
        name="prepare",
    )(where, position, mixing, corr, din, sine, inverse, onto)


def share_kernel(rows_ref, green_ref, over_x_ref, over_y_ref, edge_ref, out_ref, turn_ref, line_ref):
    modes = over_x_ref[0] * rows_ref[0:1]
    for x in range(1, CG):
        modes = modes + over_x_ref[x] * rows_ref[x : x + 1]
    cells = jnp.zeros((8, 256), F32)
    for ky in range(CG):
        acc = jnp.zeros((8, 256), F32)
        for j in range(8):
            at = ky * 8 + j
            acc = acc + jnp.broadcast_to(modes[:, at : at + 1], (8, 256)) * green_ref[8 * at : 8 * at + 8]
        cells = cells + over_y_ref[ky] * jnp.sum(acc, axis=0, keepdims=True)
    turn_ref[...] = jnp.concatenate([cells, jnp.zeros((120, 256), F32)], 0).T
    line_ref[...] = jnp.zeros_like(line_ref)
    for j in range(CZ):
        line_ref[:, 8 * j : 8 * j + 8] = turn_ref[pl.ds(j, DOMS, stride=8), :][:, :8]
    head = lax.broadcasted_iota(jnp.int32, (8, 128), 0) == 0
    edge = edge_ref[...]
    for d in range(DOMS):
        out_ref[d] = jnp.where(head, line_ref[d : d + 1], edge)


def hartree_shares(rows, green, over_x, over_y, edges):
    return pl.pallas_call(
        share_kernel,
        out_shape=jax.ShapeDtypeStruct((DOMS, 8, 128), F32),
        scratch_shapes=[pltpu.VMEM((256, 128), F32), pltpu.VMEM((DOMS, 128), F32)],
        compiler_params=LIMIT,
        interpret=INTERPRET,
        name="share",
    )(rows, green, over_x, over_y, edges)


def final_kernel(side_ref, msg_ref, own_ref, vec_ref, dens_ref, hart_ref):
    total = msg_ref[0]
    for d in range(1, DOMS):
        total = total + msg_ref[d]
    for j in range(CZ):
        hart_ref[j] = total[0:1, 8 * j : 8 * j + 8]
    lane = lax.broadcasted_iota(jnp.int32, (8, ROW), 1)

    def rows(tile):
        spread = [jnp.broadcast_to(tile[t + 1 : t + 2], (8, 128)) for t in range(7)]
        front = jnp.concatenate(spread[:5], 1)
        back = jnp.concatenate(spread[4:] + spread[5:], 1)
        return front, rolled(back, -64)

    left0, left2 = rows(msg_ref[side_ref[0]])
    right0, right2 = rows(msg_ref[side_ref[1]])
    far = G - BUFFER
    left_last = jnp.where(lane < HALF_ROW, rolled(left2, -far), rolled(left2, HALF_ROW + 12 - far))
    right_last = jnp.where(lane < HALF_ROW, rolled(right2, far), rolled(right2, HALF_ROW - 12 + far))
    left_part = (rolled(left0, -far), rolled(left0, -6), left_last)
    right_part = (rolled(right0, far), rolled(right0, 6), right_last)
    for p in range(PLANES):
        mixed = own_ref[p] + vec_ref[5:6] * left_part[p][0:1] + vec_ref[6:7] * right_part[p][0:1]
        dens_ref[p] = mixed[:, :GG]


def final_parts(sides, msg, own, vectors):
    smem = pl.BlockSpec(memory_space=pltpu.SMEM)
    vmem = pl.BlockSpec(memory_space=pltpu.VMEM)
    return pl.pallas_call(
        final_kernel,
        out_shape=(
            jax.ShapeDtypeStruct((PLANES, 1, GG), F32),
            jax.ShapeDtypeStruct((CZ, 1, CG), F32),
        ),
        in_specs=[smem, vmem, vmem, vmem],
        out_specs=(vmem, vmem),
        compiler_params=LIMIT,
        interpret=INTERPRET,
        name="final",
    )(sides, msg, own, vectors)


def exchanged(x, axis):
    return lax.all_to_all(x, axis, split_axis=0, concat_axis=0, tiled=True)


def body(orbitals, potential, density_in, occupation, position, mixing, correlation_weight):
    sine, inverse, onto, gather, over_x, over_y = tables()
    shares = exchanged(filtered_shares(orbitals[0], potential[0]), "band")
    flat = shares.reshape(NB, SHARE)
    where = jnp.stack([lax.axis_index("dom"), lax.axis_index("band")]).astype(jnp.int32)
    din = jnp.transpose(density_in, (1, 0, 2))
    vectors, sides, green = prepared(where, position, mixing, correlation_weight, din, sine, inverse, onto)
    grams = exchanged(packed_grams(flat), "band")
    poly, fresh, coarse = density_rows(grams, flat, occupation.reshape(NB, 1), vectors, gather)
    rows = exchanged(coarse, "band")
    points, own, edges = output_parts(poly, flat, fresh, vectors)
    msg = exchanged(hartree_shares(rows, green, over_x, over_y, edges), "dom")
    dens, hart = final_parts(sides, msg, own, vectors)
    orbitals_out = jnp.transpose(points.reshape(PLANES, GG, NB), (2, 0, 1)).reshape(1, NB, PLANES, GG)
    density = jnp.transpose(dens, (1, 0, 2))
    hartree = jnp.transpose(hart, (1, 2, 0)).reshape(1, 1, CG, CZ)
    return orbitals_out, density, hartree


def solution(mesh):
    return jax.shard_map(
        body,
        mesh=mesh,
        in_specs=(
            P("dom", "band", None, None),
            P("dom", None, None),
            P("dom", "band", None),
            P(),
            P(),
            P(),
            P(),
        ),
        out_specs=(
            P("dom", None, "band", None),
            P("dom", "band", None),
            P("dom", "band", None, None),
        ),
        check_vma=False,
    )
```

time: 139 us -> 71.2 us (0.51)
  waiting for transfers between devices: 38.3 us -> 7.5 us
  blocking collectives: 13.9 us -> 39.5 us
  matrix products: 22.8 us -> 0 us
  starting transfers between devices: 30.2 us -> 8.61 us
  local copies, waits for them, and re-layouts: 16.6 us -> 2.78 us
  Pallas kernels: 0 us -> 11.6 us
  other arithmetic: 9.34 us -> 0.08 us
  between operations: 6.34 us -> 0.71 us
    all_to_all x0 -> x2, blocking collectives: none -> 39.5 us  [exchanged(): return lax.all_to_all(x, axis, split_axis=0, concat_axis=0, tiled=True)]
    all_to_all x5 -> x2, waiting for transfers between devices: 38.3 us -> 7.5 us  [exchanged(): return lax.all_to_all(x, axis, split_axis=0, concat_axis=0, tiled=True)]
    dot_general x21 -> x0, matrix products: 22.8 us -> none  [the longest x4 11.7 us: transform(): return jnp.einsum('bxc,cd->bxd', values, plane_matrix, precision=HIGHEST)]
    all_to_all x5 -> x2, starting transfers between devices: 30.2 us -> 8.61 us  [exchanged(): return lax.all_to_all(x, axis, split_axis=0, concat_axis=0, tiled=True)]
    all_gather x1 -> x0, blocking collectives: 13.9 us -> none  [total_of_pieces(): tiles = lax.all_gather(x, axis)]
    pallas_call x0 -> x7, Pallas kernels: none -> 11.6 us  [the longest x1 3.77 us: filtered_shares(): pl.pallas_call(filter_kernel, out_shape=jax.ShapeDtypeStruct((BANDS, LOCA...]
    mul x12 -> x0, other arithmetic: 5.54 us -> none  [the longest x1 3.75 us: body(): plane_matrix = jnp.kron(sine_matrix, sine_matrix)]
    mul x5 -> x0, local copies, waits for them, and re-layouts: 5.13 us -> none  [the longest x1 4.75 us: body(): plane_matrix = jnp.kron(sine_matrix, sine_matrix)]
  transfers between devices with their start and end apart: 5 -> 2, of which waited for: 5 -> 2; matrix products, arithmetic and copies ran while one was open for 2% -> 0% of each run, Pallas kernels for 0% -> 4%
where the time goes in v1:
time: 71.2 us; the launch traced here: 70.8 us
  blocking collectives  39.5 us (55%)
  Pallas kernels  11.6 us (16%)
  starting transfers between devices  8.61 us (12%)
  waiting for transfers between devices  7.5 us (11%)
  local copies, waits for them, and re-layouts  2.78 us (4%)
    all_to_all x2, blocking collectives, exchanged(): return lax.all_to_all(x, axis, split_axis=0, concat_axis=0, tiled=True)  39.5 us
    all_to_all x2, starting transfers between devices, exchanged(): return lax.all_to_all(x, axis, split_axis=0, concat_axis=0, tiled=True)  8.61 us
    all_to_all x2, waiting for transfers between devices, exchanged(): return lax.all_to_all(x, axis, split_axis=0, concat_axis=0, tiled=True)  7.5 us
    pallas_call x1, Pallas kernels, filtered_shares(): pl.pallas_call(filter_kernel, out_shape=jax.ShapeDtypeStruct((BANDS, LOCA...  3.77 us
    unnamed x26, local copies, waits for them, and re-layouts  2.67 us
    pallas_call x1, Pallas kernels, density_rows(): pl.pallas_call(density_kernel, out_shape=(jax.ShapeDtypeStruct((NB, NB),...  1.86 us
    pallas_call x1, Pallas kernels, output_parts(): pl.pallas_call(output_kernel, out_shape=(jax.ShapeDtypeStruct((PLANES * G...  1.5 us
    pallas_call x1, Pallas kernels, prepared(): pl.pallas_call(prepare_kernel, out_shape=(jax.ShapeDtypeStruct((8, ROW),...  1.47 us
  transfers between devices with their start and end apart: 2, of which 2 were waited for; matrix products, arithmetic and copies ran while one was open for 0% of the time, Pallas kernels for 4%

profile of v1, /device:TPU:1, one launch (start us, length us, event | category | flops | bytes accessed | tf_op | source)
XLA Modules:
  0.0 70.8 jit_solution(3359223376725866693)
XLA Ops:
  0.6 0.0 copy-start
  0.6 1.2 %copy-done = f32[1,16,24,576]{3,2,1,0:T(8,128)S(1)} copy-done((f32[1,16,24,576]{3,2,1,0:T(8,128)S(1)}, f32[1,16,24,576]{3,2,1,0:T(8,128)}, u32[]{:S(2)}) %copy-start) | copy-done | bytes 884760
  1.8 0.0 copy-start.3
  1.8 0.8 %copy-done.3 = f32[1,24,576]{2,1,0:T(8,128)S(1)} copy-done((f32[1,24,576]{2,1,0:T(8,128)S(1)}, f32[1,24,576]{2,1,0:T(8,128)}, u32[]{:S(2)}) %copy-start.3) | copy-done | bytes 55320
  2.7 3.8 %filter.1 = f32[8,16,1792]{2,1,0:T(8,128)S(1)} custom-call(f32[16,24,576]{2,1,0:T(8,128)S(1)} %bitcast.25, f32[24,576]{1,0:T(8,128)S(1)} %bitcast.26), custom_call_target="tpu_custom_call" | custom-call | tf_op jit(solution)/shard_map/filter/pallas_call | solution.py:122
  6.4 19.3 %all_to_all.26 = f32[8,16,1792]{2,1,0:T(8,128)S(1)} all-to-all(f32[8,16,1792]{2,1,0:T(8,128)S(1)} %filter.1), channel_id=1, replica_groups=mesh['dom'=32,'band'=8] {'band'}, dimensions={0} | all-to-all | bytes 1835008 | tf_op jit(solution)/shard_map/all_to_all | solution.py:414
  25.7 1.3 %gram.1 = f32[8,72,128]{2,1,0:T(8,128)} custom-call(f32[128,1792]{1,0:T(8,128)S(1)} %bitcast.22), custom_call_target="tpu_custom_call" | custom-call | tf_op jit(solution)/shard_map/gram/pallas_call | solution.py:157
  27.1 0.0 copy-start.12
  27.1 0.0 copy-start.9
  27.1 0.0 copy-start.11
  27.1 4.3 %all-to-all-start.1 = ((f32[8,72,128]{2,1,0:T(8,128)}), f32[8,72,128]{2,1,0:T(8,128)S(1)}, u32[]{:S(2)}, u32[]{:S(2)}) async-start(f32[8,72,128]{2,1,0:T(8,128)} %gram.1), calls=%async_computation.1 | async-start | bytes 589824 | tf_op jit(solution)/shard_map/all_to_all | solution.py:414
  31.4 0.0 copy-start.10
  31.4 0.0 copy-done.12
  31.4 0.0 copy-start.6
  31.4 0.0 copy-start.7
  31.4 0.0 copy-start.8
  31.4 0.1 copy.18.occ_ref
  31.6 0.0 copy-start.5
  31.6 0.1 pad_add_fusion.where_ref
  31.6 0.0 copy-done.9
  31.6 0.0 copy-done.11
  31.6 0.6 copy-done.10
  32.2 0.0 copy-done.6
  32.3 0.0 copy-done.7
  32.3 0.0 copy-done.8
  32.3 0.0 copy-done.5
  32.3 0.0 copy-start.1
  32.3 1.5 %prepare.1 = (f32[8,640]{1,0:T(8,128)S(1)}, s32[2]{0:T(128)S(1)}, f32[512,256]{1,0:T(8,128)S(1)}) custom-call(s32[2]{0:T(128)S(1)} %pad_add_fusion.where_ref, s32[32]{0:T(128)S(1)} %copy-done.6, s32[2]{0:T(128)S(1)} %copy-done.7, s32[6]{0:T(128)S(1)} %copy-done.8, f32[3,1,576]{2,1,0:T(1,128)S(1)} %bitcast.28, f32[32,8,192]{2,1,0:T(8,128)S(1)} %copy-done.9, ...), custom_call_target="tpu_custom_call" | custom-call | flops 400000000 | bytes 2000000 | tf_op jit(solution)/shard_map/prepare/pallas_call | solution.py:321
  33.8 4.5 %all-to-all-done.1.g_ref = f32[8,72,128]{2,1,0:T(8,128)S(1)} async-done(((f32[8,72,128]{2,1,0:T(8,128)}), f32[8,72,128]{2,1,0:T(8,128)S(1)}, u32[]{:S(2)}, u32[]{:S(2)}) %all-to-all-start.1) | async-done | bytes 294944 | tf_op jit(solution)/shard_map/all_to_all | solution.py:414
  38.2 0.0 copy-done.1
  38.2 1.9 %density.1 = (f32[128,128]{1,0:T(8,128)S(1)}, f32[8,1792]{1,0:T(8,128)S(1)}, f32[8,128]{1,0:T(8,128)}) custom-call(f32[8,72,128]{2,1,0:T(8,128)S(1)} %all-to-all-done.1.g_ref, f32[128,1792]{1,0:T(8,128)S(1)} %bitcast.23, f32[128,1]{1,0:T(8,128)S(1)} %copy.18.occ_ref, f32[8,640]{1,0:T(8,128)S(1)} %get-tuple-element.14.vec_ref, f32[640,128]{1,0:T(8,128)S(1)} %copy-done.1), custom_call_target="tpu_custom_call" | custom-call | tf_op jit(solution)/shard_map/density/pallas_call | solution.py:205
  40.1 4.3 %all-to-all-start.2 = ((f32[8,1,128]{2,1,0:T(1,128)}), f32[8,1,128]{2,1,0:T(1,128)S(1)}, u32[]{:S(2)}, u32[]{:S(2)}) async-start(f32[8,1,128]{2,1,0:T(1,128)} %bitcast.11), calls=%async_computation.2 | async-start | bytes 8192 | tf_op jit(solution)/shard_map/all_to_all | solution.py:414
  44.4 0.0 copy-start.2
  44.4 0.0 copy-start.4
  44.4 1.5 %output.1 = (f32[1728,128]{1,0:T(8,128)}, f32[3,1,640]{2,1,0:T(1,128)S(1)}, f32[8,128]{1,0:T(8,128)S(1)}) custom-call(f32[128,128]{1,0:T(8,128)S(1)} %get-tuple-element.15.poly_ref, f32[128,1792]{1,0:T(8,128)S(1)} %bitcast.24, f32[8,1792]{1,0:T(8,128)S(1)} %get-tuple-element.16.fresh_ref, f32[8,640]{1,0:T(8,128)S(1)} %get-tuple-element.14.vec_ref), custom_call_target="tpu_custom_call" | custom-call | flops 200000000 | bytes 2000000 | tf_op jit(solution)/shard_map/output/pallas_call | solution.py:249
  45.9 3.0 %all-to-all-done.2 = f32[8,1,128]{2,1,0:T(1,128)S(1)} async-done(((f32[8,1,128]{2,1,0:T(1,128)}), f32[8,1,128]{2,1,0:T(1,128)S(1)}, u32[]{:S(2)}, u32[]{:S(2)}) %all-to-all-start.2) | async-done | bytes 4128 | tf_op jit(solution)/shard_map/all_to_all | solution.py:414
  48.9 0.0 copy-done.2
  48.9 0.0 copy-done.4
  48.9 0.4 share.1
  49.3 20.1 %all_to_all.27.msg_ref = f32[32,8,128]{2,1,0:T(8,128)S(1)} all-to-all(f32[32,8,128]{2,1,0:T(8,128)S(1)} %share.1), channel_id=1, replica_groups=mesh['dom'=32,'band'=8] {'dom'}, dimensions={0} | all-to-all | bytes 262144 | tf_op jit(solution)/shard_map/all_to_all | solution.py:414
  69.5 1.3 %final.1 = (f32[3,1,576]{2,1,0:T(1,128)}, f32[6,1,8]{2,1,0:T(1,128)}) custom-call(s32[2]{0:T(128)S(1)} %get-tuple-element.18.side_ref, f32[32,8,128]{2,1,0:T(8,128)S(1)} %all_to_all.27.msg_ref, f32[3,1,640]{2,1,0:T(1,128)S(1)} %get-tuple-element.22.own_ref, f32[8,640]{1,0:T(8,128)S(1)} %get-tuple-element.14.vec_ref), custom_call_target="tpu_custom_call" | custom-call | tf_op jit(solution)/shard_map/final/pallas_call | solution.py:399
Async XLA Ops:
  0.6 1.2 %copy-start = (f32[1,16,24,576]{3,2,1,0:T(8,128)S(1)}, f32[1,16,24,576]{3,2,1,0:T(8,128)}, u32[]{:S(2)}) copy-start(f32[1,16,24,576]{3,2,1,0:T(8,128)} %param.13) | copy-start | bytes 2654212
  1.8 0.8 %copy-start.3 = (f32[1,24,576]{2,1,0:T(8,128)S(1)}, f32[1,24,576]{2,1,0:T(8,128)}, u32[]{:S(2)}) copy-start(f32[1,24,576]{2,1,0:T(8,128)} %param.14) | copy-start | bytes 165892
  27.1 4.3 %copy-start.12 = (f32[128]{0:T(128)S(1)}, f32[128]{0:T(128)}, u32[]{:S(2)}) copy-start(f32[128]{0:T(128)} %param.16) | copy-start | bytes 1540
  27.1 4.6 %copy-start.9 = (f32[32,8,192]{2,1,0:T(8,128)S(1)}, f32[32,8,192]{2,1,0:T(8,128)}, u32[]{:S(2)}) copy-start(f32[32,8,192]{2,1,0:T(8,128)} %constant.21.clone.sine_ref) | copy-start | bytes 589828
  27.1 4.6 %copy-start.11 = (f32[64,192]{1,0:T(8,128)S(1)}, f32[64,192]{1,0:T(8,128)}, u32[]{:S(2)}) copy-start(f32[64,192]{1,0:T(8,128)} %constant.22.clone.inverse_ref) | copy-start | bytes 147460
  27.1 11.1 %all-to-all-start.1 = ((f32[8,72,128]{2,1,0:T(8,128)}), f32[8,72,128]{2,1,0:T(8,128)S(1)}, u32[]{:S(2)}, u32[]{:S(2)}) async-start(f32[8,72,128]{2,1,0:T(8,128)} %gram.1), calls=%async_computation.1 | async-start | bytes 589824 | tf_op jit(solution)/shard_map/all_to_all | solution.py:414
  31.4 0.8 %copy-start.10 = (f32[8,8,192]{2,1,0:T(8,128)S(1)}, f32[8,8,192]{2,1,0:T(8,128)}, u32[]{:S(2)}) copy-start(f32[8,8,192]{2,1,0:T(8,128)} %constant.23.clone.onto_ref) | copy-start | bytes 147460
  31.4 0.8 %copy-start.6 = (s32[32]{0:T(128)S(1)}, s32[32]{0:T(128)}, u32[]{:S(2)}) copy-start(s32[32]{0:T(128)} %pos_ref.1) | copy-start | bytes 388
  31.4 0.8 %copy-start.7 = (s32[2]{0:T(128)S(1)}, s32[2]{0:T(128)}, u32[]{:S(2)}) copy-start(s32[2]{0:T(128)} %mix_ref.1) | copy-start | bytes 28
  31.4 0.8 %copy-start.8 = (s32[6]{0:T(128)S(1)}, s32[6]{0:T(128)}, u32[]{:S(2)}) copy-start(s32[6]{0:T(128)} %corr_ref.1) | copy-start | bytes 76
  31.6 0.7 copy-start.5
  32.3 6.0 %copy-start.1 = (f32[640,128]{1,0:T(8,128)S(1)}, f32[640,128]{1,0:T(8,128)}, u32[]{:S(2)}) copy-start(f32[640,128]{1,0:T(8,128)} %constant.24.clone.gather_ref) | copy-start | bytes 983044
  40.1 8.8 %all-to-all-start.2 = ((f32[8,1,128]{2,1,0:T(1,128)}), f32[8,1,128]{2,1,0:T(1,128)S(1)}, u32[]{:S(2)}, u32[]{:S(2)}) async-start(f32[8,1,128]{2,1,0:T(1,128)} %bitcast.11), calls=%async_computation.2 | async-start | bytes 8192 | tf_op jit(solution)/shard_map/all_to_all | solution.py:414
  44.4 4.5 %copy-start.2 = (f32[8,8,256]{2,1,0:T(8,128)S(1)}, f32[8,8,256]{2,1,0:T(8,128)}, u32[]{:S(2)}) copy-start(f32[8,8,256]{2,1,0:T(8,128)} %constant.26.clone.over_y_ref) | copy-start | bytes 196612
  44.4 4.5 %copy-start.4 = (f32[8,8,128]{2,1,0:T(8,128)S(1)}, f32[8,8,128]{2,1,0:T(8,128)}, u32[]{:S(2)}) copy-start(f32[8,8,128]{2,1,0:T(8,128)} %constant.25.clone.over_x_ref) | copy-start | bytes 98308

commit v2 on v1

v2 whole, which is shorter than its diff:
```python
import functools
import numpy as np
import jax
import jax.numpy as jnp
from jax import lax
from jax.experimental import pallas as pl
from jax.experimental.pallas import tpu as pltpu
from jax.sharding import PartitionSpec as P

NB = 128
G = 24
GG = G * G
BUFFER = 6
CG = 8
CZ = 6
NZC = 192
DOMS = 32
BANDS = 8
LOCAL = NB // BANDS
PLANES = G // BANDS
ROW = 640
SHARE = 1792
PACKED = 72
HALF_ROW = GG // 2
EDGE = GG + HALF_ROW
POINTS = float(G * G * G)
FILTER_LOW = 1.0
FILTER_HIGH = 9.5
CENTER = 0.5 * (FILTER_HIGH + FILTER_LOW)
HALF = 0.5 * (FILTER_HIGH - FILTER_LOW)
HIGHEST = lax.Precision.HIGHEST
F32 = jnp.float32
INTERPRET = False
FILTER_LIMIT = pltpu.CompilerParams(vmem_limit_bytes=55_250_000)
LIMIT = pltpu.CompilerParams(vmem_limit_bytes=16 << 20)


def tables():
    k = np.arange(CG)
    cosine = np.sqrt(2.0 / CG) * np.cos(np.pi * k[:, None] * (k[None, :] + 0.5) / CG)
    cosine[0] *= np.sqrt(0.5)
    r = np.arange(NZC)
    sine = np.zeros((NZC + 8, NZC))
    sine[:NZC] = np.sqrt(2.0 / (NZC + 1)) * np.sin(np.pi * (r[:, None] + 1) * (r[None, :] + 1) / (NZC + 1))
    level_xy = 4.0 * np.sin(0.5 * np.pi * k / CG) ** 2
    level_z = 4.0 * np.sin(0.5 * np.pi * (r + 1) / (NZC + 1)) ** 2
    inverse = 1.0 / (level_xy[:, None, None] + level_xy[None, :, None] + level_z[None, None, :])
    scale = 8.0 / float(NZC * NZC)
    onto_x = np.broadcast_to((scale * cosine.T)[:, :, None], (CG, CG, NZC))
    lane = np.arange(GG)
    gather = np.zeros((ROW, 256))
    for ky in range(CG):
        gather[lane, ky * G + lane % G] = cosine[ky, (lane // G) // 3]
    over_x = np.broadcast_to(cosine.T[:, :, None], (CG, CG, 256))
    over_y = np.broadcast_to(cosine[:, :, None], (CG, CG, 256))
    sine = np.stack([sine[CZ * place : CZ * place + 8] for place in range(DOMS)])
    as_f32 = lambda a: np.ascontiguousarray(a, dtype=np.float32)
    return tuple(as_f32(a) for a in (sine, inverse.reshape(CG * CG, NZC), onto_x, gather, over_x, over_y))


def halves(x):
    high = x.astype(jnp.bfloat16)
    return high, (x - high.astype(F32)).astype(jnp.bfloat16)


def dot3(x, y, dims=(((1,), (0,)), ((), ()))):
    x_high, x_low = halves(x)
    y_high, y_low = halves(y)
    dot = functools.partial(lax.dot_general, dimension_numbers=dims, preferred_element_type=F32)
    return dot(x_high, y_high) + (dot(x_high, y_low) + dot(x_low, y_high))


def rolled(x, shift):
    return pltpu.roll(x, shift % ROW, 1)


def lane_index(shape):
    lane = lax.broadcasted_iota(jnp.int32, shape, 1).astype(F32)
    return lane, lane - G * jnp.floor((lane + 0.5) * (1.0 / G))


def neighbour_matrix(mat_ref):
    mat_ref[...] = jnp.zeros_like(mat_ref)
    for t in range(ROW // 128):
        top, end = max(0, 128 * t - 32), min(ROW, 128 * t + 160)
        shape = (end - top, 128)
        row = lax.broadcasted_iota(jnp.int32, shape, 0) + top
        col = lax.broadcasted_iota(jnp.int32, (8, 128), 1) + 128 * t
        _, z = lane_index((8, ROW))
        z = z[:, 128 * t : 128 * (t + 1)]
        before = jnp.where(z > 0.5, col - 1, -ROW)[0:1]
        after = jnp.where(z < G - 1.5, col + 1, -ROW)[0:1]
        col = col[0:1]
        hit = (row == before) | (row == after) | (row == col - G) | (row == col + G)
        hit = hit & (row < GG) & (col < GG)
        mat_ref[top:end, 128 * t : 128 * (t + 1)] = jnp.where(hit, 1.0, 0.0).astype(jnp.bfloat16)


def filter_kernel(orb_ref, pot_ref, out_ref, in_ref, pot_in, mat_ref, zero_ref, first_ref, side_ref, diag_ref, sems):
    copies = [pltpu.make_async_copy(pot_ref, pot_in, sems.at[3])]
    for c in range(3):
        part = pl.ds(8 * c, 8)
        copies.append(pltpu.make_async_copy(orb_ref.at[:, part, :], in_ref.at[c], sems.at[c]))
    for copy in copies:
        copy.start()
    neighbour_matrix(mat_ref)
    lane = lax.broadcasted_iota(jnp.int32, (1, ROW), 1)
    step = jnp.where(lane < GG, 0.5 / HALF, 0.0)
    diag_ref[:, GG - 64 :] = jnp.zeros((G, 128), F32)
    zero_ref[:, :, GG - 64 :] = jnp.zeros((G, LOCAL, 128), F32)
    copies[0].wait()
    diag_ref[:, :GG] = (pot_in[...] + (3.0 - CENTER)) * (1.0 / HALF)
    dot = functools.partial(jnp.dot, preferred_element_type=F32)

    def sum_sides(source, c):
        high, low = halves(source[8 * c : 8 * c + 8].reshape(8 * LOCAL, ROW))
        stack = jnp.concatenate([high, low], 0)
        for rows, cols in ((slice(0, 384), slice(0, 256)), (slice(128, 640), slice(256, 512)), (slice(384, 640), slice(512, 640))):
            both = dot(stack[:, rows], mat_ref[rows, cols])
            side = both[: 8 * LOCAL] + both[8 * LOCAL :]
            side_ref[8 * c : 8 * c + 8, :, cols] = side.reshape(8, LOCAL, cols.stop - cols.start)

    def applied(source, x):
        v = source[x]
        near = side_ref[x]
        if x > 0:
            near = near + source[x - 1]
        if x + 1 < G:
            near = near + source[x + 1]
        return diag_ref[x : x + 1] * v - step * near

    for c in range(3):
        copies[c + 1].wait()
        for x in range(8 * c, 8 * c + 8):
            zero_ref[x, :, :GG] = in_ref[c, :, x - 8 * c, :]
        sum_sides(zero_ref, c)
    for x in range(G):
        first_ref[x] = applied(zero_ref, x)
    for c in range(3):
        sum_sides(first_ref, c)
    for x in range(G):
        second = 2.0 * applied(first_ref, x) - zero_ref[x]
        p = x % PLANES
        out_ref[x // PLANES, :, p * GG : (p + 1) * GG] = second[:, :GG]
        if p == PLANES - 1:
            out_ref[x // PLANES, :, PLANES * GG :] = jnp.zeros((LOCAL, SHARE - PLANES * GG), F32)


def filtered_shares(orbitals, potential):
    return pl.pallas_call(
        filter_kernel,
        out_shape=jax.ShapeDtypeStruct((BANDS, LOCAL, SHARE), F32),
        in_specs=[pl.BlockSpec(memory_space=pltpu.HBM)] * 2,
        out_specs=pl.BlockSpec(memory_space=pltpu.VMEM),
        scratch_shapes=[
            pltpu.VMEM((3, LOCAL, 8, GG), F32),
            pltpu.VMEM((G, GG), F32),
            pltpu.VMEM((ROW, ROW), jnp.bfloat16),
            pltpu.VMEM((G, LOCAL, ROW), F32),
            pltpu.VMEM((G, LOCAL, ROW), F32),
            pltpu.VMEM((G, LOCAL, ROW), F32),
            pltpu.VMEM((G, ROW), F32),
            pltpu.SemaphoreType.DMA((4,)),
        ],
        compiler_params=FILTER_LIMIT,
        interpret=INTERPRET,
        name="filter",
    )(orbitals, potential)


def gram_kernel(f_ref, out_ref):
    high, low = halves(f_ref[...])
    both = lax.dot_general(
        high, jnp.concatenate([high, low], 0), (((1,), (1,)), ((), ())), preferred_element_type=F32
    )
    cross = both[:, NB:]
    raw = both[:, :NB] + (cross + cross.T)
    row = lax.broadcasted_iota(jnp.int32, (64, NB), 0)
    col = lax.broadcasted_iota(jnp.int32, (64, NB), 1)
    lower = pltpu.roll(raw[64:], 64, 1)
    packed = jnp.where(col >= row, raw[:64], lower)
    diag = jnp.sum(jnp.where(col == row + 64, raw[64:], 0.0), axis=0, keepdims=True)
    diag = jnp.broadcast_to(diag, (8, NB))
    for k in range(BANDS):
        out_ref[k, :64] = packed
        out_ref[k, 64:] = diag


def packed_grams(flat):
    return pl.pallas_call(
        gram_kernel,
        out_shape=jax.ShapeDtypeStruct((BANDS, PACKED, NB), F32),
        compiler_params=LIMIT,
        interpret=INTERPRET,
        name="gram",
    )(flat)


def density_kernel(g_ref, f_ref, occ_ref, din_ref, gather_ref, poly_ref, fresh_ref, coarse_ref, rows_ref):
    total = g_ref[0]
    for k in range(1, BANDS):
        total = total + g_ref[k]
    packed = total[:64]
    row = lax.broadcasted_iota(jnp.int32, (64, NB), 0)
    col = lax.broadcasted_iota(jnp.int32, (64, NB), 1)
    top = jnp.where(col > row, packed, jnp.where(col == row, 0.5 * packed, 0.0))
    low = pltpu.roll(jnp.where(col < row, packed, 0.0), 64, 1)
    low = low + jnp.where(col == row + 64, 0.5 * total[64:65], 0.0)
    half = jnp.concatenate([top, low], 0)
    raw = half + half.T
    norm = jnp.sqrt(jnp.sum(jnp.sum(raw * raw, axis=0, keepdims=True), axis=1, keepdims=True))
    a = raw / norm
    scaling = jnp.sqrt(POINTS / norm)
    eye = jnp.where(
        lax.broadcasted_iota(jnp.int32, (NB, NB), 0) == lax.broadcasted_iota(jnp.int32, (NB, NB), 1), 1.0, 0.0
    )
    square = dot3(a, a)
    tail = dot3(square, 0.0625 * square - 0.5625 * a)
    poly = scaling * (2.25 * eye + (1.6875 * square - 2.4375 * a) + tail)
    poly_ref[...] = poly
    poly_high, poly_low = halves(poly)
    both = jnp.concatenate([poly_high, poly_low], 1)
    dot = functools.partial(jnp.dot, preferred_element_type=F32)
    weight = jnp.sum(eye * (occ_ref[...] * (1.0 / NB)), axis=1, keepdims=True)
    weight = jnp.broadcast_to(weight, (NB, 256))
    for c in range(SHARE // 256):
        cols = slice(256 * c, 256 * (c + 1))
        high, low = halves(f_ref[:, cols])
        current = dot(both, jnp.concatenate([high, high], 0)) + dot(poly_high, low)
        line = jnp.sum(current * current * weight, axis=0, keepdims=True)
        fresh_ref[:, cols] = jnp.broadcast_to(line, (8, 256))
    planes = fresh_ref[:, :ROW] + fresh_ref[:, GG : GG + ROW] + fresh_ref[:, 2 * GG : 2 * GG + ROW]
    rows_ref[...] = jnp.zeros_like(rows_ref)
    rows_ref[0:8, :GG] = planes[:, :GG]
    rows_ref[8:9, :GG] = din_ref[0] + din_ref[1] + din_ref[2]
    cells = dot3(rows_ref[...], gather_ref[...])
    row = lax.broadcasted_iota(jnp.int32, (8, NB), 0)
    inputs = jnp.broadcast_to(cells[8:9], (8, 256))
    tile = jnp.where(row == 0, cells[:8, :128], cells[:8, 128:])
    tile = jnp.where(row == 2, inputs[:, :128], jnp.where(row == 3, inputs[:, 128:], tile))
    for k in range(BANDS):
        coarse_ref[k] = tile


def density_rows(grams, flat, occupation, din, gather):
    return pl.pallas_call(
        density_kernel,
        out_shape=(
            jax.ShapeDtypeStruct((NB, NB), F32),
            jax.ShapeDtypeStruct((8, SHARE), F32),
            jax.ShapeDtypeStruct((BANDS, 8, 128), F32),
        ),
        scratch_shapes=[pltpu.VMEM((16, ROW), F32)],
        compiler_params=LIMIT,
        interpret=INTERPRET,
        name="density",
    )(grams, flat, occupation, din, gather)


def output_kernel(
    pos_ref, mix_ref, corr_ref, poly_ref, f_ref, fresh_ref, din_ref, sine_ref, inverse_ref, onto_ref,
    out_ref, own_ref, edge_ref, vec_ref, side_ref, green_ref, left_ref, right_ref,
):
    poly_high, poly_low = halves(poly_ref[...])
    dot = functools.partial(jnp.dot, preferred_element_type=F32)
    for c in range(SHARE // 128):
        turned = f_ref[:, 128 * c : 128 * (c + 1)].T
        high, low = halves(turned)
        value = dot(high, poly_high) + (dot(high, poly_low) + dot(low, poly_high))
        count = min(128, PLANES * GG - 128 * c)
        out_ref[128 * c : 128 * c + count] = value[:count]

    if INTERPRET:
        dom, band = pos_ref[DOMS], pos_ref[DOMS + 1]
    else:
        dom, band = lax.axis_index("dom"), lax.axis_index("band")
    own = pos_ref[dom]
    lane, z = lane_index((8, ROW))
    corr = jnp.zeros((8, ROW), F32)
    for j in range(BUFFER):
        here = (jnp.abs(z - j) < 0.5) | (jnp.abs(z - (G - BUFFER + j)) < 0.5)
        corr = jnp.where(here, corr_ref[j].astype(F32), corr)
    corr = corr * (1.0 / 16.0)
    fresh_weight = jnp.full((8, ROW), mix_ref[0].astype(F32))
    input_weight = jnp.full((8, ROW), mix_ref[1].astype(F32))
    both = fresh_weight + input_weight
    fresh_weight = fresh_weight / both
    input_weight = input_weight / both
    has_left = jnp.where(jnp.full((8, ROW), own) > 0, 1.0, 0.0)
    has_right = jnp.where(jnp.full((8, ROW), own) < DOMS - 1, 1.0, 0.0)
    low_z = z < BUFFER - 0.5
    high_z = z > G - BUFFER - 0.5
    middle = (z > BUFFER - 0.5) & (z < G - BUFFER - 0.5)
    from_left = jnp.where(low_z, corr * has_left, 0.0)
    from_right = jnp.where(high_z, (1.0 - corr) * has_right, 0.0)
    keep = 1.0 - from_left - from_right
    cell = 1.0 / 27.0
    vec_ref[0:1] = (cell * fresh_weight * jnp.where(high_z, corr * has_right, keep))[0:1]
    vec_ref[1:2] = jnp.where(high_z, 0.0, cell * input_weight)[0:1]
    vec_ref[2:3] = (fresh_weight * from_left)[0:1]
    vec_ref[3:4] = (fresh_weight * from_right)[0:1]

    low_edge = low_z & (lane < GG)
    high_edge = high_z & (lane < GG)
    edges = []
    for p in range(PLANES):
        plane = fresh_ref[:, p * GG : p * GG + ROW]
        own_ref[p] = (fresh_weight * keep * plane)[0:1, :GG] + input_weight[0:1, :GG] * din_ref[p]
        edges.append((jnp.where(low_edge, plane, 0.0), jnp.where(high_edge, plane, 0.0)))
    first = (edges[0][0] + edges[0][1]) + (rolled(edges[1][0], 12) + rolled(edges[1][1], -12))
    last = edges[2][0] + edges[2][1]
    moved = rolled(edges[2][0], 12 - HALF_ROW) + rolled(edges[2][1], -12 - HALF_ROW)
    last = jnp.where(lane < HALF_ROW, jnp.where(middle, moved, last), 0.0)
    first = first + rolled(jnp.where(lane < 64, last, 0.0), GG)
    rest = rolled(last, -64)
    edge_ref[0:1] = jnp.zeros((1, 128), F32)
    for t in range(7):
        source, at = (first, 128 * t) if t < 5 else (rest, 128 * (t - 5))
        edge_ref[t + 1 : t + 2] = source[0:1, at : at + 128]

    left, right = jnp.int32(0), jnp.int32(0)
    for d in range(DOMS):
        left = jnp.where(pos_ref[d] == own - 1, d, left)
        right = jnp.where(pos_ref[d] == own + 1, d, right)
        right_ref[8 * d : 8 * d + 8] = sine_ref[pos_ref[d]]
    side_ref[0] = left
    side_ref[1] = right
    mine = sine_ref[own]
    onto = onto_ref[band]
    for ky in range(CG):
        part = inverse_ref[8 * ky : 8 * ky + 8] * onto
        for j in range(8):
            at = ky * 64 + j * 8
            left_ref[at : at + 8] = part * mine[j : j + 1]
    green_ref[...] = dot3(left_ref[...], right_ref[...], (((1,), (1,)), ((), ())))


def output_parts(position, mixing, corr, poly, flat, fresh, din, sine, inverse, onto):
    if INTERPRET:
        position = jnp.append(position, jnp.stack([lax.axis_index("dom"), lax.axis_index("band")]))
    smem = pl.BlockSpec(memory_space=pltpu.SMEM)
    vmem = pl.BlockSpec(memory_space=pltpu.VMEM)
    return pl.pallas_call(
        output_kernel,
        out_shape=(
            jax.ShapeDtypeStruct((PLANES * GG, NB), F32),
            jax.ShapeDtypeStruct((PLANES, 1, GG), F32),
            jax.ShapeDtypeStruct((8, 128), F32),
            jax.ShapeDtypeStruct((8, ROW), F32),
            jax.ShapeDtypeStruct((2,), jnp.int32),
            jax.ShapeDtypeStruct((512, 256), F32),
        ),
        in_specs=[smem] * 3 + [vmem] * 7,
        out_specs=(vmem, vmem, vmem, vmem, smem, vmem),
        scratch_shapes=[pltpu.VMEM((512, NZC), F32), pltpu.VMEM((256, NZC), F32)],
        cost_estimate=pl.CostEstimate(flops=500_000_000, bytes_accessed=4_000_000, transcendentals=0),
        compiler_params=LIMIT,
        interpret=INTERPRET,
        name="output",
    )(position, mixing, corr, poly, flat, fresh, din, sine, inverse, onto)


def share_kernel(rows_ref, vec_ref, green_ref, over_x_ref, over_y_ref, edge_ref, out_ref, turn_ref, line_ref):
    fresh = jnp.concatenate([rows_ref[:, 0, :], rows_ref[:, 1, :]], 1)
    inputs = jnp.concatenate([rows_ref[:, 2, :], rows_ref[:, 3, :]], 1)
    cells = fresh * vec_ref[0:1, :256] + inputs * vec_ref[1:2, :256]
    cells = cells + (pltpu.roll(cells, 255, 1) + pltpu.roll(cells, 254, 1))
    modes = over_x_ref[0] * cells[0:1]
    for x in range(1, CG):
        modes = modes + over_x_ref[x] * cells[x : x + 1]
    cells = jnp.zeros((8, 256), F32)
    for ky in range(CG):
        acc = jnp.zeros((8, 256), F32)
        for j in range(8):
            at = ky * 8 + j
            acc = acc + jnp.broadcast_to(modes[:, G * ky + 3 * j : G * ky + 3 * j + 1], (8, 256)) * green_ref[8 * at : 8 * at + 8]
        cells = cells + over_y_ref[ky] * jnp.sum(acc, axis=0, keepdims=True)
    turn_ref[...] = jnp.concatenate([cells, jnp.zeros((120, 256), F32)], 0).T
    line_ref[...] = jnp.zeros_like(line_ref)
    for j in range(CZ):
        line_ref[:, 8 * j : 8 * j + 8] = turn_ref[pl.ds(j, DOMS, stride=8), :][:, :8]
    head = lax.broadcasted_iota(jnp.int32, (8, 128), 0) == 0
    edge = edge_ref[...]
    for d in range(DOMS):
        out_ref[d] = jnp.where(head, line_ref[d : d + 1], edge)


def hartree_shares(rows, vectors, green, over_x, over_y, edges):
    return pl.pallas_call(
        share_kernel,
        out_shape=jax.ShapeDtypeStruct((DOMS, 8, 128), F32),
        scratch_shapes=[pltpu.VMEM((256, 128), F32), pltpu.VMEM((DOMS, 128), F32)],
        compiler_params=LIMIT,
        interpret=INTERPRET,
        name="share",
    )(rows, vectors, green, over_x, over_y, edges)


def final_kernel(side_ref, msg_ref, own_ref, vec_ref, dens_ref, hart_ref):
    total = msg_ref[0]
    for d in range(1, DOMS):
        total = total + msg_ref[d]
    for j in range(CZ):
        hart_ref[j] = total[0:1, 8 * j : 8 * j + 8]
    lane = lax.broadcasted_iota(jnp.int32, (8, ROW), 1)

    def rows(tile):
        spread = [jnp.broadcast_to(tile[t + 1 : t + 2], (8, 128)) for t in range(7)]
        front = jnp.concatenate(spread[:5], 1)
        back = jnp.concatenate(spread[4:] + spread[5:], 1)
        return front, rolled(back, -64)

    left0, left2 = rows(msg_ref[side_ref[0]])
    right0, right2 = rows(msg_ref[side_ref[1]])
    far = G - BUFFER
    left_last = jnp.where(lane < HALF_ROW, rolled(left2, -far), rolled(left2, HALF_ROW + 12 - far))
    right_last = jnp.where(lane < HALF_ROW, rolled(right2, far), rolled(right2, HALF_ROW - 12 + far))
    left_part = (rolled(left0, -far), rolled(left0, -6), left_last)
    right_part = (rolled(right0, far), rolled(right0, 6), right_last)
    for p in range(PLANES):
        mixed = own_ref[p] + vec_ref[2:3, :GG] * left_part[p][0:1, :GG]
        dens_ref[p] = mixed + vec_ref[3:4, :GG] * right_part[p][0:1, :GG]


def final_parts(sides, msg, own, vectors):
    smem = pl.BlockSpec(memory_space=pltpu.SMEM)
    vmem = pl.BlockSpec(memory_space=pltpu.VMEM)
    return pl.pallas_call(
        final_kernel,
        out_shape=(
            jax.ShapeDtypeStruct((PLANES, 1, GG), F32),
            jax.ShapeDtypeStruct((CZ, 1, CG), F32),
        ),
        in_specs=[smem, vmem, vmem, vmem],
        out_specs=(vmem, vmem),
        compiler_params=LIMIT,
        interpret=INTERPRET,
        name="final",
    )(sides, msg, own, vectors)


def exchanged(x, axis):
    return lax.all_to_all(x, axis, split_axis=0, concat_axis=0, tiled=True)


def body(orbitals, potential, density_in, occupation, position, mixing, correlation_weight):
    sine, inverse, onto, gather, over_x, over_y = tables()
    shares = exchanged(filtered_shares(orbitals[0], potential[0]), "band")
    flat = shares.reshape(NB, SHARE)
    din = jnp.transpose(density_in, (1, 0, 2))
    grams = exchanged(packed_grams(flat), "band")
    poly, fresh, coarse = density_rows(grams, flat, occupation.reshape(1, NB), din, gather)
    rows = exchanged(coarse, "band")
    points, own, edges, vectors, sides, green = output_parts(
        position, mixing, correlation_weight, poly, flat, fresh, din, sine, inverse, onto
    )
    msg = exchanged(hartree_shares(rows, vectors, green, over_x, over_y, edges), "dom")
    dens, hart = final_parts(sides, msg, own, vectors)
    orbitals_out = jnp.transpose(points.reshape(PLANES, GG, NB), (2, 0, 1)).reshape(1, NB, PLANES, GG)
    density = jnp.transpose(dens, (1, 0, 2))
    hartree = jnp.transpose(hart, (1, 2, 0)).reshape(1, 1, CG, CZ)
    return orbitals_out, density, hartree


def solution(mesh):
    return jax.shard_map(
        body,
        mesh=mesh,
        in_specs=(
            P("dom", "band", None, None),
            P("dom", None, None),
            P("dom", "band", None),
            P(),
            P(),
            P(),
            P(),
        ),
        out_specs=(
            P("dom", None, "band", None),
            P("dom", "band", None),
            P("dom", "band", None, None),
        ),
        check_vma=False,
    )
```

time: 71.2 us -> 68.6 us (0.963)
  blocking collectives: 39.5 us -> 50 us
  waiting for transfers between devices: 7.5 us -> 1.77 us
  starting transfers between devices: 8.61 us -> 3.94 us
  Pallas kernels: 11.6 us -> 9.69 us
    all_to_all x2 -> x3, blocking collectives: 39.5 us -> 50 us  [exchanged(): return lax.all_to_all(x, axis, split_axis=0, concat_axis=0, tiled=True)]
    all_to_all x2 -> x1, waiting for transfers between devices: 7.5 us -> 1.77 us  [exchanged(): return lax.all_to_all(x, axis, split_axis=0, concat_axis=0, tiled=True)]
    all_to_all x2 -> x1, starting transfers between devices: 8.61 us -> 3.94 us  [exchanged(): return lax.all_to_all(x, axis, split_axis=0, concat_axis=0, tiled=True)]
    pallas_call x1 -> x0, Pallas kernels: 1.47 us -> none  [prepared(): pl.pallas_call(prepare_kernel, out_shape=(jax.ShapeDtypeStruct((8, ROW),...]
    pallas_call x1, Pallas kernels: 3.77 us -> 3 us  [filtered_shares(): pl.pallas_call(filter_kernel, out_shape=jax.ShapeDtypeStruct((BANDS, LOCA...]
    pallas_call x1, Pallas kernels: 1.5 us -> 2.27 us  [output_parts(): pl.pallas_call(output_kernel, out_shape=(jax.ShapeDtypeStruct((PLANES * G...]
    pallas_call x1, Pallas kernels: 1.34 us -> 0.62 us  [packed_grams(): pl.pallas_call(gram_kernel, out_shape=jax.ShapeDtypeStruct((BANDS, PACKED...]
    unnamed x26 -> x24, local copies, waits for them, and re-layouts: 2.67 us -> 2.15 us
  transfers between devices with their start and end apart: 2 -> 1, of which waited for: 2 -> 1; matrix products, arithmetic and copies ran while one was open for 0% -> 0% of each run, Pallas kernels for 4% -> 3%
where the time goes in v2:
time: 68.6 us; the launch traced here: 68.2 us
  blocking collectives  50 us (73%)
  Pallas kernels  9.69 us (14%)
  starting transfers between devices  3.94 us (6%)
  local copies, waits for them, and re-layouts  2.15 us (3%)
  waiting for transfers between devices  1.77 us (3%)
  between operations  0.72 us (1%)
    all_to_all x3, blocking collectives, exchanged(): return lax.all_to_all(x, axis, split_axis=0, concat_axis=0, tiled=True)  50 us
    all_to_all x1, starting transfers between devices, exchanged(): return lax.all_to_all(x, axis, split_axis=0, concat_axis=0, tiled=True)  3.94 us
    pallas_call x1, Pallas kernels, filtered_shares(): pl.pallas_call(filter_kernel, out_shape=jax.ShapeDtypeStruct((BANDS, LOCA...  3 us
    pallas_call x1, Pallas kernels, output_parts(): pl.pallas_call(output_kernel, out_shape=(jax.ShapeDtypeStruct((PLANES * G...  2.27 us
    unnamed x24, local copies, waits for them, and re-layouts  2.15 us
    pallas_call x1, Pallas kernels, density_rows(): pl.pallas_call(density_kernel, out_shape=(jax.ShapeDtypeStruct((NB, NB),...  2.02 us
    all_to_all x1, waiting for transfers between devices, exchanged(): return lax.all_to_all(x, axis, split_axis=0, concat_axis=0, tiled=True)  1.77 us
  transfers between devices with their start and end apart: 1, of which 1 were waited for; matrix products, arithmetic and copies ran while one was open for 0% of the time, Pallas kernels for 3%

profile of v2, /device:TPU:1, one launch (start us, length us, event | category | flops | bytes accessed | tf_op | source)
XLA Modules:
  0.0 68.2 jit_solution(15280978241930508783)
XLA Ops:
  0.6 0.0 copy-start.3
  0.6 0.8 %copy-done.3 = f32[1,24,576]{2,1,0:T(8,128)S(1)} copy-done((f32[1,24,576]{2,1,0:T(8,128)S(1)}, f32[1,24,576]{2,1,0:T(8,128)}, u32[]{:S(2)}) %copy-start.3) | copy-done | bytes 55320
  1.5 3.0 %filter.1 = f32[8,16,1792]{2,1,0:T(8,128)S(1)} custom-call(f32[16,24,576]{2,1,0:T(8,128)} %bitcast.23, f32[24,576]{1,0:T(8,128)S(1)} %bitcast.19), custom_call_target="tpu_custom_call" | custom-call | tf_op jit(solution)/shard_map/filter/pallas_call | solution.py:150
  4.5 19.3 %all_to_all.20 = f32[8,16,1792]{2,1,0:T(8,128)S(1)} all-to-all(f32[8,16,1792]{2,1,0:T(8,128)S(1)} %filter.1), channel_id=1, replica_groups=mesh['dom'=32,'band'=8] {'band'}, dimensions={0} | all-to-all | bytes 1835008 | tf_op jit(solution)/shard_map/all_to_all | solution.py:443
  23.8 0.0 copy-start
  23.8 0.6 gram.1
  24.4 0.0 copy-start.4
  24.4 10.5 %all_to_all.21.g_ref = f32[8,72,128]{2,1,0:T(8,128)S(1)} all-to-all(f32[8,72,128]{2,1,0:T(8,128)S(1)} %gram.1), channel_id=1, replica_groups=mesh['dom'=32,'band'=8] {'band'}, dimensions={0} | all-to-all | bytes 589824 | tf_op jit(solution)/shard_map/all_to_all | solution.py:443
  34.9 0.0 copy-start.5
  34.9 0.0 copy-done
  34.9 0.0 copy-done.4
  34.9 0.6 copy-done.5
  35.6 0.0 copy-start.9
  35.6 0.0 copy-start.11
  35.6 2.0 %density.1 = (f32[128,128]{1,0:T(8,128)S(1)}, f32[8,1792]{1,0:T(8,128)S(1)}, f32[8,8,128]{2,1,0:T(8,128)}) custom-call(f32[8,72,128]{2,1,0:T(8,128)S(1)} %all_to_all.21.g_ref, f32[128,1792]{1,0:T(8,128)S(1)} %bitcast.17, f32[1,128]{1,0:T(1,128)S(1)} %bitcast.22, f32[3,1,576]{2,1,0:T(1,128)S(1)} %bitcast.20, f32[640,256]{1,0:T(8,128)S(1)} %copy-done), custom_call_target="tpu_custom_call" | custom-call | tf_op jit(solution)/shard_map/density/pallas_call | solution.py:246
  37.6 0.0 copy-start.10
  37.6 3.9 %all-to-all-start.2 = ((f32[8,8,128]{2,1,0:T(8,128)}), f32[8,8,128]{2,1,0:T(8,128)S(1)}, u32[]{:S(2)}, u32[]{:S(2)}) async-start(f32[8,8,128]{2,1,0:T(8,128)} %get-tuple-element.18), calls=%async_computation.2 | async-start | bytes 65536 | tf_op jit(solution)/shard_map/all_to_all | solution.py:443
  41.6 0.0 copy-start.6
  41.6 0.0 copy-start.7
  41.6 0.0 copy-start.8
  41.6 0.0 copy-done.9
  41.6 0.0 copy-done.11
  41.6 0.0 copy-done.10
  41.6 0.6 copy-done.6
  42.2 0.0 copy-done.7
  42.2 0.0 copy-done.8
  42.2 0.0 copy-start.1
  42.2 0.0 copy-start.2
  42.2 2.3 %output.1 = (f32[1728,128]{1,0:T(8,128)}, f32[3,1,576]{2,1,0:T(1,128)S(1)}, f32[8,128]{1,0:T(8,128)S(1)}, f32[8,640]{1,0:T(8,128)S(1)}, s32[2]{0:T(128)S(1)}, /*index=5*/f32[512,256]{1,0:T(8,128)S(1)}) custom-call(s32[32]{0:T(128)S(1)} %copy-done.6, s32[2]{0:T(128)S(1)} %copy-done.7, s32[6]{0:T(128)S(1)} %copy-done.8, ...), custom_call_target="tpu_custom_call" | custom-call | flops 500000000 | bytes 4000000 | tf_op jit(solution)/shard_map/output/pallas_call | solution.py:343
  44.5 1.8 %all-to-all-done.2.rows_ref = f32[8,8,128]{2,1,0:T(8,128)S(1)} async-done(((f32[8,8,128]{2,1,0:T(8,128)}), f32[8,8,128]{2,1,0:T(8,128)S(1)}, u32[]{:S(2)}, u32[]{:S(2)}) %all-to-all-start.2) | async-done | bytes 32800 | tf_op jit(solution)/shard_map/all_to_all | solution.py:443
  46.3 0.0 copy-done.1
  46.3 0.0 copy-done.2
  46.3 0.5 share.1
  46.8 20.2 %all_to_all.22.msg_ref = f32[32,8,128]{2,1,0:T(8,128)S(1)} all-to-all(f32[32,8,128]{2,1,0:T(8,128)S(1)} %share.1), channel_id=1, replica_groups=mesh['dom'=32,'band'=8] {'dom'}, dimensions={0} | all-to-all | bytes 262144 | tf_op jit(solution)/shard_map/all_to_all | solution.py:443
  66.9 1.3 %final.1 = (f32[3,1,576]{2,1,0:T(1,128)}, f32[6,1,8]{2,1,0:T(1,128)}) custom-call(s32[2]{0:T(128)S(1)} %get-tuple-element.17.side_ref, f32[32,8,128]{2,1,0:T(8,128)S(1)} %all_to_all.22.msg_ref, f32[3,1,576]{2,1,0:T(1,128)S(1)} %get-tuple-element.22.own_ref, f32[8,640]{1,0:T(8,128)S(1)} %get-tuple-element.19.vec_ref), custom_call_target="tpu_custom_call" | custom-call | tf_op jit(solution)/shard_map/final/pallas_call | solution.py:428
Async XLA Ops:
  0.6 0.8 %copy-start.3 = (f32[1,24,576]{2,1,0:T(8,128)S(1)}, f32[1,24,576]{2,1,0:T(8,128)}, u32[]{:S(2)}) copy-start(f32[1,24,576]{2,1,0:T(8,128)} %param.14) | copy-start | bytes 165892
  23.8 11.2 %copy-start = (f32[640,256]{1,0:T(8,128)S(1)}, f32[640,256]{1,0:T(8,128)}, u32[]{:S(2)}) copy-start(f32[640,256]{1,0:T(8,128)} %constant.12.clone.gather_ref) | copy-start | bytes 1966084
  24.4 10.5 %copy-start.4 = (f32[1,3,576]{2,0,1:T(1,128)S(1)}, f32[1,3,576]{2,0,1:T(1,128)}, u32[]{:S(2)}) copy-start(f32[1,3,576]{2,0,1:T(1,128)} %param.15) | copy-start | bytes 20740
  34.9 0.7 copy-start.5
  35.6 6.0 %copy-start.9 = (f32[32,8,192]{2,1,0:T(8,128)S(1)}, f32[32,8,192]{2,1,0:T(8,128)}, u32[]{:S(2)}) copy-start(f32[32,8,192]{2,1,0:T(8,128)} %constant.13.clone.sine_ref) | copy-start | bytes 589828
  35.6 6.0 %copy-start.11 = (f32[64,192]{1,0:T(8,128)S(1)}, f32[64,192]{1,0:T(8,128)}, u32[]{:S(2)}) copy-start(f32[64,192]{1,0:T(8,128)} %constant.14.clone.inverse_ref) | copy-start | bytes 147460
  37.6 4.0 %copy-start.10 = (f32[8,8,192]{2,1,0:T(8,128)S(1)}, f32[8,8,192]{2,1,0:T(8,128)}, u32[]{:S(2)}) copy-start(f32[8,8,192]{2,1,0:T(8,128)} %constant.15.clone.onto_ref) | copy-start | bytes 147460
  37.6 8.7 %all-to-all-start.2 = ((f32[8,8,128]{2,1,0:T(8,128)}), f32[8,8,128]{2,1,0:T(8,128)S(1)}, u32[]{:S(2)}, u32[]{:S(2)}) async-start(f32[8,8,128]{2,1,0:T(8,128)} %get-tuple-element.18), calls=%async_computation.2 | async-start | bytes 65536 | tf_op jit(solution)/shard_map/all_to_all | solution.py:443
  41.6 0.7 copy-start.6
  41.6 0.7 copy-start.7
  41.6 0.7 %copy-start.8 = (s32[6]{0:T(128)S(1)}, s32[6]{0:T(128)}, u32[]{:S(2)}) copy-start(s32[6]{0:T(128)} %corr_ref.1) | copy-start | bytes 76
  42.2 4.1 %copy-start.1 = (f32[8,8,256]{2,1,0:T(8,128)S(1)}, f32[8,8,256]{2,1,0:T(8,128)}, u32[]{:S(2)}) copy-start(f32[8,8,256]{2,1,0:T(8,128)} %constant.17.clone.over_y_ref) | copy-start | bytes 196612
  42.2 4.1 %copy-start.2 = (f32[8,8,256]{2,1,0:T(8,128)S(1)}, f32[8,8,256]{2,1,0:T(8,128)}, u32[]{:S(2)}) copy-start(f32[8,8,256]{2,1,0:T(8,128)} %constant.16.clone.over_x_ref) | copy-start | bytes 196612

commit v3 on v2

--- a/solution.py
+++ b/solution.py
@@ -31,7 +31,6 @@
 HIGHEST = lax.Precision.HIGHEST
 F32 = jnp.float32
 INTERPRET = False
-FILTER_LIMIT = pltpu.CompilerParams(vmem_limit_bytes=55_250_000)
 LIMIT = pltpu.CompilerParams(vmem_limit_bytes=16 << 20)
 
 
@@ -96,20 +95,13 @@
         mat_ref[top:end, 128 * t : 128 * (t + 1)] = jnp.where(hit, 1.0, 0.0).astype(jnp.bfloat16)
 
 
-def filter_kernel(orb_ref, pot_ref, out_ref, in_ref, pot_in, mat_ref, zero_ref, first_ref, side_ref, diag_ref, sems):
-    copies = [pltpu.make_async_copy(pot_ref, pot_in, sems.at[3])]
-    for c in range(3):
-        part = pl.ds(8 * c, 8)
-        copies.append(pltpu.make_async_copy(orb_ref.at[:, part, :], in_ref.at[c], sems.at[c]))
-    for copy in copies:
-        copy.start()
-    neighbour_matrix(mat_ref)
-    lane = lax.broadcasted_iota(jnp.int32, (1, ROW), 1)
-    step = jnp.where(lane < GG, 0.5 / HALF, 0.0)
+def filter_kernel(orb_ref, pot_ref, mat_ref, occ_ref, out_ref, weight_ref, zero_ref, first_ref, side_ref, diag_ref):
+    eye = lax.broadcasted_iota(jnp.int32, (NB, NB), 0) == lax.broadcasted_iota(jnp.int32, (NB, NB), 1)
+    weight = jnp.sum(jnp.where(eye, occ_ref[...] * (1.0 / NB), 0.0), axis=1, keepdims=True)
+    weight_ref[...] = jnp.broadcast_to(weight, (NB, 256))
     diag_ref[:, GG - 64 :] = jnp.zeros((G, 128), F32)
     zero_ref[:, :, GG - 64 :] = jnp.zeros((G, LOCAL, 128), F32)
-    copies[0].wait()
-    diag_ref[:, :GG] = (pot_in[...] + (3.0 - CENTER)) * (1.0 / HALF)
+    diag_ref[:, :GG] = (pot_ref[...] + (3.0 - CENTER)) * 2.0
     dot = functools.partial(jnp.dot, preferred_element_type=F32)
 
     def sum_sides(source, c):
@@ -127,45 +119,49 @@
             near = near + source[x - 1]
         if x + 1 < G:
             near = near + source[x + 1]
-        return diag_ref[x : x + 1] * v - step * near
+        return diag_ref[x : x + 1] * v - near
 
     for c in range(3):
-        copies[c + 1].wait()
         for x in range(8 * c, 8 * c + 8):
-            zero_ref[x, :, :GG] = in_ref[c, :, x - 8 * c, :]
+            zero_ref[x, :, :GG] = orb_ref[:, x, :]
         sum_sides(zero_ref, c)
     for x in range(G):
         first_ref[x] = applied(zero_ref, x)
     for c in range(3):
         sum_sides(first_ref, c)
     for x in range(G):
-        second = 2.0 * applied(first_ref, x) - zero_ref[x]
+        second = (0.5 / HALF**2) * applied(first_ref, x) - zero_ref[x]
         p = x % PLANES
         out_ref[x // PLANES, :, p * GG : (p + 1) * GG] = second[:, :GG]
         if p == PLANES - 1:
             out_ref[x // PLANES, :, PLANES * GG :] = jnp.zeros((LOCAL, SHARE - PLANES * GG), F32)
 
 
-def filtered_shares(orbitals, potential):
+def filtered_shares(orbitals, potential, occupation):
+    matrix = pl.pallas_call(
+        neighbour_matrix,
+        out_shape=jax.ShapeDtypeStruct((ROW, ROW), jnp.bfloat16),
+        cost_estimate=pl.CostEstimate(flops=20_000_000_000, bytes_accessed=4_000_000, transcendentals=0),
+        compiler_params=LIMIT,
+        interpret=INTERPRET,
+        name="matrix",
+    )()
     return pl.pallas_call(
         filter_kernel,
-        out_shape=jax.ShapeDtypeStruct((BANDS, LOCAL, SHARE), F32),
-        in_specs=[pl.BlockSpec(memory_space=pltpu.HBM)] * 2,
-        out_specs=pl.BlockSpec(memory_space=pltpu.VMEM),
+        out_shape=(
+            jax.ShapeDtypeStruct((BANDS, LOCAL, SHARE), F32),
+            jax.ShapeDtypeStruct((NB, 256), F32),
+        ),
         scratch_shapes=[
-            pltpu.VMEM((3, LOCAL, 8, GG), F32),
-            pltpu.VMEM((G, GG), F32),
-            pltpu.VMEM((ROW, ROW), jnp.bfloat16),
             pltpu.VMEM((G, LOCAL, ROW), F32),
             pltpu.VMEM((G, LOCAL, ROW), F32),
             pltpu.VMEM((G, LOCAL, ROW), F32),
             pltpu.VMEM((G, ROW), F32),
-            pltpu.SemaphoreType.DMA((4,)),
         ],
-        compiler_params=FILTER_LIMIT,
+        compiler_params=LIMIT,
         interpret=INTERPRET,
         name="filter",
-    )(orbitals, potential)
+    )(orbitals, potential, matrix, occupation)
 
 
 def gram_kernel(f_ref, out_ref):
@@ -196,7 +192,7 @@
     )(flat)
 
 
-def density_kernel(g_ref, f_ref, occ_ref, din_ref, gather_ref, poly_ref, fresh_ref, coarse_ref, rows_ref):
+def density_kernel(g_ref, f_ref, weight_ref, din_ref, gather_ref, poly_ref, fresh_ref, coarse_ref, rows_ref):
     total = g_ref[0]
     for k in range(1, BANDS):
         total = total + g_ref[k]
@@ -221,13 +217,11 @@
     poly_high, poly_low = halves(poly)
     both = jnp.concatenate([poly_high, poly_low], 1)
     dot = functools.partial(jnp.dot, preferred_element_type=F32)
-    weight = jnp.sum(eye * (occ_ref[...] * (1.0 / NB)), axis=1, keepdims=True)
-    weight = jnp.broadcast_to(weight, (NB, 256))
     for c in range(SHARE // 256):
         cols = slice(256 * c, 256 * (c + 1))
         high, low = halves(f_ref[:, cols])
         current = dot(both, jnp.concatenate([high, high], 0)) + dot(poly_high, low)
-        line = jnp.sum(current * current * weight, axis=0, keepdims=True)
+        line = jnp.sum(current * current * weight_ref[...], axis=0, keepdims=True)
         fresh_ref[:, cols] = jnp.broadcast_to(line, (8, 256))
     planes = fresh_ref[:, :ROW] + fresh_ref[:, GG : GG + ROW] + fresh_ref[:, 2 * GG : 2 * GG + ROW]
     rows_ref[...] = jnp.zeros_like(rows_ref)
@@ -242,7 +236,7 @@
         coarse_ref[k] = tile
 
 
-def density_rows(grams, flat, occupation, din, gather):
+def density_rows(grams, flat, weight, din, gather):
     return pl.pallas_call(
         density_kernel,
         out_shape=(
@@ -254,7 +248,7 @@
         compiler_params=LIMIT,
         interpret=INTERPRET,
         name="density",
-    )(grams, flat, occupation, din, gather)
+    )(grams, flat, weight, din, gather)
 
 
 def output_kernel(
@@ -445,11 +439,12 @@
 
 def body(orbitals, potential, density_in, occupation, position, mixing, correlation_weight):
     sine, inverse, onto, gather, over_x, over_y = tables()
-    shares = exchanged(filtered_shares(orbitals[0], potential[0]), "band")
+    filtered, weight = filtered_shares(orbitals[0], potential[0], occupation.reshape(1, NB))
+    shares = exchanged(filtered, "band")
     flat = shares.reshape(NB, SHARE)
     din = jnp.transpose(density_in, (1, 0, 2))
     grams = exchanged(packed_grams(flat), "band")
-    poly, fresh, coarse = density_rows(grams, flat, occupation.reshape(1, NB), din, gather)
+    poly, fresh, coarse = density_rows(grams, flat, weight, din, gather)
     rows = exchanged(coarse, "band")
     points, own, edges, vectors, sides, green = output_parts(
         position, mixing, correlation_weight, poly, flat, fresh, din, sine, inverse, onto

time: 68.6 us -> 66.8 us (0.974)
  Pallas kernels: 9.69 us -> 8.39 us
    pallas_call x1 -> x2, Pallas kernels: 3 us -> 1.69 us  [the longest x1 1.5 us: filtered_shares(): pl.pallas_call(filter_kernel, out_shape=(jax.ShapeDtypeStruct((BANDS, LOC...]
    unnamed x24 -> x26, local copies, waits for them, and re-layouts: 2.15 us -> 1.69 us
where the time goes in v3:
time: 66.8 us; the launch traced here: 66.5 us
  blocking collectives  50 us (75%)
  Pallas kernels  8.39 us (13%)
  starting transfers between devices  3.94 us (6%)
  waiting for transfers between devices  1.77 us (3%)
  local copies, waits for them, and re-layouts  1.69 us (3%)
  between operations  0.73 us (1%)
    all_to_all x3, blocking collectives, exchanged(): return lax.all_to_all(x, axis, split_axis=0, concat_axis=0, tiled=True)  50 us
    all_to_all x1, starting transfers between devices, exchanged(): return lax.all_to_all(x, axis, split_axis=0, concat_axis=0, tiled=True)  3.94 us
    pallas_call x1, Pallas kernels, output_parts(): pl.pallas_call(output_kernel, out_shape=(jax.ShapeDtypeStruct((PLANES * G...  2.27 us
    pallas_call x1, Pallas kernels, density_rows(): pl.pallas_call(density_kernel, out_shape=(jax.ShapeDtypeStruct((NB, NB),...  2.02 us
    all_to_all x1, waiting for transfers between devices, exchanged(): return lax.all_to_all(x, axis, split_axis=0, concat_axis=0, tiled=True)  1.77 us
    unnamed x26, local copies, waits for them, and re-layouts  1.69 us
    pallas_call x1, Pallas kernels, filtered_shares(): pl.pallas_call(filter_kernel, out_shape=(jax.ShapeDtypeStruct((BANDS, LOC...  1.5 us
  transfers between devices with their start and end apart: 1, of which 1 were waited for; matrix products, arithmetic and copies ran while one was open for 0% of the time, Pallas kernels for 3%

profile of v3, /device:TPU:1, one launch (start us, length us, event | category | flops | bytes accessed | tf_op | source)
XLA Modules:
  0.0 66.5 jit_solution(1895281000747761309)
XLA Ops:
  0.6 0.0 copy-start.4
  0.6 0.0 copy-start
  0.6 0.2 matrix.1.mat_ref
  0.9 0.0 copy-start.6
  0.9 0.6 copy-done.4
  1.5 0.4 copy-done
  1.9 0.0 copy-done.6
  1.9 1.5 %filter.1 = (f32[8,16,1792]{2,1,0:T(8,128)S(1)}, f32[128,256]{1,0:T(8,128)S(1)}) custom-call(f32[16,24,576]{2,1,0:T(8,128)S(1)} %bitcast.19, f32[24,576]{1,0:T(8,128)S(1)} %bitcast.20, bf16[640,640]{1,0:T(8,128)(2,1)S(1)} %matrix.1.mat_ref, f32[1,128]{1,0:T(1,128)S(1)} %bitcast.23), custom_call_target="tpu_custom_call" | custom-call | tf_op jit(solution)/shard_map/filter/pallas_call | solution.py:149
  3.4 19.3 %all_to_all.20 = f32[8,16,1792]{2,1,0:T(8,128)S(1)} all-to-all(f32[8,16,1792]{2,1,0:T(8,128)S(1)} %get-tuple-element.16), channel_id=1, replica_groups=mesh['dom'=32,'band'=8] {'band'}, dimensions={0} | all-to-all | bytes 1835008 | tf_op jit(solution)/shard_map/all_to_all | solution.py:437
  22.7 0.0 copy-start.1
  22.7 0.0 copy-start.5
  22.7 0.6 gram.1
  23.3 10.5 %all_to_all.21.g_ref = f32[8,72,128]{2,1,0:T(8,128)S(1)} all-to-all(f32[8,72,128]{2,1,0:T(8,128)S(1)} %gram.1), channel_id=1, replica_groups=mesh['dom'=32,'band'=8] {'band'}, dimensions={0} | all-to-all | bytes 589824 | tf_op jit(solution)/shard_map/all_to_all | solution.py:437
  33.8 0.0 copy-done.1
  33.8 0.0 copy-done.5
  33.8 0.0 copy-start.10
  33.8 0.0 copy-start.12
  33.8 2.0 %density.1 = (f32[128,128]{1,0:T(8,128)S(1)}, f32[8,1792]{1,0:T(8,128)S(1)}, f32[8,8,128]{2,1,0:T(8,128)}) custom-call(f32[8,72,128]{2,1,0:T(8,128)S(1)} %all_to_all.21.g_ref, f32[128,1792]{1,0:T(8,128)S(1)} %bitcast.17, f32[128,256]{1,0:T(8,128)S(1)} %get-tuple-element.17.weight_ref, f32[3,1,576]{2,1,0:T(1,128)S(1)} %bitcast.21, f32[640,256]{1,0:T(8,128)S(1)} %copy-done.1), custom_call_target="tpu_custom_call" | custom-call | tf_op jit(solution)/shard_map/density/pallas_call | solution.py:240
  35.9 0.0 copy-start.11
  35.9 3.9 %all-to-all-start.2 = ((f32[8,8,128]{2,1,0:T(8,128)}), f32[8,8,128]{2,1,0:T(8,128)S(1)}, u32[]{:S(2)}, u32[]{:S(2)}) async-start(f32[8,8,128]{2,1,0:T(8,128)} %get-tuple-element.22), calls=%async_computation.2 | async-start | bytes 65536 | tf_op jit(solution)/shard_map/all_to_all | solution.py:437
  39.8 0.0 copy-start.7
  39.8 0.0 copy-start.8
  39.8 0.0 copy-start.9
  39.8 0.0 copy-done.10
  39.8 0.0 copy-done.12
  39.8 0.0 copy-done.11
  39.9 0.6 copy-done.7
  40.5 0.0 copy-done.8
  40.5 0.0 copy-done.9
  40.5 0.0 copy-start.2
  40.5 0.0 copy-start.3
  40.5 2.3 %output.1 = (f32[1728,128]{1,0:T(8,128)}, f32[3,1,576]{2,1,0:T(1,128)S(1)}, f32[8,128]{1,0:T(8,128)S(1)}, f32[8,640]{1,0:T(8,128)S(1)}, s32[2]{0:T(128)S(1)}, /*index=5*/f32[512,256]{1,0:T(8,128)S(1)}) custom-call(s32[32]{0:T(128)S(1)} %copy-done.7, s32[2]{0:T(128)S(1)} %copy-done.8, s32[6]{0:T(128)S(1)} %copy-done.9, ...), custom_call_target="tpu_custom_call" | custom-call | flops 500000000 | bytes 4000000 | tf_op jit(solution)/shard_map/output/pallas_call | solution.py:337
  42.8 1.8 %all-to-all-done.2.rows_ref = f32[8,8,128]{2,1,0:T(8,128)S(1)} async-done(((f32[8,8,128]{2,1,0:T(8,128)}), f32[8,8,128]{2,1,0:T(8,128)S(1)}, u32[]{:S(2)}, u32[]{:S(2)}) %all-to-all-start.2) | async-done | bytes 32800 | tf_op jit(solution)/shard_map/all_to_all | solution.py:437
  44.5 0.0 copy-done.2
  44.5 0.0 copy-done.3
  44.6 0.5 share.1
  45.0 20.1 %all_to_all.22.msg_ref = f32[32,8,128]{2,1,0:T(8,128)S(1)} all-to-all(f32[32,8,128]{2,1,0:T(8,128)S(1)} %share.1), channel_id=1, replica_groups=mesh['dom'=32,'band'=8] {'dom'}, dimensions={0} | all-to-all | bytes 262144 | tf_op jit(solution)/shard_map/all_to_all | solution.py:437
  65.2 1.3 %final.1 = (f32[3,1,576]{2,1,0:T(1,128)}, f32[6,1,8]{2,1,0:T(1,128)}) custom-call(s32[2]{0:T(128)S(1)} %get-tuple-element.21.side_ref, f32[32,8,128]{2,1,0:T(8,128)S(1)} %all_to_all.22.msg_ref, f32[3,1,576]{2,1,0:T(1,128)S(1)} %get-tuple-element.26.own_ref, f32[8,640]{1,0:T(8,128)S(1)} %get-tuple-element.23.vec_ref), custom_call_target="tpu_custom_call" | custom-call | tf_op jit(solution)/shard_map/final/pallas_call | solution.py:422
Async XLA Ops:
  0.6 0.8 %copy-start.4 = (f32[1,24,576]{2,1,0:T(8,128)S(1)}, f32[1,24,576]{2,1,0:T(8,128)}, u32[]{:S(2)}) copy-start(f32[1,24,576]{2,1,0:T(8,128)} %param.14) | copy-start | bytes 165892
  0.6 1.2 %copy-start = (f32[1,16,24,576]{3,2,1,0:T(8,128)S(1)}, f32[1,16,24,576]{3,2,1,0:T(8,128)}, u32[]{:S(2)}) copy-start(f32[1,16,24,576]{3,2,1,0:T(8,128)} %param.13) | copy-start | bytes 2654212
  0.9 1.0 %copy-start.6 = (f32[128]{0:T(128)S(1)}, f32[128]{0:T(128)}, u32[]{:S(2)}) copy-start(f32[128]{0:T(128)} %param.16) | copy-start | bytes 1540
  22.7 11.2 %copy-start.1 = (f32[640,256]{1,0:T(8,128)S(1)}, f32[640,256]{1,0:T(8,128)}, u32[]{:S(2)}) copy-start(f32[640,256]{1,0:T(8,128)} %constant.12.clone.gather_ref) | copy-start | bytes 1966084
  22.7 11.2 %copy-start.5 = (f32[1,3,576]{2,0,1:T(1,128)S(1)}, f32[1,3,576]{2,0,1:T(1,128)}, u32[]{:S(2)}) copy-start(f32[1,3,576]{2,0,1:T(1,128)} %param.15) | copy-start | bytes 20740
  33.8 6.0 %copy-start.10 = (f32[32,8,192]{2,1,0:T(8,128)S(1)}, f32[32,8,192]{2,1,0:T(8,128)}, u32[]{:S(2)}) copy-start(f32[32,8,192]{2,1,0:T(8,128)} %constant.13.clone.sine_ref) | copy-start | bytes 589828
  33.8 6.0 %copy-start.12 = (f32[64,192]{1,0:T(8,128)S(1)}, f32[64,192]{1,0:T(8,128)}, u32[]{:S(2)}) copy-start(f32[64,192]{1,0:T(8,128)} %constant.14.clone.inverse_ref) | copy-start | bytes 147460
  35.9 4.0 %copy-start.11 = (f32[8,8,192]{2,1,0:T(8,128)S(1)}, f32[8,8,192]{2,1,0:T(8,128)}, u32[]{:S(2)}) copy-start(f32[8,8,192]{2,1,0:T(8,128)} %constant.15.clone.onto_ref) | copy-start | bytes 147460
  35.9 8.7 %all-to-all-start.2 = ((f32[8,8,128]{2,1,0:T(8,128)}), f32[8,8,128]{2,1,0:T(8,128)S(1)}, u32[]{:S(2)}, u32[]{:S(2)}) async-start(f32[8,8,128]{2,1,0:T(8,128)} %get-tuple-element.22), calls=%async_computation.2 | async-start | bytes 65536 | tf_op jit(solution)/shard_map/all_to_all | solution.py:437
  39.8 0.7 copy-start.7
  39.8 0.7 %copy-start.8 = (s32[2]{0:T(128)S(1)}, s32[2]{0:T(128)}, u32[]{:S(2)}) copy-start(s32[2]{0:T(128)} %mix_ref.1) | copy-start | bytes 28
  39.8 0.7 %copy-start.9 = (s32[6]{0:T(128)S(1)}, s32[6]{0:T(128)}, u32[]{:S(2)}) copy-start(s32[6]{0:T(128)} %corr_ref.1) | copy-start | bytes 76
  40.5 4.1 %copy-start.2 = (f32[8,8,256]{2,1,0:T(8,128)S(1)}, f32[8,8,256]{2,1,0:T(8,128)}, u32[]{:S(2)}) copy-start(f32[8,8,256]{2,1,0:T(8,128)} %constant.17.clone.over_y_ref) | copy-start | bytes 196612
  40.5 4.1 %copy-start.3 = (f32[8,8,256]{2,1,0:T(8,128)S(1)}, f32[8,8,256]{2,1,0:T(8,128)}, u32[]{:S(2)}) copy-start(f32[8,8,256]{2,1,0:T(8,128)} %constant.16.clone.over_x_ref) | copy-start | bytes 196612

commit v4 on v3

--- a/solution.py
+++ b/solution.py
@@ -95,10 +95,7 @@
         mat_ref[top:end, 128 * t : 128 * (t + 1)] = jnp.where(hit, 1.0, 0.0).astype(jnp.bfloat16)
 
 
-def filter_kernel(orb_ref, pot_ref, mat_ref, occ_ref, out_ref, weight_ref, zero_ref, first_ref, side_ref, diag_ref):
-    eye = lax.broadcasted_iota(jnp.int32, (NB, NB), 0) == lax.broadcasted_iota(jnp.int32, (NB, NB), 1)
-    weight = jnp.sum(jnp.where(eye, occ_ref[...] * (1.0 / NB), 0.0), axis=1, keepdims=True)
-    weight_ref[...] = jnp.broadcast_to(weight, (NB, 256))
+def filter_kernel(orb_ref, pot_ref, mat_ref, vec_ref, out_ref, zero_ref, first_ref, side_ref, diag_ref):
     diag_ref[:, GG - 64 :] = jnp.zeros((G, 128), F32)
     zero_ref[:, :, GG - 64 :] = jnp.zeros((G, LOCAL, 128), F32)
     diag_ref[:, :GG] = (pot_ref[...] + (3.0 - CENTER)) * 2.0
@@ -137,7 +134,7 @@
             out_ref[x // PLANES, :, PLANES * GG :] = jnp.zeros((LOCAL, SHARE - PLANES * GG), F32)
 
 
-def filtered_shares(orbitals, potential, occupation):
+def filtered_shares(orbitals, potential, vectors):
     matrix = pl.pallas_call(
         neighbour_matrix,
         out_shape=jax.ShapeDtypeStruct((ROW, ROW), jnp.bfloat16),
@@ -148,10 +145,7 @@
     )()
     return pl.pallas_call(
         filter_kernel,
-        out_shape=(
-            jax.ShapeDtypeStruct((BANDS, LOCAL, SHARE), F32),
-            jax.ShapeDtypeStruct((NB, 256), F32),
-        ),
+        out_shape=jax.ShapeDtypeStruct((BANDS, LOCAL, SHARE), F32),
         scratch_shapes=[
             pltpu.VMEM((G, LOCAL, ROW), F32),
             pltpu.VMEM((G, LOCAL, ROW), F32),
@@ -161,7 +155,7 @@
         compiler_params=LIMIT,
         interpret=INTERPRET,
         name="filter",
-    )(orbitals, potential, matrix, occupation)
+    )(orbitals, potential, matrix, vectors)
 
 
 def gram_kernel(f_ref, out_ref):
@@ -192,7 +186,11 @@
     )(flat)
 
 
-def density_kernel(g_ref, f_ref, weight_ref, din_ref, gather_ref, poly_ref, fresh_ref, coarse_ref, rows_ref):
+def density_kernel(
+    g_ref, f_ref, weight_ref, din_ref, gather_ref, vec_ref,
+    out_ref, coarse_ref, own_ref, edge_ref,
+    point_ref, fresh_ref, rows_ref, sems,
+):
     total = g_ref[0]
     for k in range(1, BANDS):
         total = total + g_ref[k]
@@ -213,19 +211,31 @@
     square = dot3(a, a)
     tail = dot3(square, 0.0625 * square - 0.5625 * a)
     poly = scaling * (2.25 * eye + (1.6875 * square - 2.4375 * a) + tail)
-    poly_ref[...] = poly
     poly_high, poly_low = halves(poly)
+    dot = functools.partial(jnp.dot, preferred_element_type=F32)
+
+    copies = []
+    for c in range(7):
+        start, count = 256 * c, min(256, PLANES * GG - 256 * c)
+        for at in range(start, start + count, 128):
+            high, low = halves(f_ref[:, at : at + 128].T)
+            value = dot(high, poly_high) + (dot(high, poly_low) + dot(low, poly_high))
+            point_ref[at : at + 128] = value
+        part = pl.ds(start, count)
+        copies.append(pltpu.make_async_copy(point_ref.at[part], out_ref.at[part], sems.at[c]))
+        copies[-1].start()
+
     both = jnp.concatenate([poly_high, poly_low], 1)
-    dot = functools.partial(jnp.dot, preferred_element_type=F32)
     for c in range(SHARE // 256):
         cols = slice(256 * c, 256 * (c + 1))
         high, low = halves(f_ref[:, cols])
         current = dot(both, jnp.concatenate([high, high], 0)) + dot(poly_high, low)
         line = jnp.sum(current * current * weight_ref[...], axis=0, keepdims=True)
         fresh_ref[:, cols] = jnp.broadcast_to(line, (8, 256))
-    planes = fresh_ref[:, :ROW] + fresh_ref[:, GG : GG + ROW] + fresh_ref[:, 2 * GG : 2 * GG + ROW]
+    planes = [fresh_ref[:, p * GG : p * GG + ROW] for p in range(PLANES)]
+
     rows_ref[...] = jnp.zeros_like(rows_ref)
-    rows_ref[0:8, :GG] = planes[:, :GG]
+    rows_ref[0:8, :GG] = (planes[0] + planes[1] + planes[2])[:, :GG]
     rows_ref[8:9, :GG] = din_ref[0] + din_ref[1] + din_ref[2]
     cells = dot3(rows_ref[...], gather_ref[...])
     row = lax.broadcasted_iota(jnp.int32, (8, NB), 0)
@@ -235,72 +245,14 @@
     for k in range(BANDS):
         coarse_ref[k] = tile
 
-
-def density_rows(grams, flat, weight, din, gather):
-    return pl.pallas_call(
-        density_kernel,
-        out_shape=(
-            jax.ShapeDtypeStruct((NB, NB), F32),
-            jax.ShapeDtypeStruct((8, SHARE), F32),
-            jax.ShapeDtypeStruct((BANDS, 8, 128), F32),
-        ),
-        scratch_shapes=[pltpu.VMEM((16, ROW), F32)],
-        compiler_params=LIMIT,
-        interpret=INTERPRET,
-        name="density",
-    )(grams, flat, weight, din, gather)
-
-
-def output_kernel(
-    pos_ref, mix_ref, corr_ref, poly_ref, f_ref, fresh_ref, din_ref, sine_ref, inverse_ref, onto_ref,
-    out_ref, own_ref, edge_ref, vec_ref, side_ref, green_ref, left_ref, right_ref,
-):
-    poly_high, poly_low = halves(poly_ref[...])
-    dot = functools.partial(jnp.dot, preferred_element_type=F32)
-    for c in range(SHARE // 128):
-        turned = f_ref[:, 128 * c : 128 * (c + 1)].T
-        high, low = halves(turned)
-        value = dot(high, poly_high) + (dot(high, poly_low) + dot(low, poly_high))
-        count = min(128, PLANES * GG - 128 * c)
-        out_ref[128 * c : 128 * c + count] = value[:count]
-
-    if INTERPRET:
-        dom, band = pos_ref[DOMS], pos_ref[DOMS + 1]
-    else:
-        dom, band = lax.axis_index("dom"), lax.axis_index("band")
-    own = pos_ref[dom]
     lane, z = lane_index((8, ROW))
-    corr = jnp.zeros((8, ROW), F32)
-    for j in range(BUFFER):
-        here = (jnp.abs(z - j) < 0.5) | (jnp.abs(z - (G - BUFFER + j)) < 0.5)
-        corr = jnp.where(here, corr_ref[j].astype(F32), corr)
-    corr = corr * (1.0 / 16.0)
-    fresh_weight = jnp.full((8, ROW), mix_ref[0].astype(F32))
-    input_weight = jnp.full((8, ROW), mix_ref[1].astype(F32))
-    both = fresh_weight + input_weight
-    fresh_weight = fresh_weight / both
-    input_weight = input_weight / both
-    has_left = jnp.where(jnp.full((8, ROW), own) > 0, 1.0, 0.0)
-    has_right = jnp.where(jnp.full((8, ROW), own) < DOMS - 1, 1.0, 0.0)
-    low_z = z < BUFFER - 0.5
-    high_z = z > G - BUFFER - 0.5
+    low_edge = (z < BUFFER - 0.5) & (lane < GG)
+    high_edge = (z > G - BUFFER - 0.5) & (lane < GG)
     middle = (z > BUFFER - 0.5) & (z < G - BUFFER - 0.5)
-    from_left = jnp.where(low_z, corr * has_left, 0.0)
-    from_right = jnp.where(high_z, (1.0 - corr) * has_right, 0.0)
-    keep = 1.0 - from_left - from_right
-    cell = 1.0 / 27.0
-    vec_ref[0:1] = (cell * fresh_weight * jnp.where(high_z, corr * has_right, keep))[0:1]
-    vec_ref[1:2] = jnp.where(high_z, 0.0, cell * input_weight)[0:1]
-    vec_ref[2:3] = (fresh_weight * from_left)[0:1]
-    vec_ref[3:4] = (fresh_weight * from_right)[0:1]
-
-    low_edge = low_z & (lane < GG)
-    high_edge = high_z & (lane < GG)
     edges = []
     for p in range(PLANES):
-        plane = fresh_ref[:, p * GG : p * GG + ROW]
-        own_ref[p] = (fresh_weight * keep * plane)[0:1, :GG] + input_weight[0:1, :GG] * din_ref[p]
-        edges.append((jnp.where(low_edge, plane, 0.0), jnp.where(high_edge, plane, 0.0)))
+        own_ref[p] = vec_ref[4:5, :GG] * planes[p][0:1, :GG] + vec_ref[5:6, :GG] * din_ref[p]
+        edges.append((jnp.where(low_edge, planes[p], 0.0), jnp.where(high_edge, planes[p], 0.0)))
     first = (edges[0][0] + edges[0][1]) + (rolled(edges[1][0], 12) + rolled(edges[1][1], -12))
     last = edges[2][0] + edges[2][1]
     moved = rolled(edges[2][0], 12 - HALF_ROW) + rolled(edges[2][1], -12 - HALF_ROW)
@@ -311,6 +263,69 @@
     for t in range(7):
         source, at = (first, 128 * t) if t < 5 else (rest, 128 * (t - 5))
         edge_ref[t + 1 : t + 2] = source[0:1, at : at + 128]
+    for copy in copies:
+        copy.wait()
+
+
+def density_parts(grams, flat, weight, din, gather, vectors):
+    vmem = pl.BlockSpec(memory_space=pltpu.VMEM)
+    return pl.pallas_call(
+        density_kernel,
+        out_shape=(
+            jax.ShapeDtypeStruct((PLANES * GG, NB), F32),
+            jax.ShapeDtypeStruct((BANDS, 8, 128), F32),
+            jax.ShapeDtypeStruct((PLANES, 1, GG), F32),
+            jax.ShapeDtypeStruct((8, 128), F32),
+        ),
+        in_specs=[vmem] * 6,
+        out_specs=(pl.BlockSpec(memory_space=pltpu.HBM), vmem, vmem, vmem),
+        scratch_shapes=[
+            pltpu.VMEM((SHARE, NB), F32),
+            pltpu.VMEM((8, SHARE), F32),
+            pltpu.VMEM((16, ROW), F32),
+            pltpu.SemaphoreType.DMA((7,)),
+        ],
+        compiler_params=LIMIT,
+        interpret=INTERPRET,
+        name="density",
+    )(grams, flat, weight, din, gather, vectors)
+
+
+def place_kernel(
+    pos_ref, mix_ref, corr_ref, occ_ref, sine_ref, inverse_ref, onto_ref,
+    vec_ref, side_ref, green_ref, weight_ref, left_ref, right_ref,
+):
+    if INTERPRET:
+        dom, band = pos_ref[DOMS], pos_ref[DOMS + 1]
+    else:
+        dom, band = lax.axis_index("dom"), lax.axis_index("band")
+    own = pos_ref[dom]
+    shape = (8, ROW)
+    _, z = lane_index(shape)
+    corr = jnp.zeros(shape, F32)
+    for j in range(BUFFER):
+        here = (jnp.abs(z - j) < 0.5) | (jnp.abs(z - (G - BUFFER + j)) < 0.5)
+        corr = jnp.where(here, corr_ref[j].astype(F32), corr)
+    corr = corr * (1.0 / 16.0)
+    fresh_weight = jnp.full(shape, mix_ref[0].astype(F32))
+    input_weight = jnp.full(shape, mix_ref[1].astype(F32))
+    both = fresh_weight + input_weight
+    fresh_weight = fresh_weight / both
+    input_weight = input_weight / both
+    has_left = jnp.where(jnp.full(shape, own) > 0, 1.0, 0.0)
+    has_right = jnp.where(jnp.full(shape, own) < DOMS - 1, 1.0, 0.0)
+    low_z = z < BUFFER - 0.5
+    high_z = z > G - BUFFER - 0.5
+    from_left = jnp.where(low_z, corr * has_left, 0.0)
+    from_right = jnp.where(high_z, (1.0 - corr) * has_right, 0.0)
+    keep = 1.0 - from_left - from_right
+    cell = 1.0 / 27.0
+    vec_ref[0:1] = (cell * fresh_weight * jnp.where(high_z, corr * has_right, keep))[0:1]
+    vec_ref[1:2] = jnp.where(high_z, 0.0, cell * input_weight)[0:1]
+    vec_ref[2:3] = (fresh_weight * from_left)[0:1]
+    vec_ref[3:4] = (fresh_weight * from_right)[0:1]
+    vec_ref[4:5] = (fresh_weight * keep)[0:1]
+    vec_ref[5:6] = input_weight[0:1]
 
     left, right = jnp.int32(0), jnp.int32(0)
     for d in range(DOMS):
@@ -326,32 +341,33 @@
         for j in range(8):
             at = ky * 64 + j * 8
             left_ref[at : at + 8] = part * mine[j : j + 1]
+    eye = lax.broadcasted_iota(jnp.int32, (NB, NB), 0) == lax.broadcasted_iota(jnp.int32, (NB, NB), 1)
+    weight = jnp.sum(jnp.where(eye, occ_ref[...] * (1.0 / NB), 0.0), axis=1, keepdims=True)
+    weight_ref[...] = jnp.broadcast_to(weight, (NB, 256))
     green_ref[...] = dot3(left_ref[...], right_ref[...], (((1,), (1,)), ((), ())))
 
 
-def output_parts(position, mixing, corr, poly, flat, fresh, din, sine, inverse, onto):
+def placed(position, mixing, corr, occupation, sine, inverse, onto):
     if INTERPRET:
         position = jnp.append(position, jnp.stack([lax.axis_index("dom"), lax.axis_index("band")]))
     smem = pl.BlockSpec(memory_space=pltpu.SMEM)
     vmem = pl.BlockSpec(memory_space=pltpu.VMEM)
     return pl.pallas_call(
-        output_kernel,
+        place_kernel,
         out_shape=(
-            jax.ShapeDtypeStruct((PLANES * GG, NB), F32),
-            jax.ShapeDtypeStruct((PLANES, 1, GG), F32),
-            jax.ShapeDtypeStruct((8, 128), F32),
             jax.ShapeDtypeStruct((8, ROW), F32),
             jax.ShapeDtypeStruct((2,), jnp.int32),
             jax.ShapeDtypeStruct((512, 256), F32),
+            jax.ShapeDtypeStruct((NB, 256), F32),
         ),
-        in_specs=[smem] * 3 + [vmem] * 7,
-        out_specs=(vmem, vmem, vmem, vmem, smem, vmem),
+        in_specs=[smem] * 3 + [vmem] * 4,
+        out_specs=(vmem, smem, vmem, vmem),
         scratch_shapes=[pltpu.VMEM((512, NZC), F32), pltpu.VMEM((256, NZC), F32)],
-        cost_estimate=pl.CostEstimate(flops=500_000_000, bytes_accessed=4_000_000, transcendentals=0),
-        compiler_params=LIMIT,
-        interpret=INTERPRET,
-        name="output",
-    )(position, mixing, corr, poly, flat, fresh, din, sine, inverse, onto)
+        cost_estimate=pl.CostEstimate(flops=1_000_000, bytes_accessed=100_000, transcendentals=0),
+        compiler_params=LIMIT,
+        interpret=INTERPRET,
+        name="place",
+    )(position, mixing, corr, occupation, sine, inverse, onto)
 
 
 def share_kernel(rows_ref, vec_ref, green_ref, over_x_ref, over_y_ref, edge_ref, out_ref, turn_ref, line_ref):
@@ -439,16 +455,15 @@
 
 def body(orbitals, potential, density_in, occupation, position, mixing, correlation_weight):
     sine, inverse, onto, gather, over_x, over_y = tables()
-    filtered, weight = filtered_shares(orbitals[0], potential[0], occupation.reshape(1, NB))
-    shares = exchanged(filtered, "band")
-    flat = shares.reshape(NB, SHARE)
     din = jnp.transpose(density_in, (1, 0, 2))
+    vectors, sides, green, weight = placed(
+        position, mixing, correlation_weight, occupation.reshape(1, NB), sine, inverse, onto
+    )
+    filtered = filtered_shares(orbitals[0], potential[0], vectors)
+    flat = exchanged(filtered, "band").reshape(NB, SHARE)
     grams = exchanged(packed_grams(flat), "band")
-    poly, fresh, coarse = density_rows(grams, flat, weight, din, gather)
+    points, coarse, own, edges = density_parts(grams, flat, weight, din, gather, vectors)
     rows = exchanged(coarse, "band")
-    points, own, edges, vectors, sides, green = output_parts(
-        position, mixing, correlation_weight, poly, flat, fresh, din, sine, inverse, onto
-    )
     msg = exchanged(hartree_shares(rows, vectors, green, over_x, over_y, edges), "dom")
     dens, hart = final_parts(sides, msg, own, vectors)
     orbitals_out = jnp.transpose(points.reshape(PLANES, GG, NB), (2, 0, 1)).reshape(1, NB, PLANES, GG)

time: 66.8 us -> 67.5 us (1.010)
  blocking collectives: 50 us -> 57.8 us
  starting transfers between devices: 3.94 us -> 0 us
  waiting for transfers between devices: 1.77 us -> 0 us
  local copies, waits for them, and re-layouts: 1.69 us -> 0.87 us
    all_to_all x3 -> x4, blocking collectives: 50 us -> 57.8 us  [exchanged(): return lax.all_to_all(x, axis, split_axis=0, concat_axis=0, tiled=True)]
    all_to_all x1 -> x0, starting transfers between devices: 3.94 us -> none  [exchanged(): return lax.all_to_all(x, axis, split_axis=0, concat_axis=0, tiled=True)]
    all_to_all x1 -> x0, waiting for transfers between devices: 1.77 us -> none  [exchanged(): return lax.all_to_all(x, axis, split_axis=0, concat_axis=0, tiled=True)]
    unnamed x26, local copies, waits for them, and re-layouts: 1.69 us -> 0.87 us
  transfers between devices with their start and end apart: 1 -> 0, of which waited for: 1 -> 0; matrix products, arithmetic and copies ran while one was open for 0% -> 0% of each run, Pallas kernels for 3% -> 0%
where the time goes in v4:
time: 67.5 us; the launch traced here: 67.2 us
  blocking collectives  57.8 us (86%)
  Pallas kernels  7.82 us (12%)
  local copies, waits for them, and re-layouts  0.87 us (1%)
  between operations  0.76 us (1%)
    all_to_all x4, blocking collectives, exchanged(): return lax.all_to_all(x, axis, split_axis=0, concat_axis=0, tiled=True)  57.8 us
    pallas_call x1, Pallas kernels, density_parts(): pl.pallas_call(density_kernel, out_shape=(jax.ShapeDtypeStruct((PLANES *...  2.22 us
    pallas_call x1, Pallas kernels, filtered_shares(): pl.pallas_call(filter_kernel, out_shape=jax.ShapeDtypeStruct((BANDS, LOCA...  1.56 us
    pallas_call x1, Pallas kernels, placed(): pl.pallas_call(place_kernel, out_shape=(jax.ShapeDtypeStruct((8, ROW), F3...  1.44 us

profile of v4, /device:TPU:1, one launch (start us, length us, event | category | flops | bytes accessed | tf_op | source)
XLA Modules:
  0.0 67.2 jit_solution(11166088194855467938)
XLA Ops:
  0.6 0.0 copy-start.2
  0.6 0.0 copy-start.5
  0.7 0.0 copy-start.6
  0.7 0.0 copy-start.12
  0.7 0.0 copy-start
  0.7 0.2 matrix.1.mat_ref
  0.9 0.0 copy-start.9
  0.9 0.0 copy-start.10
  0.9 0.0 copy-start.11
  0.9 0.7 copy-done.2
  1.6 0.0 copy-done.5
  1.6 0.0 copy-done.6
  1.6 0.0 copy-done.12
  1.6 0.1 copy-done.9
  1.7 0.0 copy-done.10
  1.7 0.0 copy-done.11
  1.7 0.0 copy-start.7
  1.7 1.4 %place.1 = (f32[8,640]{1,0:T(8,128)S(1)}, s32[2]{0:T(128)S(1)}, f32[512,256]{1,0:T(8,128)S(1)}, f32[128,256]{1,0:T(8,128)S(1)}) custom-call(s32[32]{0:T(128)S(1)} %copy-done.9, s32[2]{0:T(128)S(1)} %copy-done.10, s32[6]{0:T(128)S(1)} %copy-done.11, f32[1,128]{1,0:T(1,128)S(1)} %bitcast.21, f32[32,8,192]{2,1,0:T(8,128)S(1)} %copy-done.2, ...), custom_call_target="tpu_custom_call" | custom-call | flops 1000000 | bytes 100000 | tf_op jit(solution)/shard_map/place/pallas_call | solution.py:355
  3.2 0.0 copy-done
  3.2 0.0 copy-done.7
  3.2 1.6 %filter.1 = f32[8,16,1792]{2,1,0:T(8,128)S(1)} custom-call(f32[16,24,576]{2,1,0:T(8,128)S(1)} %bitcast.18, f32[24,576]{1,0:T(8,128)S(1)} %bitcast.19, bf16[640,640]{1,0:T(8,128)(2,1)S(1)} %matrix.1.mat_ref, f32[8,640]{1,0:T(8,128)S(1)} %get-tuple-element.13.vec_ref), custom_call_target="tpu_custom_call" | custom-call | tf_op jit(solution)/shard_map/filter/pallas_call | solution.py:146
  4.8 19.3 %all_to_all.20 = f32[8,16,1792]{2,1,0:T(8,128)S(1)} all-to-all(f32[8,16,1792]{2,1,0:T(8,128)S(1)} %filter.1), channel_id=1, replica_groups=mesh['dom'=32,'band'=8] {'band'}, dimensions={0} | all-to-all | bytes 1835008 | tf_op jit(solution)/shard_map/all_to_all | solution.py:453
  24.1 0.0 copy-start.1
  24.1 0.0 copy-start.8
  24.1 0.6 gram.1
  24.7 10.5 %all_to_all.21.g_ref = f32[8,72,128]{2,1,0:T(8,128)S(1)} all-to-all(f32[8,72,128]{2,1,0:T(8,128)S(1)} %gram.1), channel_id=1, replica_groups=mesh['dom'=32,'band'=8] {'band'}, dimensions={0} | all-to-all | bytes 589824 | tf_op jit(solution)/shard_map/all_to_all | solution.py:453
  35.2 0.0 copy-done.1
  35.2 0.0 copy-done.8
  35.2 0.0 copy-start.4
  35.2 2.2 %density.1 = (f32[1728,128]{1,0:T(8,128)}, f32[8,8,128]{2,1,0:T(8,128)S(1)}, f32[3,1,576]{2,1,0:T(1,128)S(1)}, f32[8,128]{1,0:T(8,128)S(1)}) custom-call(f32[8,72,128]{2,1,0:T(8,128)S(1)} %all_to_all.21.g_ref, f32[128,1792]{1,0:T(8,128)S(1)} %bitcast.17, f32[128,256]{1,0:T(8,128)S(1)} %get-tuple-element.14.weight_ref, f32[3,1,576]{2,1,0:T(1,128)S(1)} %bitcast.20, ...), custom_call_target="tpu_custom_call" | custom-call | tf_op jit(solution)/shard_map/density/pallas_call | solution.py:272
  37.5 0.0 copy-start.3
  37.5 7.8 %all_to_all.22.rows_ref = f32[8,8,128]{2,1,0:T(8,128)S(1)} all-to-all(f32[8,8,128]{2,1,0:T(8,128)S(1)} %get-tuple-element.17), channel_id=1, replica_groups=mesh['dom'=32,'band'=8] {'band'}, dimensions={0} | all-to-all | bytes 65536 | tf_op jit(solution)/shard_map/all_to_all | solution.py:453
  45.3 0.0 copy-done.4
  45.3 0.0 copy-done.3
  45.3 0.5 share.1
  45.8 20.1 %all_to_all.23.msg_ref = f32[32,8,128]{2,1,0:T(8,128)S(1)} all-to-all(f32[32,8,128]{2,1,0:T(8,128)S(1)} %share.1), channel_id=1, replica_groups=mesh['dom'=32,'band'=8] {'dom'}, dimensions={0} | all-to-all | bytes 262144 | tf_op jit(solution)/shard_map/all_to_all | solution.py:453
  65.9 1.3 %final.1 = (f32[3,1,576]{2,1,0:T(1,128)}, f32[6,1,8]{2,1,0:T(1,128)}) custom-call(s32[2]{0:T(128)S(1)} %get-tuple-element.16.side_ref, f32[32,8,128]{2,1,0:T(8,128)S(1)} %all_to_all.23.msg_ref, f32[3,1,576]{2,1,0:T(1,128)S(1)} %get-tuple-element.20.own_ref, f32[8,640]{1,0:T(8,128)S(1)} %get-tuple-element.13.vec_ref), custom_call_target="tpu_custom_call" | custom-call | tf_op jit(solution)/shard_map/final/pallas_call | solution.py:438
Async XLA Ops:
  0.6 1.0 %copy-start.2 = (f32[32,8,192]{2,1,0:T(8,128)S(1)}, f32[32,8,192]{2,1,0:T(8,128)}, u32[]{:S(2)}) copy-start(f32[32,8,192]{2,1,0:T(8,128)} %constant.12.clone.sine_ref) | copy-start | bytes 589828
  0.6 0.9 %copy-start.5 = (f32[8,8,192]{2,1,0:T(8,128)S(1)}, f32[8,8,192]{2,1,0:T(8,128)}, u32[]{:S(2)}) copy-start(f32[8,8,192]{2,1,0:T(8,128)} %constant.14.clone.onto_ref) | copy-start | bytes 147460
  0.7 0.9 %copy-start.6 = (f32[64,192]{1,0:T(8,128)S(1)}, f32[64,192]{1,0:T(8,128)}, u32[]{:S(2)}) copy-start(f32[64,192]{1,0:T(8,128)} %constant.13.clone.inverse_ref) | copy-start | bytes 147460
  0.7 0.9 %copy-start.12 = (f32[128]{0:T(128)S(1)}, f32[128]{0:T(128)}, u32[]{:S(2)}) copy-start(f32[128]{0:T(128)} %param.16) | copy-start | bytes 1540
  0.7 2.5 %copy-start = (f32[1,16,24,576]{3,2,1,0:T(8,128)S(1)}, f32[1,16,24,576]{3,2,1,0:T(8,128)}, u32[]{:S(2)}) copy-start(f32[1,16,24,576]{3,2,1,0:T(8,128)} %param.13) | copy-start | bytes 2654212
  0.9 0.8 %copy-start.9 = (s32[32]{0:T(128)S(1)}, s32[32]{0:T(128)}, u32[]{:S(2)}) copy-start(s32[32]{0:T(128)} %pos_ref.1) | copy-start | bytes 388
  0.9 0.8 %copy-start.10 = (s32[2]{0:T(128)S(1)}, s32[2]{0:T(128)}, u32[]{:S(2)}) copy-start(s32[2]{0:T(128)} %mix_ref.1) | copy-start | bytes 28
  0.9 0.8 %copy-start.11 = (s32[6]{0:T(128)S(1)}, s32[6]{0:T(128)}, u32[]{:S(2)}) copy-start(s32[6]{0:T(128)} %corr_ref.1) | copy-start | bytes 76
  1.7 1.5 %copy-start.7 = (f32[1,24,576]{2,1,0:T(8,128)S(1)}, f32[1,24,576]{2,1,0:T(8,128)}, u32[]{:S(2)}) copy-start(f32[1,24,576]{2,1,0:T(8,128)} %param.14) | copy-start | bytes 165892
  24.1 11.2 %copy-start.1 = (f32[640,256]{1,0:T(8,128)S(1)}, f32[640,256]{1,0:T(8,128)}, u32[]{:S(2)}) copy-start(f32[640,256]{1,0:T(8,128)} %constant.15.clone.gather_ref) | copy-start | bytes 1966084
  24.1 11.2 %copy-start.8 = (f32[1,3,576]{2,0,1:T(1,128)S(1)}, f32[1,3,576]{2,0,1:T(1,128)}, u32[]{:S(2)}) copy-start(f32[1,3,576]{2,0,1:T(1,128)} %param.15) | copy-start | bytes 20740
  35.2 10.0 %copy-start.4 = (f32[8,8,256]{2,1,0:T(8,128)S(1)}, f32[8,8,256]{2,1,0:T(8,128)}, u32[]{:S(2)}) copy-start(f32[8,8,256]{2,1,0:T(8,128)} %constant.16.clone.over_x_ref) | copy-start | bytes 196612
  37.5 7.8 %copy-start.3 = (f32[8,8,256]{2,1,0:T(8,128)S(1)}, f32[8,8,256]{2,1,0:T(8,128)}, u32[]{:S(2)}) copy-start(f32[8,8,256]{2,1,0:T(8,128)} %constant.17.clone.over_y_ref) | copy-start | bytes 196612

commit v5 on v3

--- a/solution.py
+++ b/solution.py
@@ -186,6 +186,7 @@
     return pl.pallas_call(
         gram_kernel,
         out_shape=jax.ShapeDtypeStruct((BANDS, PACKED, NB), F32),
+        cost_estimate=pl.CostEstimate(flops=20_000_000_000, bytes_accessed=4_000_000, transcendentals=0),
         compiler_params=LIMIT,
         interpret=INTERPRET,
         name="gram",
@@ -245,6 +246,7 @@
             jax.ShapeDtypeStruct((BANDS, 8, 128), F32),
         ),
         scratch_shapes=[pltpu.VMEM((16, ROW), F32)],
+        cost_estimate=pl.CostEstimate(flops=20_000_000_000, bytes_accessed=4_000_000, transcendentals=0),
         compiler_params=LIMIT,
         interpret=INTERPRET,
         name="density",
@@ -253,16 +255,20 @@
 
 def output_kernel(
     pos_ref, mix_ref, corr_ref, poly_ref, f_ref, fresh_ref, din_ref, sine_ref, inverse_ref, onto_ref,
-    out_ref, own_ref, edge_ref, vec_ref, side_ref, green_ref, left_ref, right_ref,
+    out_ref, own_ref, edge_ref, vec_ref, side_ref, green_ref, left_ref, right_ref, point_ref, sems,
 ):
     poly_high, poly_low = halves(poly_ref[...])
     dot = functools.partial(jnp.dot, preferred_element_type=F32)
-    for c in range(SHARE // 128):
-        turned = f_ref[:, 128 * c : 128 * (c + 1)].T
-        high, low = halves(turned)
-        value = dot(high, poly_high) + (dot(high, poly_low) + dot(low, poly_high))
-        count = min(128, PLANES * GG - 128 * c)
-        out_ref[128 * c : 128 * c + count] = value[:count]
+    copies = []
+    for c in range(7):
+        start, count = 256 * c, min(256, PLANES * GG - 256 * c)
+        for at in range(start, start + count, 128):
+            high, low = halves(f_ref[:, at : at + 128].T)
+            value = dot(high, poly_high) + (dot(high, poly_low) + dot(low, poly_high))
+            point_ref[at : at + 128] = value
+        part = pl.ds(start, count)
+        copies.append(pltpu.make_async_copy(point_ref.at[part], out_ref.at[part], sems.at[c]))
+        copies[-1].start()
 
     if INTERPRET:
         dom, band = pos_ref[DOMS], pos_ref[DOMS + 1]
@@ -312,13 +318,11 @@
         source, at = (first, 128 * t) if t < 5 else (rest, 128 * (t - 5))
         edge_ref[t + 1 : t + 2] = source[0:1, at : at + 128]
 
-    left, right = jnp.int32(0), jnp.int32(0)
     for d in range(DOMS):
-        left = jnp.where(pos_ref[d] == own - 1, d, left)
-        right = jnp.where(pos_ref[d] == own + 1, d, right)
+        place = jnp.full((1, 128), pos_ref[d])
+        side_ref[0, d : d + 1] = jnp.where(place == own - 1, 1.0, 0.0)
+        side_ref[1, d : d + 1] = jnp.where(place == own + 1, 1.0, 0.0)
         right_ref[8 * d : 8 * d + 8] = sine_ref[pos_ref[d]]
-    side_ref[0] = left
-    side_ref[1] = right
     mine = sine_ref[own]
     onto = onto_ref[band]
     for ky in range(CG):
@@ -327,6 +331,8 @@
             at = ky * 64 + j * 8
             left_ref[at : at + 8] = part * mine[j : j + 1]
     green_ref[...] = dot3(left_ref[...], right_ref[...], (((1,), (1,)), ((), ())))
+    for copy in copies:
+        copy.wait()
 
 
 def output_parts(position, mixing, corr, poly, flat, fresh, din, sine, inverse, onto):
@@ -341,12 +347,17 @@
             jax.ShapeDtypeStruct((PLANES, 1, GG), F32),
             jax.ShapeDtypeStruct((8, 128), F32),
             jax.ShapeDtypeStruct((8, ROW), F32),
-            jax.ShapeDtypeStruct((2,), jnp.int32),
+            jax.ShapeDtypeStruct((2, DOMS, 128), F32),
             jax.ShapeDtypeStruct((512, 256), F32),
         ),
         in_specs=[smem] * 3 + [vmem] * 7,
-        out_specs=(vmem, vmem, vmem, vmem, smem, vmem),
-        scratch_shapes=[pltpu.VMEM((512, NZC), F32), pltpu.VMEM((256, NZC), F32)],
+        out_specs=(pl.BlockSpec(memory_space=pltpu.HBM), vmem, vmem, vmem, vmem, vmem),
+        scratch_shapes=[
+            pltpu.VMEM((512, NZC), F32),
+            pltpu.VMEM((256, NZC), F32),
+            pltpu.VMEM((SHARE, NB), F32),
+            pltpu.SemaphoreType.DMA((7,)),
+        ],
         cost_estimate=pl.CostEstimate(flops=500_000_000, bytes_accessed=4_000_000, transcendentals=0),
         compiler_params=LIMIT,
         interpret=INTERPRET,
@@ -398,14 +409,20 @@
         hart_ref[j] = total[0:1, 8 * j : 8 * j + 8]
     lane = lax.broadcasted_iota(jnp.int32, (8, ROW), 1)
 
+    def picked(side):
+        tile = jnp.zeros((8, 128), F32)
+        for d in range(DOMS):
+            tile = tile + side_ref[side, d : d + 1] * msg_ref[d]
+        return tile
+
     def rows(tile):
         spread = [jnp.broadcast_to(tile[t + 1 : t + 2], (8, 128)) for t in range(7)]
         front = jnp.concatenate(spread[:5], 1)
         back = jnp.concatenate(spread[4:] + spread[5:], 1)
         return front, rolled(back, -64)
 
-    left0, left2 = rows(msg_ref[side_ref[0]])
-    right0, right2 = rows(msg_ref[side_ref[1]])
+    left0, left2 = rows(picked(0))
+    right0, right2 = rows(picked(1))
     far = G - BUFFER
     left_last = jnp.where(lane < HALF_ROW, rolled(left2, -far), rolled(left2, HALF_ROW + 12 - far))
     right_last = jnp.where(lane < HALF_ROW, rolled(right2, far), rolled(right2, HALF_ROW - 12 + far))
@@ -417,16 +434,12 @@
 
 
 def final_parts(sides, msg, own, vectors):
-    smem = pl.BlockSpec(memory_space=pltpu.SMEM)
-    vmem = pl.BlockSpec(memory_space=pltpu.VMEM)
     return pl.pallas_call(
         final_kernel,
         out_shape=(
             jax.ShapeDtypeStruct((PLANES, 1, GG), F32),
             jax.ShapeDtypeStruct((CZ, 1, CG), F32),
         ),
-        in_specs=[smem, vmem, vmem, vmem],
-        out_specs=(vmem, vmem),
         compiler_params=LIMIT,
         interpret=INTERPRET,
         name="final",

time: 66.8 us -> 66.3 us (level)
  Pallas kernels: 8.39 us -> 7.65 us
where the time goes in v5:
time: 66.3 us; the launch traced here: 66 us
  blocking collectives  50 us (75%)
  Pallas kernels  7.65 us (12%)
  starting transfers between devices  3.94 us (6%)
  waiting for transfers between devices  2.01 us (3%)
  local copies, waits for them, and re-layouts  1.69 us (3%)
  between operations  0.74 us (1%)
    all_to_all x3, blocking collectives, exchanged(): return lax.all_to_all(x, axis, split_axis=0, concat_axis=0, tiled=True)  50 us
    all_to_all x1, starting transfers between devices, exchanged(): return lax.all_to_all(x, axis, split_axis=0, concat_axis=0, tiled=True)  3.94 us
    pallas_call x1, Pallas kernels, output_parts(): pl.pallas_call(output_kernel, out_shape=(jax.ShapeDtypeStruct((PLANES * G...  2.03 us
    pallas_call x1, Pallas kernels, density_rows(): pl.pallas_call(density_kernel, out_shape=(jax.ShapeDtypeStruct((NB, NB),...  2.02 us
    all_to_all x1, waiting for transfers between devices, exchanged(): return lax.all_to_all(x, axis, split_axis=0, concat_axis=0, tiled=True)  2.01 us
    unnamed x26, local copies, waits for them, and re-layouts  1.69 us
    pallas_call x1, Pallas kernels, filtered_shares(): pl.pallas_call(filter_kernel, out_shape=(jax.ShapeDtypeStruct((BANDS, LOC...  1.5 us
  transfers between devices with their start and end apart: 1, of which 1 were waited for; matrix products, arithmetic and copies ran while one was open for 0% of the time, Pallas kernels for 3%

profile of v5, /device:TPU:1, one launch (start us, length us, event | category | flops | bytes accessed | tf_op | source)
XLA Modules:
  0.0 66.0 jit_solution(10896124177772856466)
XLA Ops:
  0.6 0.0 copy-start.3
  0.6 0.0 copy-start
  0.6 0.2 matrix.1.mat_ref
  0.9 0.0 copy-start.4
  0.9 0.6 copy-done.3
  1.5 0.4 copy-done
  1.9 0.0 copy-done.4
  1.9 1.5 %filter.1 = (f32[8,16,1792]{2,1,0:T(8,128)S(1)}, f32[128,256]{1,0:T(8,128)S(1)}) custom-call(f32[16,24,576]{2,1,0:T(8,128)S(1)} %bitcast.16, f32[24,576]{1,0:T(8,128)S(1)} %bitcast.20, bf16[640,640]{1,0:T(8,128)(2,1)S(1)} %matrix.1.mat_ref, f32[1,128]{1,0:T(1,128)S(1)} %bitcast.21), custom_call_target="tpu_custom_call" | custom-call | tf_op jit(solution)/shard_map/filter/pallas_call | solution.py:149
  3.4 19.3 %all_to_all.20 = f32[8,16,1792]{2,1,0:T(8,128)S(1)} all-to-all(f32[8,16,1792]{2,1,0:T(8,128)S(1)} %get-tuple-element.16), channel_id=1, replica_groups=mesh['dom'=32,'band'=8] {'band'}, dimensions={0} | all-to-all | bytes 1835008 | tf_op jit(solution)/shard_map/all_to_all | solution.py:450
  22.7 0.0 copy-start.9
  22.7 0.6 gram.1
  23.3 0.0 copy-start.5
  23.3 10.5 %all_to_all.21.g_ref = f32[8,72,128]{2,1,0:T(8,128)S(1)} all-to-all(f32[8,72,128]{2,1,0:T(8,128)S(1)} %gram.1), channel_id=1, replica_groups=mesh['dom'=32,'band'=8] {'band'}, dimensions={0} | all-to-all | bytes 589824 | tf_op jit(solution)/shard_map/all_to_all | solution.py:450
  33.8 0.0 copy-done.9
  33.8 0.0 copy-done.5
  33.8 0.0 copy-start.10
  33.8 0.0 copy-start.12
  33.9 2.0 %density.1 = (f32[128,128]{1,0:T(8,128)S(1)}, f32[8,1792]{1,0:T(8,128)S(1)}, f32[8,8,128]{2,1,0:T(8,128)}) custom-call(f32[8,72,128]{2,1,0:T(8,128)S(1)} %all_to_all.21.g_ref, f32[128,1792]{1,0:T(8,128)S(1)} %bitcast.18, f32[128,256]{1,0:T(8,128)S(1)} %get-tuple-element.17.weight_ref, f32[3,1,576]{2,1,0:T(1,128)S(1)} %bitcast.22, f32[640,256]{1,0:T(8,128)S(1)} %copy-done.9), custom_call_target="tpu_custom_call" | custom-call | flops 20000000000 | bytes 4000000 | tf_op jit(solution)/shard_map/density/pallas_call | solution.py:241
  35.9 0.0 copy-start.11
  35.9 3.9 %all-to-all-start.2 = ((f32[8,8,128]{2,1,0:T(8,128)}), f32[8,8,128]{2,1,0:T(8,128)S(1)}, u32[]{:S(2)}, u32[]{:S(2)}) async-start(f32[8,8,128]{2,1,0:T(8,128)} %get-tuple-element.22), calls=%async_computation.2 | async-start | bytes 65536 | tf_op jit(solution)/shard_map/all_to_all | solution.py:450
  39.8 0.0 copy-start.6
  39.8 0.0 copy-start.7
  39.8 0.0 copy-start.8
  39.8 0.0 copy-done.10
  39.8 0.0 copy-done.12
  39.8 0.0 copy-done.11
  39.9 0.6 copy-done.6
  40.5 0.0 copy-done.7
  40.5 0.0 copy-done.8
  40.5 0.0 copy-start.1
  40.5 0.0 copy-start.2
  40.5 2.0 %output.1 = (f32[1728,128]{1,0:T(8,128)}, f32[3,1,576]{2,1,0:T(1,128)S(1)}, f32[8,128]{1,0:T(8,128)S(1)}, f32[8,640]{1,0:T(8,128)S(1)}, f32[2,32,128]{2,1,0:T(8,128)S(1)}, /*index=5*/f32[512,256]{1,0:T(8,128)S(1)}) custom-call(s32[32]{0:T(128)S(1)} %copy-done.6, s32[2]{0:T(128)S(1)} %copy-done.7, s32[6]{0:T(128)S(1)} %copy-done.8, ...), custom_call_target="tpu_custom_call" | custom-call | flops 500000000 | bytes 4000000 | tf_op jit(solution)/shard_map/output/pallas_call | solution.py:343
  42.5 2.0 %all-to-all-done.2.rows_ref = f32[8,8,128]{2,1,0:T(8,128)S(1)} async-done(((f32[8,8,128]{2,1,0:T(8,128)}), f32[8,8,128]{2,1,0:T(8,128)S(1)}, u32[]{:S(2)}, u32[]{:S(2)}) %all-to-all-start.2) | async-done | bytes 32800 | tf_op jit(solution)/shard_map/all_to_all | solution.py:450
  44.5 0.0 copy-done.1
  44.6 0.0 copy-done.2
  44.6 0.5 share.1
  45.0 20.2 %all_to_all.22.msg_ref = f32[32,8,128]{2,1,0:T(8,128)S(1)} all-to-all(f32[32,8,128]{2,1,0:T(8,128)S(1)} %share.1), channel_id=1, replica_groups=mesh['dom'=32,'band'=8] {'dom'}, dimensions={0} | all-to-all | bytes 262144 | tf_op jit(solution)/shard_map/all_to_all | solution.py:450
  65.2 0.8 %final.1 = (f32[3,1,576]{2,1,0:T(1,128)}, f32[6,1,8]{2,1,0:T(1,128)}) custom-call(f32[2,32,128]{2,1,0:T(8,128)S(1)} %get-tuple-element.21.side_ref, f32[32,8,128]{2,1,0:T(8,128)S(1)} %all_to_all.22.msg_ref, f32[3,1,576]{2,1,0:T(1,128)S(1)} %get-tuple-element.26.own_ref, f32[8,640]{1,0:T(8,128)S(1)} %get-tuple-element.23.vec_ref), custom_call_target="tpu_custom_call" | custom-call | tf_op jit(solution)/shard_map/final/pallas_call | solution.py:437
Async XLA Ops:
  0.6 0.8 %copy-start.3 = (f32[1,24,576]{2,1,0:T(8,128)S(1)}, f32[1,24,576]{2,1,0:T(8,128)}, u32[]{:S(2)}) copy-start(f32[1,24,576]{2,1,0:T(8,128)} %param.14) | copy-start | bytes 165892
  0.6 1.2 %copy-start = (f32[1,16,24,576]{3,2,1,0:T(8,128)S(1)}, f32[1,16,24,576]{3,2,1,0:T(8,128)}, u32[]{:S(2)}) copy-start(f32[1,16,24,576]{3,2,1,0:T(8,128)} %param.13) | copy-start | bytes 2654212
  0.9 1.0 %copy-start.4 = (f32[128]{0:T(128)S(1)}, f32[128]{0:T(128)}, u32[]{:S(2)}) copy-start(f32[128]{0:T(128)} %param.16) | copy-start | bytes 1540
  22.7 11.2 %copy-start.9 = (f32[640,256]{1,0:T(8,128)S(1)}, f32[640,256]{1,0:T(8,128)}, u32[]{:S(2)}) copy-start(f32[640,256]{1,0:T(8,128)} %constant.12.clone.gather_ref) | copy-start | bytes 1966084
  23.3 10.5 %copy-start.5 = (f32[1,3,576]{2,0,1:T(1,128)S(1)}, f32[1,3,576]{2,0,1:T(1,128)}, u32[]{:S(2)}) copy-start(f32[1,3,576]{2,0,1:T(1,128)} %param.15) | copy-start | bytes 20740
  33.8 6.0 %copy-start.10 = (f32[32,8,192]{2,1,0:T(8,128)S(1)}, f32[32,8,192]{2,1,0:T(8,128)}, u32[]{:S(2)}) copy-start(f32[32,8,192]{2,1,0:T(8,128)} %constant.13.clone.sine_ref) | copy-start | bytes 589828
  33.8 6.0 %copy-start.12 = (f32[64,192]{1,0:T(8,128)S(1)}, f32[64,192]{1,0:T(8,128)}, u32[]{:S(2)}) copy-start(f32[64,192]{1,0:T(8,128)} %constant.14.clone.inverse_ref) | copy-start | bytes 147460
  35.9 4.0 %copy-start.11 = (f32[8,8,192]{2,1,0:T(8,128)S(1)}, f32[8,8,192]{2,1,0:T(8,128)}, u32[]{:S(2)}) copy-start(f32[8,8,192]{2,1,0:T(8,128)} %constant.15.clone.onto_ref) | copy-start | bytes 147460
  35.9 8.7 %all-to-all-start.2 = ((f32[8,8,128]{2,1,0:T(8,128)}), f32[8,8,128]{2,1,0:T(8,128)S(1)}, u32[]{:S(2)}, u32[]{:S(2)}) async-start(f32[8,8,128]{2,1,0:T(8,128)} %get-tuple-element.22), calls=%async_computation.2 | async-start | bytes 65536 | tf_op jit(solution)/shard_map/all_to_all | solution.py:450
  39.8 0.7 copy-start.6
  39.8 0.7 %copy-start.7 = (s32[2]{0:T(128)S(1)}, s32[2]{0:T(128)}, u32[]{:S(2)}) copy-start(s32[2]{0:T(128)} %mix_ref.1) | copy-start | bytes 28
  39.8 0.7 %copy-start.8 = (s32[6]{0:T(128)S(1)}, s32[6]{0:T(128)}, u32[]{:S(2)}) copy-start(s32[6]{0:T(128)} %corr_ref.1) | copy-start | bytes 76
  40.5 4.1 %copy-start.1 = (f32[8,8,256]{2,1,0:T(8,128)S(1)}, f32[8,8,256]{2,1,0:T(8,128)}, u32[]{:S(2)}) copy-start(f32[8,8,256]{2,1,0:T(8,128)} %constant.17.clone.over_y_ref) | copy-start | bytes 196612
  40.5 4.1 %copy-start.2 = (f32[8,8,256]{2,1,0:T(8,128)S(1)}, f32[8,8,256]{2,1,0:T(8,128)}, u32[]{:S(2)}) copy-start(f32[8,8,256]{2,1,0:T(8,128)} %constant.16.clone.over_x_ref) | copy-start | bytes 196612

commit v6 on v4

--- a/solution.py
+++ b/solution.py
@@ -95,7 +95,17 @@
         mat_ref[top:end, 128 * t : 128 * (t + 1)] = jnp.where(hit, 1.0, 0.0).astype(jnp.bfloat16)
 
 
-def filter_kernel(orb_ref, pot_ref, mat_ref, vec_ref, out_ref, zero_ref, first_ref, side_ref, diag_ref):
+def filter_kernel(
+    orb_ref, pot_ref, mat_ref, occ_ref, pos_ref, mix_ref, corr_ref,
+    out_ref, weight_ref, int_ref, zero_ref, first_ref, side_ref, diag_ref,
+):
+    eye = lax.broadcasted_iota(jnp.int32, (NB, NB), 0) == lax.broadcasted_iota(jnp.int32, (NB, NB), 1)
+    weight = jnp.sum(jnp.where(eye, occ_ref[...] * (1.0 / NB), 0.0), axis=1, keepdims=True)
+    weight_ref[...] = jnp.broadcast_to(weight, (NB, 256))
+    int_ref[...] = jnp.zeros((8, 128), jnp.int32)
+    int_ref[0:1, :DOMS] = pos_ref[...]
+    int_ref[1:2, :2] = mix_ref[...]
+    int_ref[2:3, :BUFFER] = corr_ref[...]
     diag_ref[:, GG - 64 :] = jnp.zeros((G, 128), F32)
     zero_ref[:, :, GG - 64 :] = jnp.zeros((G, LOCAL, 128), F32)
     diag_ref[:, :GG] = (pot_ref[...] + (3.0 - CENTER)) * 2.0
@@ -134,7 +144,7 @@
             out_ref[x // PLANES, :, PLANES * GG :] = jnp.zeros((LOCAL, SHARE - PLANES * GG), F32)
 
 
-def filtered_shares(orbitals, potential, vectors):
+def filtered_shares(orbitals, potential, occupation, *integers):
     matrix = pl.pallas_call(
         neighbour_matrix,
         out_shape=jax.ShapeDtypeStruct((ROW, ROW), jnp.bfloat16),
@@ -145,7 +155,11 @@
     )()
     return pl.pallas_call(
         filter_kernel,
-        out_shape=jax.ShapeDtypeStruct((BANDS, LOCAL, SHARE), F32),
+        out_shape=(
+            jax.ShapeDtypeStruct((BANDS, LOCAL, SHARE), F32),
+            jax.ShapeDtypeStruct((NB, 256), F32),
+            jax.ShapeDtypeStruct((8, 128), jnp.int32),
+        ),
         scratch_shapes=[
             pltpu.VMEM((G, LOCAL, ROW), F32),
             pltpu.VMEM((G, LOCAL, ROW), F32),
@@ -155,7 +169,7 @@
         compiler_params=LIMIT,
         interpret=INTERPRET,
         name="filter",
-    )(orbitals, potential, matrix, vectors)
+    )(orbitals, potential, matrix, occupation, *integers)
 
 
 def gram_kernel(f_ref, out_ref):
@@ -180,17 +194,65 @@
     return pl.pallas_call(
         gram_kernel,
         out_shape=jax.ShapeDtypeStruct((BANDS, PACKED, NB), F32),
+        cost_estimate=pl.CostEstimate(flops=20_000_000_000, bytes_accessed=4_000_000, transcendentals=0),
         compiler_params=LIMIT,
         interpret=INTERPRET,
         name="gram",
     )(flat)
 
 
+def lane_weights(int_ref, own, vec_ref):
+    shape = (8, ROW)
+    _, z = lane_index(shape)
+    corr = jnp.zeros(shape, F32)
+    for j in range(BUFFER):
+        here = (jnp.abs(z - j) < 0.5) | (jnp.abs(z - (G - BUFFER + j)) < 0.5)
+        corr = jnp.where(here, int_ref[2, j].astype(F32), corr)
+    corr = corr * (1.0 / 16.0)
+    fresh_weight = jnp.full(shape, int_ref[1, 0].astype(F32))
+    input_weight = jnp.full(shape, int_ref[1, 1].astype(F32))
+    both = fresh_weight + input_weight
+    fresh_weight = fresh_weight / both
+    input_weight = input_weight / both
+    has_left = jnp.where(jnp.full(shape, own) > 0, 1.0, 0.0)
+    has_right = jnp.where(jnp.full(shape, own) < DOMS - 1, 1.0, 0.0)
+    low_z = z < BUFFER - 0.5
+    high_z = z > G - BUFFER - 0.5
+    from_left = jnp.where(low_z, corr * has_left, 0.0)
+    from_right = jnp.where(high_z, (1.0 - corr) * has_right, 0.0)
+    keep = 1.0 - from_left - from_right
+    cell = 1.0 / 27.0
+    vec_ref[0:1] = (cell * fresh_weight * jnp.where(high_z, corr * has_right, keep))[0:1]
+    vec_ref[1:2] = jnp.where(high_z, 0.0, cell * input_weight)[0:1]
+    vec_ref[2:3] = (fresh_weight * from_left)[0:1]
+    vec_ref[3:4] = (fresh_weight * from_right)[0:1]
+    vec_ref[4:5] = (fresh_weight * keep)[0:1]
+    vec_ref[5:6] = input_weight[0:1]
+
+
+def poisson_operator(int_ref, own, band, sine_ref, inverse_ref, onto_ref, side_ref, green_ref, left_ref, right_ref):
+    for d in range(DOMS):
+        place = jnp.full((1, 128), int_ref[0, d])
+        side_ref[0, d : d + 1] = jnp.where(place == own - 1, 1.0, 0.0)
+        side_ref[1, d : d + 1] = jnp.where(place == own + 1, 1.0, 0.0)
+        right_ref[8 * d : 8 * d + 8] = sine_ref[int_ref[0, d]]
+    mine = sine_ref[own]
+    onto = onto_ref[band]
+    for ky in range(CG):
+        part = inverse_ref[8 * ky : 8 * ky + 8] * onto
+        for j in range(8):
+            at = ky * 64 + j * 8
+            left_ref[at : at + 8] = part * mine[j : j + 1]
+    green_ref[...] = dot3(left_ref[...], right_ref[...], (((1,), (1,)), ((), ())))
+
+
 def density_kernel(
-    g_ref, f_ref, weight_ref, din_ref, gather_ref, vec_ref,
-    out_ref, coarse_ref, own_ref, edge_ref,
-    point_ref, fresh_ref, rows_ref, sems,
+    g_ref, f_ref, weight_ref, din_ref, gather_ref, int_ref, sine_ref, inverse_ref, onto_ref,
+    out_ref, coarse_ref, own_ref, edge_ref, vec_ref, side_ref, green_ref,
+    point_ref, fresh_ref, rows_ref, left_ref, right_ref, scalar_ref, sems,
 ):
+    scalars = pltpu.make_async_copy(int_ref, scalar_ref, sems.at[7])
+    scalars.start()
     total = g_ref[0]
     for k in range(1, BANDS):
         total = total + g_ref[k]
@@ -245,6 +307,13 @@
     for k in range(BANDS):
         coarse_ref[k] = tile
 
+    scalars.wait()
+    if INTERPRET:
+        dom, band = scalar_ref[3, 0], scalar_ref[3, 1]
+    else:
+        dom, band = lax.axis_index("dom"), lax.axis_index("band")
+    own = scalar_ref[0, dom]
+    lane_weights(scalar_ref, own, vec_ref)
     lane, z = lane_index((8, ROW))
     low_edge = (z < BUFFER - 0.5) & (lane < GG)
     high_edge = (z > G - BUFFER - 0.5) & (lane < GG)
@@ -263,11 +332,17 @@
     for t in range(7):
         source, at = (first, 128 * t) if t < 5 else (rest, 128 * (t - 5))
         edge_ref[t + 1 : t + 2] = source[0:1, at : at + 128]
+    poisson_operator(
+        scalar_ref, own, band, sine_ref, inverse_ref, onto_ref, side_ref, green_ref, left_ref, right_ref
+    )
     for copy in copies:
         copy.wait()
 
 
-def density_parts(grams, flat, weight, din, gather, vectors):
+def density_parts(grams, flat, weight, din, gather, integers, sine, inverse, onto):
+    if INTERPRET:
+        axes = jnp.stack([lax.axis_index("dom"), lax.axis_index("band")])
+        integers = integers.at[3, :2].set(axes)
     vmem = pl.BlockSpec(memory_space=pltpu.VMEM)
     return pl.pallas_call(
         density_kernel,
@@ -276,98 +351,25 @@
             jax.ShapeDtypeStruct((BANDS, 8, 128), F32),
             jax.ShapeDtypeStruct((PLANES, 1, GG), F32),
             jax.ShapeDtypeStruct((8, 128), F32),
+            jax.ShapeDtypeStruct((8, ROW), F32),
+            jax.ShapeDtypeStruct((2, DOMS, 128), F32),
+            jax.ShapeDtypeStruct((512, 256), F32),
         ),
-        in_specs=[vmem] * 6,
-        out_specs=(pl.BlockSpec(memory_space=pltpu.HBM), vmem, vmem, vmem),
+        in_specs=[vmem] * 9,
+        out_specs=(pl.BlockSpec(memory_space=pltpu.HBM), vmem, vmem, vmem, vmem, vmem, vmem),
         scratch_shapes=[
             pltpu.VMEM((SHARE, NB), F32),
             pltpu.VMEM((8, SHARE), F32),
             pltpu.VMEM((16, ROW), F32),
-            pltpu.SemaphoreType.DMA((7,)),
+            pltpu.VMEM((512, NZC), F32),
+            pltpu.VMEM((256, NZC), F32),
+            pltpu.SMEM((8, 128), jnp.int32),
+            pltpu.SemaphoreType.DMA((8,)),
         ],
         compiler_params=LIMIT,
         interpret=INTERPRET,
         name="density",
-    )(grams, flat, weight, din, gather, vectors)
-
-
-def place_kernel(
-    pos_ref, mix_ref, corr_ref, occ_ref, sine_ref, inverse_ref, onto_ref,
-    vec_ref, side_ref, green_ref, weight_ref, left_ref, right_ref,
-):
-    if INTERPRET:
-        dom, band = pos_ref[DOMS], pos_ref[DOMS + 1]
-    else:
-        dom, band = lax.axis_index("dom"), lax.axis_index("band")
-    own = pos_ref[dom]
-    shape = (8, ROW)
-    _, z = lane_index(shape)
-    corr = jnp.zeros(shape, F32)
-    for j in range(BUFFER):
-        here = (jnp.abs(z - j) < 0.5) | (jnp.abs(z - (G - BUFFER + j)) < 0.5)
-        corr = jnp.where(here, corr_ref[j].astype(F32), corr)
-    corr = corr * (1.0 / 16.0)
-    fresh_weight = jnp.full(shape, mix_ref[0].astype(F32))
-    input_weight = jnp.full(shape, mix_ref[1].astype(F32))
-    both = fresh_weight + input_weight
-    fresh_weight = fresh_weight / both
-    input_weight = input_weight / both
-    has_left = jnp.where(jnp.full(shape, own) > 0, 1.0, 0.0)
-    has_right = jnp.where(jnp.full(shape, own) < DOMS - 1, 1.0, 0.0)
-    low_z = z < BUFFER - 0.5
-    high_z = z > G - BUFFER - 0.5
-    from_left = jnp.where(low_z, corr * has_left, 0.0)
-    from_right = jnp.where(high_z, (1.0 - corr) * has_right, 0.0)
-    keep = 1.0 - from_left - from_right
-    cell = 1.0 / 27.0
-    vec_ref[0:1] = (cell * fresh_weight * jnp.where(high_z, corr * has_right, keep))[0:1]
-    vec_ref[1:2] = jnp.where(high_z, 0.0, cell * input_weight)[0:1]
-    vec_ref[2:3] = (fresh_weight * from_left)[0:1]
-    vec_ref[3:4] = (fresh_weight * from_right)[0:1]
-    vec_ref[4:5] = (fresh_weight * keep)[0:1]
-    vec_ref[5:6] = input_weight[0:1]
-
-    left, right = jnp.int32(0), jnp.int32(0)
-    for d in range(DOMS):
-        left = jnp.where(pos_ref[d] == own - 1, d, left)
-        right = jnp.where(pos_ref[d] == own + 1, d, right)
-        right_ref[8 * d : 8 * d + 8] = sine_ref[pos_ref[d]]
-    side_ref[0] = left
-    side_ref[1] = right
-    mine = sine_ref[own]
-    onto = onto_ref[band]
-    for ky in range(CG):
-        part = inverse_ref[8 * ky : 8 * ky + 8] * onto
-        for j in range(8):
-            at = ky * 64 + j * 8
-            left_ref[at : at + 8] = part * mine[j : j + 1]
-    eye = lax.broadcasted_iota(jnp.int32, (NB, NB), 0) == lax.broadcasted_iota(jnp.int32, (NB, NB), 1)
-    weight = jnp.sum(jnp.where(eye, occ_ref[...] * (1.0 / NB), 0.0), axis=1, keepdims=True)
-    weight_ref[...] = jnp.broadcast_to(weight, (NB, 256))
-    green_ref[...] = dot3(left_ref[...], right_ref[...], (((1,), (1,)), ((), ())))
-
-
-def placed(position, mixing, corr, occupation, sine, inverse, onto):
-    if INTERPRET:
-        position = jnp.append(position, jnp.stack([lax.axis_index("dom"), lax.axis_index("band")]))
-    smem = pl.BlockSpec(memory_space=pltpu.SMEM)
-    vmem = pl.BlockSpec(memory_space=pltpu.VMEM)
-    return pl.pallas_call(
-        place_kernel,
-        out_shape=(
-            jax.ShapeDtypeStruct((8, ROW), F32),
-            jax.ShapeDtypeStruct((2,), jnp.int32),
-            jax.ShapeDtypeStruct((512, 256), F32),
-            jax.ShapeDtypeStruct((NB, 256), F32),
-        ),
-        in_specs=[smem] * 3 + [vmem] * 4,
-        out_specs=(vmem, smem, vmem, vmem),
-        scratch_shapes=[pltpu.VMEM((512, NZC), F32), pltpu.VMEM((256, NZC), F32)],
-        cost_estimate=pl.CostEstimate(flops=1_000_000, bytes_accessed=100_000, transcendentals=0),
-        compiler_params=LIMIT,
-        interpret=INTERPRET,
-        name="place",
-    )(position, mixing, corr, occupation, sine, inverse, onto)
+    )(grams, flat, weight, din, gather, integers, sine, inverse, onto)
 
 
 def share_kernel(rows_ref, vec_ref, green_ref, over_x_ref, over_y_ref, edge_ref, out_ref, turn_ref, line_ref):
@@ -414,14 +416,20 @@
         hart_ref[j] = total[0:1, 8 * j : 8 * j + 8]
     lane = lax.broadcasted_iota(jnp.int32, (8, ROW), 1)
 
+    def picked(side):
+        tile = jnp.zeros((8, 128), F32)
+        for d in range(DOMS):
+            tile = tile + side_ref[side, d : d + 1] * msg_ref[d]
+        return tile
+
     def rows(tile):
         spread = [jnp.broadcast_to(tile[t + 1 : t + 2], (8, 128)) for t in range(7)]
         front = jnp.concatenate(spread[:5], 1)
         back = jnp.concatenate(spread[4:] + spread[5:], 1)
         return front, rolled(back, -64)
 
-    left0, left2 = rows(msg_ref[side_ref[0]])
-    right0, right2 = rows(msg_ref[side_ref[1]])
+    left0, left2 = rows(picked(0))
+    right0, right2 = rows(picked(1))
     far = G - BUFFER
     left_last = jnp.where(lane < HALF_ROW, rolled(left2, -far), rolled(left2, HALF_ROW + 12 - far))
     right_last = jnp.where(lane < HALF_ROW, rolled(right2, far), rolled(right2, HALF_ROW - 12 + far))
@@ -433,16 +441,12 @@
 
 
 def final_parts(sides, msg, own, vectors):
-    smem = pl.BlockSpec(memory_space=pltpu.SMEM)
-    vmem = pl.BlockSpec(memory_space=pltpu.VMEM)
     return pl.pallas_call(
         final_kernel,
         out_shape=(
             jax.ShapeDtypeStruct((PLANES, 1, GG), F32),
             jax.ShapeDtypeStruct((CZ, 1, CG), F32),
         ),
-        in_specs=[smem, vmem, vmem, vmem],
-        out_specs=(vmem, vmem),
         compiler_params=LIMIT,
         interpret=INTERPRET,
         name="final",
@@ -456,13 +460,13 @@
 def body(orbitals, potential, density_in, occupation, position, mixing, correlation_weight):
     sine, inverse, onto, gather, over_x, over_y = tables()
     din = jnp.transpose(density_in, (1, 0, 2))
-    vectors, sides, green, weight = placed(
-        position, mixing, correlation_weight, occupation.reshape(1, NB), sine, inverse, onto
-    )
-    filtered = filtered_shares(orbitals[0], potential[0], vectors)
+    small = [v.reshape(1, -1) for v in (occupation, position, mixing, correlation_weight)]
+    filtered, weight, integers = filtered_shares(orbitals[0], potential[0], *small)
     flat = exchanged(filtered, "band").reshape(NB, SHARE)
     grams = exchanged(packed_grams(flat), "band")
-    points, coarse, own, edges = density_parts(grams, flat, weight, din, gather, vectors)
+    points, coarse, own, edges, vectors, sides, green = density_parts(
+        grams, flat, weight, din, gather, integers, sine, inverse, onto
+    )
     rows = exchanged(coarse, "band")
     msg = exchanged(hartree_shares(rows, vectors, green, over_x, over_y, edges), "dom")
     dens, hart = final_parts(sides, msg, own, vectors)

time: 67.5 us -> 66 us (0.978)
  Pallas kernels: 7.82 us -> 5.97 us
    pallas_call x2 -> x1, Pallas kernels: 3 us -> 1.49 us  [filtered_shares(): pl.pallas_call(filter_kernel, out_shape=(jax.ShapeDtypeStruct((BANDS, LOC...]
where the time goes in v6:
time: 66 us; the launch traced here: 65.7 us
  blocking collectives  57.9 us (88%)
  Pallas kernels  5.97 us (9%)
  local copies, waits for them, and re-layouts  1.04 us (2%)
  between operations  0.78 us (1%)
    all_to_all x4, blocking collectives, exchanged(): return lax.all_to_all(x, axis, split_axis=0, concat_axis=0, tiled=True)  57.9 us
    pallas_call x1, Pallas kernels, density_parts(): pl.pallas_call(density_kernel, out_shape=(jax.ShapeDtypeStruct((PLANES *...  2.37 us
    pallas_call x1, Pallas kernels, filtered_shares(): pl.pallas_call(filter_kernel, out_shape=(jax.ShapeDtypeStruct((BANDS, LOC...  1.49 us

profile of v6, /device:TPU:1, one launch (start us, length us, event | category | flops | bytes accessed | tf_op | source)
XLA Modules:
  0.0 65.7 jit_solution(5765537254357317410)
XLA Ops:
  0.6 0.0 copy-start.7
  0.6 0.0 copy-start
  0.7 0.0 copy-start.12
  0.7 0.2 matrix.1.mat_ref
  0.9 0.0 copy-start.9
  0.9 0.0 copy-start.10
  0.9 0.0 copy-start.11
  0.9 0.6 copy-done.7
  1.5 0.4 copy-done
  1.9 0.0 copy-done.12
  1.9 0.0 copy-done.9
  1.9 0.0 copy-done.10
  1.9 0.0 copy-done.11
  1.9 1.5 %filter.1 = (f32[8,16,1792]{2,1,0:T(8,128)S(1)}, f32[128,256]{1,0:T(8,128)S(1)}, s32[8,128]{1,0:T(8,128)S(1)}) custom-call(f32[16,24,576]{2,1,0:T(8,128)S(1)} %bitcast.21, f32[24,576]{1,0:T(8,128)S(1)} %bitcast.22, bf16[640,640]{1,0:T(8,128)(2,1)S(1)} %matrix.1.mat_ref, f32[1,128]{1,0:T(1,128)S(1)} %bitcast.24, s32[1,32]{1,0:T(1,128)S(1)} %bitcast.25, ...), custom_call_target="tpu_custom_call" | custom-call | tf_op jit(solution)/shard_map/filter/pallas_call | solution.py:156
  3.4 19.3 %all_to_all.20 = f32[8,16,1792]{2,1,0:T(8,128)S(1)} all-to-all(f32[8,16,1792]{2,1,0:T(8,128)S(1)} %get-tuple-element.15), channel_id=1, replica_groups=mesh['dom'=32,'band'=8] {'band'}, dimensions={0} | all-to-all | bytes 1835008 | tf_op jit(solution)/shard_map/all_to_all | solution.py:457
  22.7 0.0 copy-start.1
  22.7 0.6 gram.1
  23.3 0.0 copy-start.2
  23.3 0.0 copy-start.3
  23.3 0.0 copy-start.6
  23.4 0.0 copy-start.8
  23.4 10.7 %all_to_all.21.g_ref = f32[8,72,128]{2,1,0:T(8,128)S(1)} all-to-all(f32[8,72,128]{2,1,0:T(8,128)S(1)} %gram.1), channel_id=1, replica_groups=mesh['dom'=32,'band'=8] {'band'}, dimensions={0} | all-to-all | bytes 589824 | tf_op jit(solution)/shard_map/all_to_all | solution.py:457
  34.0 0.0 copy-done.1
  34.0 0.0 copy-done.2
  34.0 0.0 copy-done.3
  34.0 0.0 copy-done.6
  34.0 0.0 copy-done.8
  34.1 0.0 copy-start.5
  34.1 2.4 %density.1 = (f32[1728,128]{1,0:T(8,128)}, f32[8,8,128]{2,1,0:T(8,128)S(1)}, f32[3,1,576]{2,1,0:T(1,128)S(1)}, f32[8,128]{1,0:T(8,128)S(1)}, f32[8,640]{1,0:T(8,...) custom-call(f32[8,72,128]{2,1,0:T(8,128)S(1)} %all_to_all.21.g_ref, f32[128,1792]{1,0:T(8,128)S(1)} %bitcast.20, ...), custom_call_target="tpu_custom_call" | custom-call | tf_op jit(solution)/shard_map/density/pallas_call | solution.py:347
  36.4 0.0 copy-start.4
  36.5 7.8 %all_to_all.22.rows_ref = f32[8,8,128]{2,1,0:T(8,128)S(1)} all-to-all(f32[8,8,128]{2,1,0:T(8,128)S(1)} %get-tuple-element.20), channel_id=1, replica_groups=mesh['dom'=32,'band'=8] {'band'}, dimensions={0} | all-to-all | bytes 65536 | tf_op jit(solution)/shard_map/all_to_all | solution.py:457
  44.2 0.0 copy-done.5
  44.2 0.0 copy-done.4
  44.3 0.5 share.1
  44.7 20.1 %all_to_all.23.msg_ref = f32[32,8,128]{2,1,0:T(8,128)S(1)} all-to-all(f32[32,8,128]{2,1,0:T(8,128)S(1)} %share.1), channel_id=1, replica_groups=mesh['dom'=32,'band'=8] {'dom'}, dimensions={0} | all-to-all | bytes 262144 | tf_op jit(solution)/shard_map/all_to_all | solution.py:457
  64.9 0.8 %final.1 = (f32[3,1,576]{2,1,0:T(1,128)}, f32[6,1,8]{2,1,0:T(1,128)}) custom-call(f32[2,32,128]{2,1,0:T(8,128)S(1)} %get-tuple-element.19.side_ref, f32[32,8,128]{2,1,0:T(8,128)S(1)} %all_to_all.23.msg_ref, f32[3,1,576]{2,1,0:T(1,128)S(1)} %get-tuple-element.24.own_ref, f32[8,640]{1,0:T(8,128)S(1)} %get-tuple-element.21.vec_ref), custom_call_target="tpu_custom_call" | custom-call | tf_op jit(solution)/shard_map/final/pallas_call | solution.py:444
Async XLA Ops:
  0.6 0.8 %copy-start.7 = (f32[1,24,576]{2,1,0:T(8,128)S(1)}, f32[1,24,576]{2,1,0:T(8,128)}, u32[]{:S(2)}) copy-start(f32[1,24,576]{2,1,0:T(8,128)} %param.14) | copy-start | bytes 165892
  0.6 1.2 %copy-start = (f32[1,16,24,576]{3,2,1,0:T(8,128)S(1)}, f32[1,16,24,576]{3,2,1,0:T(8,128)}, u32[]{:S(2)}) copy-start(f32[1,16,24,576]{3,2,1,0:T(8,128)} %param.13) | copy-start | bytes 2654212
  0.7 1.2 %copy-start.12 = (s32[6]{0:T(128)S(1)}, s32[6]{0:T(128)}, u32[]{:S(2)}) copy-start(s32[6]{0:T(128)} %param.19) | copy-start | bytes 76
  0.9 1.0 %copy-start.9 = (f32[128]{0:T(128)S(1)}, f32[128]{0:T(128)}, u32[]{:S(2)}) copy-start(f32[128]{0:T(128)} %param.16) | copy-start | bytes 1540
  0.9 1.0 %copy-start.10 = (s32[32]{0:T(128)S(1)}, s32[32]{0:T(128)}, u32[]{:S(2)}) copy-start(s32[32]{0:T(128)} %param.17) | copy-start | bytes 388
  0.9 1.0 %copy-start.11 = (s32[2]{0:T(128)S(1)}, s32[2]{0:T(128)}, u32[]{:S(2)}) copy-start(s32[2]{0:T(128)} %param.18) | copy-start | bytes 28
  22.7 11.3 %copy-start.1 = (f32[640,256]{1,0:T(8,128)S(1)}, f32[640,256]{1,0:T(8,128)}, u32[]{:S(2)}) copy-start(f32[640,256]{1,0:T(8,128)} %constant.12.clone.gather_ref) | copy-start | bytes 1966084
  23.3 10.7 %copy-start.2 = (f32[32,8,192]{2,1,0:T(8,128)S(1)}, f32[32,8,192]{2,1,0:T(8,128)}, u32[]{:S(2)}) copy-start(f32[32,8,192]{2,1,0:T(8,128)} %constant.13.clone.sine_ref) | copy-start | bytes 589828
  23.3 10.7 %copy-start.3 = (f32[8,8,192]{2,1,0:T(8,128)S(1)}, f32[8,8,192]{2,1,0:T(8,128)}, u32[]{:S(2)}) copy-start(f32[8,8,192]{2,1,0:T(8,128)} %constant.15.clone.onto_ref) | copy-start | bytes 147460
  23.3 10.7 %copy-start.6 = (f32[64,192]{1,0:T(8,128)S(1)}, f32[64,192]{1,0:T(8,128)}, u32[]{:S(2)}) copy-start(f32[64,192]{1,0:T(8,128)} %constant.14.clone.inverse_ref) | copy-start | bytes 147460
  23.4 10.7 %copy-start.8 = (f32[1,3,576]{2,0,1:T(1,128)S(1)}, f32[1,3,576]{2,0,1:T(1,128)}, u32[]{:S(2)}) copy-start(f32[1,3,576]{2,0,1:T(1,128)} %param.15) | copy-start | bytes 20740
  34.1 10.2 %copy-start.5 = (f32[8,8,256]{2,1,0:T(8,128)S(1)}, f32[8,8,256]{2,1,0:T(8,128)}, u32[]{:S(2)}) copy-start(f32[8,8,256]{2,1,0:T(8,128)} %constant.16.clone.over_x_ref) | copy-start | bytes 196612
  36.4 7.8 %copy-start.4 = (f32[8,8,256]{2,1,0:T(8,128)S(1)}, f32[8,8,256]{2,1,0:T(8,128)}, u32[]{:S(2)}) copy-start(f32[8,8,256]{2,1,0:T(8,128)} %constant.17.clone.over_y_ref) | copy-start | bytes 196612

commit v7 on v6

--- a/solution.py
+++ b/solution.py
@@ -30,6 +30,8 @@
 HALF = 0.5 * (FILTER_HIGH - FILTER_LOW)
 HIGHEST = lax.Precision.HIGHEST
 F32 = jnp.float32
+EARLY = range(4)
+LATE = range(4, 7)
 INTERPRET = False
 LIMIT = pltpu.CompilerParams(vmem_limit_bytes=16 << 20)
 
@@ -246,9 +248,28 @@
     green_ref[...] = dot3(left_ref[...], right_ref[...], (((1,), (1,)), ((), ())))
 
 
+def write_points(chunks, f_ref, poly, out_ref, point_ref, sems):
+    poly_high, poly_low = halves(poly)
+    dot = functools.partial(jnp.dot, preferred_element_type=F32)
+    copies = []
+    for c in chunks:
+        start, count = 256 * c, min(256, PLANES * GG - 256 * c)
+        here = 256 * (c - chunks[0])
+        for at in range(0, count, 128):
+            high, low = halves(f_ref[:, start + at : start + at + 128].T)
+            value = dot(high, poly_high) + (dot(high, poly_low) + dot(low, poly_high))
+            point_ref[here + at : here + at + 128] = value
+        copy = pltpu.make_async_copy(
+            point_ref.at[pl.ds(here, count)], out_ref.at[pl.ds(start, count)], sems.at[c - chunks[0]]
+        )
+        copy.start()
+        copies.append(copy)
+    return copies
+
+
 def density_kernel(
     g_ref, f_ref, weight_ref, din_ref, gather_ref, int_ref, sine_ref, inverse_ref, onto_ref,
-    out_ref, coarse_ref, own_ref, edge_ref, vec_ref, side_ref, green_ref,
+    out_ref, coarse_ref, own_ref, edge_ref, vec_ref, side_ref, green_ref, poly_ref,
     point_ref, fresh_ref, rows_ref, left_ref, right_ref, scalar_ref, sems,
 ):
     scalars = pltpu.make_async_copy(int_ref, scalar_ref, sems.at[7])
@@ -276,16 +297,8 @@
     poly_high, poly_low = halves(poly)
     dot = functools.partial(jnp.dot, preferred_element_type=F32)
 
-    copies = []
-    for c in range(7):
-        start, count = 256 * c, min(256, PLANES * GG - 256 * c)
-        for at in range(start, start + count, 128):
-            high, low = halves(f_ref[:, at : at + 128].T)
-            value = dot(high, poly_high) + (dot(high, poly_low) + dot(low, poly_high))
-            point_ref[at : at + 128] = value
-        part = pl.ds(start, count)
-        copies.append(pltpu.make_async_copy(point_ref.at[part], out_ref.at[part], sems.at[c]))
-        copies[-1].start()
+    copies = write_points(EARLY, f_ref, poly, out_ref, point_ref, sems)
+    poly_ref[...] = poly
 
     both = jnp.concatenate([poly_high, poly_low], 1)
     for c in range(SHARE // 256):
@@ -354,11 +367,12 @@
             jax.ShapeDtypeStruct((8, ROW), F32),
             jax.ShapeDtypeStruct((2, DOMS, 128), F32),
             jax.ShapeDtypeStruct((512, 256), F32),
+            jax.ShapeDtypeStruct((NB, NB), F32),
         ),
         in_specs=[vmem] * 9,
-        out_specs=(pl.BlockSpec(memory_space=pltpu.HBM), vmem, vmem, vmem, vmem, vmem, vmem),
+        out_specs=(pl.BlockSpec(memory_space=pltpu.HBM), *[vmem] * 7),
         scratch_shapes=[
-            pltpu.VMEM((SHARE, NB), F32),
+            pltpu.VMEM((256 * len(EARLY), NB), F32),
             pltpu.VMEM((8, SHARE), F32),
             pltpu.VMEM((16, ROW), F32),
             pltpu.VMEM((512, NZC), F32),
@@ -408,7 +422,10 @@
     )(rows, vectors, green, over_x, over_y, edges)
 
 
-def final_kernel(side_ref, msg_ref, own_ref, vec_ref, dens_ref, hart_ref):
+def final_kernel(
+    side_ref, msg_ref, own_ref, vec_ref, f_ref, poly_ref, early_ref, dens_ref, hart_ref, out_ref, point_ref, sems
+):
+    copies = write_points(LATE, f_ref, poly_ref[...], out_ref, point_ref, sems)
     total = msg_ref[0]
     for d in range(1, DOMS):
         total = total + msg_ref[d]
@@ -438,19 +455,28 @@
     for p in range(PLANES):
         mixed = own_ref[p] + vec_ref[2:3, :GG] * left_part[p][0:1, :GG]
         dens_ref[p] = mixed + vec_ref[3:4, :GG] * right_part[p][0:1, :GG]
-
-
-def final_parts(sides, msg, own, vectors):
+    for copy in copies:
+        copy.wait()
+
+
+def final_parts(sides, msg, own, vectors, flat, poly, points):
+    vmem = pl.BlockSpec(memory_space=pltpu.VMEM)
+    hbm = pl.BlockSpec(memory_space=pltpu.HBM)
     return pl.pallas_call(
         final_kernel,
         out_shape=(
             jax.ShapeDtypeStruct((PLANES, 1, GG), F32),
             jax.ShapeDtypeStruct((CZ, 1, CG), F32),
+            jax.ShapeDtypeStruct((PLANES * GG, NB), F32),
         ),
+        in_specs=[vmem] * 6 + [hbm],
+        out_specs=(vmem, vmem, hbm),
+        input_output_aliases={6: 2},
+        scratch_shapes=[pltpu.VMEM((256 * len(LATE), NB), F32), pltpu.SemaphoreType.DMA((len(LATE),))],
         compiler_params=LIMIT,
         interpret=INTERPRET,
         name="final",
-    )(sides, msg, own, vectors)
+    )(sides, msg, own, vectors, flat, poly, points)
 
 
 def exchanged(x, axis):
@@ -464,12 +490,12 @@
     filtered, weight, integers = filtered_shares(orbitals[0], potential[0], *small)
     flat = exchanged(filtered, "band").reshape(NB, SHARE)
     grams = exchanged(packed_grams(flat), "band")
-    points, coarse, own, edges, vectors, sides, green = density_parts(
+    points, coarse, own, edges, vectors, sides, green, poly = density_parts(
         grams, flat, weight, din, gather, integers, sine, inverse, onto
     )
     rows = exchanged(coarse, "band")
     msg = exchanged(hartree_shares(rows, vectors, green, over_x, over_y, edges), "dom")
-    dens, hart = final_parts(sides, msg, own, vectors)
+    dens, hart, points = final_parts(sides, msg, own, vectors, flat, poly, points)
     orbitals_out = jnp.transpose(points.reshape(PLANES, GG, NB), (2, 0, 1)).reshape(1, NB, PLANES, GG)
     density = jnp.transpose(dens, (1, 0, 2))
     hartree = jnp.transpose(hart, (1, 2, 0)).reshape(1, 1, CG, CZ)

time: 66 us -> 66.7 us (1.011)
  Pallas kernels: 5.97 us -> 6.69 us
    pallas_call x1, Pallas kernels: 0.8 us -> 1.67 us  [final_parts(): pl.pallas_call(final_kernel, out_shape=(jax.ShapeDtypeStruct((PLANES, 1,...]
where the time goes in v7:
time: 66.7 us; the launch traced here: 66.4 us
  blocking collectives  57.9 us (87%)
  Pallas kernels  6.69 us (10%)
  local copies, waits for them, and re-layouts  1.04 us (2%)
  between operations  0.78 us (1%)
    all_to_all x4, blocking collectives, exchanged(): return lax.all_to_all(x, axis, split_axis=0, concat_axis=0, tiled=True)  57.9 us
    pallas_call x1, Pallas kernels, density_parts(): pl.pallas_call(density_kernel, out_shape=(jax.ShapeDtypeStruct((PLANES *...  2.22 us
    pallas_call x1, Pallas kernels, final_parts(): pl.pallas_call(final_kernel, out_shape=(jax.ShapeDtypeStruct((PLANES, 1,...  1.67 us
    pallas_call x1, Pallas kernels, filtered_shares(): pl.pallas_call(filter_kernel, out_shape=(jax.ShapeDtypeStruct((BANDS, LOC...  1.49 us

profile of v7, /device:TPU:1, one launch (start us, length us, event | category | flops | bytes accessed | tf_op | source)
XLA Modules:
  0.0 66.4 jit_solution(5529602000830501053)
XLA Ops:
  0.6 0.0 copy-start.7
  0.6 0.0 copy-start
  0.7 0.0 copy-start.12
  0.7 0.2 matrix.1.mat_ref
  0.9 0.0 copy-start.9
  0.9 0.0 copy-start.10
  0.9 0.0 copy-start.11
  0.9 0.6 copy-done.7
  1.5 0.4 copy-done
  1.9 0.0 copy-done.12
  1.9 0.0 copy-done.9
  1.9 0.0 copy-done.10
  1.9 0.0 copy-done.11
  1.9 1.5 %filter.1 = (f32[8,16,1792]{2,1,0:T(8,128)S(1)}, f32[128,256]{1,0:T(8,128)S(1)}, s32[8,128]{1,0:T(8,128)S(1)}) custom-call(f32[16,24,576]{2,1,0:T(8,128)S(1)} %bitcast.22, f32[24,576]{1,0:T(8,128)S(1)} %bitcast.23, bf16[640,640]{1,0:T(8,128)(2,1)S(1)} %matrix.1.mat_ref, f32[1,128]{1,0:T(1,128)S(1)} %bitcast.25, s32[1,32]{1,0:T(1,128)S(1)} %bitcast.26, ...), custom_call_target="tpu_custom_call" | custom-call | tf_op jit(solution)/shard_map/filter/pallas_call | solution.py:158
  3.4 19.3 %all_to_all.20 = f32[8,16,1792]{2,1,0:T(8,128)S(1)} all-to-all(f32[8,16,1792]{2,1,0:T(8,128)S(1)} %get-tuple-element.17), channel_id=1, replica_groups=mesh['dom'=32,'band'=8] {'band'}, dimensions={0} | all-to-all | bytes 1835008 | tf_op jit(solution)/shard_map/all_to_all | solution.py:483
  22.7 0.0 copy-start.1
  22.7 0.6 gram.1
  23.3 0.0 copy-start.2
  23.3 0.0 copy-start.3
  23.3 0.0 copy-start.6
  23.4 0.0 copy-start.8
  23.4 10.7 %all_to_all.21.g_ref = f32[8,72,128]{2,1,0:T(8,128)S(1)} all-to-all(f32[8,72,128]{2,1,0:T(8,128)S(1)} %gram.1), channel_id=1, replica_groups=mesh['dom'=32,'band'=8] {'band'}, dimensions={0} | all-to-all | bytes 589824 | tf_op jit(solution)/shard_map/all_to_all | solution.py:483
  34.0 0.0 copy-done.1
  34.0 0.0 copy-done.2
  34.0 0.0 copy-done.3
  34.0 0.0 copy-done.6
  34.0 0.0 copy-done.8
  34.1 0.0 copy-start.5
  34.1 2.2 %density.1 = (f32[1728,128]{1,0:T(8,128)}, f32[8,8,128]{2,1,0:T(8,128)S(1)}, f32[3,1,576]{2,1,0:T(1,128)S(1)}, f32[8,128]{1,0:T(8,128)S(1)}, f32[8,640]{1,0:T(8,...) custom-call(f32[8,72,128]{2,1,0:T(8,128)S(1)} %all_to_all.21.g_ref, ...), custom_call_target="tpu_custom_call" | custom-call | tf_op jit(solution)/shard_map/density/pallas_call | solution.py:360
  36.3 0.0 copy-start.4
  36.3 7.8 %all_to_all.22.rows_ref = f32[8,8,128]{2,1,0:T(8,128)S(1)} all-to-all(f32[8,8,128]{2,1,0:T(8,128)S(1)} %get-tuple-element.21), channel_id=1, replica_groups=mesh['dom'=32,'band'=8] {'band'}, dimensions={0} | all-to-all | bytes 65536 | tf_op jit(solution)/shard_map/all_to_all | solution.py:483
  44.1 0.0 copy-done.5
  44.1 0.0 copy-done.4
  44.1 0.5 share.1
  44.6 20.1 %all_to_all.23.msg_ref = f32[32,8,128]{2,1,0:T(8,128)S(1)} all-to-all(f32[32,8,128]{2,1,0:T(8,128)S(1)} %share.1), channel_id=1, replica_groups=mesh['dom'=32,'band'=8] {'dom'}, dimensions={0} | all-to-all | bytes 262144 | tf_op jit(solution)/shard_map/all_to_all | solution.py:483
  64.7 1.7 %final.1 = (f32[3,1,576]{2,1,0:T(1,128)}, f32[6,1,8]{2,1,0:T(1,128)}, f32[1728,128]{1,0:T(8,128)}) custom-call(f32[2,32,128]{2,1,0:T(8,128)S(1)} %get-tuple-element.20.side_ref, f32[32,8,128]{2,1,0:T(8,128)S(1)} %all_to_all.23.msg_ref, f32[3,1,576]{2,1,0:T(1,128)S(1)} %get-tuple-element.25.own_ref, ...), custom_call_target="tpu_custom_call", output_to_operand_aliasing={{2}: (6, {})} | custom-call | tf_op jit(solution)/shard_map/final/pallas_call | solution.py:465
Async XLA Ops:
  0.6 0.8 %copy-start.7 = (f32[1,24,576]{2,1,0:T(8,128)S(1)}, f32[1,24,576]{2,1,0:T(8,128)}, u32[]{:S(2)}) copy-start(f32[1,24,576]{2,1,0:T(8,128)} %param.14) | copy-start | bytes 165892
  0.6 1.2 %copy-start = (f32[1,16,24,576]{3,2,1,0:T(8,128)S(1)}, f32[1,16,24,576]{3,2,1,0:T(8,128)}, u32[]{:S(2)}) copy-start(f32[1,16,24,576]{3,2,1,0:T(8,128)} %param.13) | copy-start | bytes 2654212
  0.7 1.2 %copy-start.12 = (s32[6]{0:T(128)S(1)}, s32[6]{0:T(128)}, u32[]{:S(2)}) copy-start(s32[6]{0:T(128)} %param.19) | copy-start | bytes 76
  0.9 1.0 %copy-start.9 = (f32[128]{0:T(128)S(1)}, f32[128]{0:T(128)}, u32[]{:S(2)}) copy-start(f32[128]{0:T(128)} %param.16) | copy-start | bytes 1540
  0.9 1.0 %copy-start.10 = (s32[32]{0:T(128)S(1)}, s32[32]{0:T(128)}, u32[]{:S(2)}) copy-start(s32[32]{0:T(128)} %param.17) | copy-start | bytes 388
  0.9 1.0 %copy-start.11 = (s32[2]{0:T(128)S(1)}, s32[2]{0:T(128)}, u32[]{:S(2)}) copy-start(s32[2]{0:T(128)} %param.18) | copy-start | bytes 28
  22.7 11.3 %copy-start.1 = (f32[640,256]{1,0:T(8,128)S(1)}, f32[640,256]{1,0:T(8,128)}, u32[]{:S(2)}) copy-start(f32[640,256]{1,0:T(8,128)} %constant.12.clone.gather_ref) | copy-start | bytes 1966084
  23.3 10.7 %copy-start.2 = (f32[32,8,192]{2,1,0:T(8,128)S(1)}, f32[32,8,192]{2,1,0:T(8,128)}, u32[]{:S(2)}) copy-start(f32[32,8,192]{2,1,0:T(8,128)} %constant.13.clone.sine_ref) | copy-start | bytes 589828
  23.3 10.7 %copy-start.3 = (f32[8,8,192]{2,1,0:T(8,128)S(1)}, f32[8,8,192]{2,1,0:T(8,128)}, u32[]{:S(2)}) copy-start(f32[8,8,192]{2,1,0:T(8,128)} %constant.15.clone.onto_ref) | copy-start | bytes 147460
  23.3 10.7 %copy-start.6 = (f32[64,192]{1,0:T(8,128)S(1)}, f32[64,192]{1,0:T(8,128)}, u32[]{:S(2)}) copy-start(f32[64,192]{1,0:T(8,128)} %constant.14.clone.inverse_ref) | copy-start | bytes 147460
  23.4 10.7 %copy-start.8 = (f32[1,3,576]{2,0,1:T(1,128)S(1)}, f32[1,3,576]{2,0,1:T(1,128)}, u32[]{:S(2)}) copy-start(f32[1,3,576]{2,0,1:T(1,128)} %param.15) | copy-start | bytes 20740
  34.1 10.0 %copy-start.5 = (f32[8,8,256]{2,1,0:T(8,128)S(1)}, f32[8,8,256]{2,1,0:T(8,128)}, u32[]{:S(2)}) copy-start(f32[8,8,256]{2,1,0:T(8,128)} %constant.16.clone.over_x_ref) | copy-start | bytes 196612
  36.3 7.8 %copy-start.4 = (f32[8,8,256]{2,1,0:T(8,128)S(1)}, f32[8,8,256]{2,1,0:T(8,128)}, u32[]{:S(2)}) copy-start(f32[8,8,256]{2,1,0:T(8,128)} %constant.17.clone.over_y_ref) | copy-start | bytes 196612

commit v8 on v6

--- a/solution.py
+++ b/solution.py
@@ -230,26 +230,25 @@
     vec_ref[5:6] = input_weight[0:1]
 
 
-def poisson_operator(int_ref, own, band, sine_ref, inverse_ref, onto_ref, side_ref, green_ref, left_ref, right_ref):
+def poisson_tables(int_ref, own, band, sine_ref, inverse_ref, onto_ref, side_ref, mine_ref, weigh_ref, right_ref, all_ref):
     for d in range(DOMS):
         place = jnp.full((1, 128), int_ref[0, d])
         side_ref[0, d : d + 1] = jnp.where(place == own - 1, 1.0, 0.0)
         side_ref[1, d : d + 1] = jnp.where(place == own + 1, 1.0, 0.0)
-        right_ref[8 * d : 8 * d + 8] = sine_ref[int_ref[0, d]]
-    mine = sine_ref[own]
+        all_ref[8 * d : 8 * d + 8] = sine_ref[int_ref[0, d]]
+    mine_ref[...] = sine_ref[own]
     onto = onto_ref[band]
     for ky in range(CG):
-        part = inverse_ref[8 * ky : 8 * ky + 8] * onto
-        for j in range(8):
-            at = ky * 64 + j * 8
-            left_ref[at : at + 8] = part * mine[j : j + 1]
-    green_ref[...] = dot3(left_ref[...], right_ref[...], (((1,), (1,)), ((), ())))
+        weigh_ref[8 * ky : 8 * ky + 8] = inverse_ref[8 * ky : 8 * ky + 8] * onto
+    high, low = halves(all_ref[...])
+    right_ref[0] = high
+    right_ref[1] = low
 
 
 def density_kernel(
     g_ref, f_ref, weight_ref, din_ref, gather_ref, int_ref, sine_ref, inverse_ref, onto_ref,
-    out_ref, coarse_ref, own_ref, edge_ref, vec_ref, side_ref, green_ref,
-    point_ref, fresh_ref, rows_ref, left_ref, right_ref, scalar_ref, sems,
+    out_ref, coarse_ref, own_ref, edge_ref, vec_ref, side_ref, mine_ref, weigh_ref, right_ref,
+    point_ref, fresh_ref, rows_ref, all_ref, scalar_ref, sems,
 ):
     scalars = pltpu.make_async_copy(int_ref, scalar_ref, sems.at[7])
     scalars.start()
@@ -332,8 +331,8 @@
     for t in range(7):
         source, at = (first, 128 * t) if t < 5 else (rest, 128 * (t - 5))
         edge_ref[t + 1 : t + 2] = source[0:1, at : at + 128]
-    poisson_operator(
-        scalar_ref, own, band, sine_ref, inverse_ref, onto_ref, side_ref, green_ref, left_ref, right_ref
+    poisson_tables(
+        scalar_ref, own, band, sine_ref, inverse_ref, onto_ref, side_ref, mine_ref, weigh_ref, right_ref, all_ref
     )
     for copy in copies:
         copy.wait()
@@ -353,15 +352,16 @@
             jax.ShapeDtypeStruct((8, 128), F32),
             jax.ShapeDtypeStruct((8, ROW), F32),
             jax.ShapeDtypeStruct((2, DOMS, 128), F32),
-            jax.ShapeDtypeStruct((512, 256), F32),
+            jax.ShapeDtypeStruct((8, NZC), F32),
+            jax.ShapeDtypeStruct((CG * CG, NZC), F32),
+            jax.ShapeDtypeStruct((2, 256, NZC), jnp.bfloat16),
         ),
         in_specs=[vmem] * 9,
-        out_specs=(pl.BlockSpec(memory_space=pltpu.HBM), vmem, vmem, vmem, vmem, vmem, vmem),
+        out_specs=(pl.BlockSpec(memory_space=pltpu.HBM), *[vmem] * 8),
         scratch_shapes=[
             pltpu.VMEM((SHARE, NB), F32),
             pltpu.VMEM((8, SHARE), F32),
             pltpu.VMEM((16, ROW), F32),
-            pltpu.VMEM((512, NZC), F32),
             pltpu.VMEM((256, NZC), F32),
             pltpu.SMEM((8, 128), jnp.int32),
             pltpu.SemaphoreType.DMA((8,)),
@@ -372,7 +372,9 @@
     )(grams, flat, weight, din, gather, integers, sine, inverse, onto)
 
 
-def share_kernel(rows_ref, vec_ref, green_ref, over_x_ref, over_y_ref, edge_ref, out_ref, turn_ref, line_ref):
+def share_kernel(
+    rows_ref, vec_ref, mine_ref, weigh_ref, right_ref, over_x_ref, over_y_ref, edge_ref, out_ref, turn_ref, line_ref
+):
     fresh = jnp.concatenate([rows_ref[:, 0, :], rows_ref[:, 1, :]], 1)
     inputs = jnp.concatenate([rows_ref[:, 2, :], rows_ref[:, 3, :]], 1)
     cells = fresh * vec_ref[0:1, :256] + inputs * vec_ref[1:2, :256]
@@ -380,13 +382,19 @@
     modes = over_x_ref[0] * cells[0:1]
     for x in range(1, CG):
         modes = modes + over_x_ref[x] * cells[x : x + 1]
-    cells = jnp.zeros((8, 256), F32)
+    spectrum = jnp.zeros((8, NZC), F32)
     for ky in range(CG):
-        acc = jnp.zeros((8, 256), F32)
+        acc = jnp.zeros((8, NZC), F32)
         for j in range(8):
-            at = ky * 8 + j
-            acc = acc + jnp.broadcast_to(modes[:, G * ky + 3 * j : G * ky + 3 * j + 1], (8, 256)) * green_ref[8 * at : 8 * at + 8]
-        cells = cells + over_y_ref[ky] * jnp.sum(acc, axis=0, keepdims=True)
+            at = G * ky + 3 * j
+            acc = acc + jnp.broadcast_to(modes[:, at : at + 1], (8, NZC)) * mine_ref[j : j + 1]
+        acc = acc * weigh_ref[8 * ky : 8 * ky + 8]
+        spectrum = spectrum + over_y_ref[ky, :, :NZC] * jnp.sum(acc, axis=0, keepdims=True)
+    high, low = halves(spectrum)
+    dot = functools.partial(
+        lax.dot_general, dimension_numbers=(((1,), (1,)), ((), ())), preferred_element_type=F32
+    )
+    cells = dot(high, right_ref[0]) + (dot(high, right_ref[1]) + dot(low, right_ref[0]))
     turn_ref[...] = jnp.concatenate([cells, jnp.zeros((120, 256), F32)], 0).T
     line_ref[...] = jnp.zeros_like(line_ref)
     for j in range(CZ):
@@ -397,7 +405,7 @@
         out_ref[d] = jnp.where(head, line_ref[d : d + 1], edge)
 
 
-def hartree_shares(rows, vectors, green, over_x, over_y, edges):
+def hartree_shares(rows, vectors, mine, weigh, right, over_x, over_y, edges):
     return pl.pallas_call(
         share_kernel,
         out_shape=jax.ShapeDtypeStruct((DOMS, 8, 128), F32),
@@ -405,7 +413,7 @@
         compiler_params=LIMIT,
         interpret=INTERPRET,
         name="share",
-    )(rows, vectors, green, over_x, over_y, edges)
+    )(rows, vectors, mine, weigh, right, over_x, over_y, edges)
 
 
 def final_kernel(side_ref, msg_ref, own_ref, vec_ref, dens_ref, hart_ref):
@@ -464,11 +472,11 @@
     filtered, weight, integers = filtered_shares(orbitals[0], potential[0], *small)
     flat = exchanged(filtered, "band").reshape(NB, SHARE)
     grams = exchanged(packed_grams(flat), "band")
-    points, coarse, own, edges, vectors, sides, green = density_parts(
+    points, coarse, own, edges, vectors, sides, mine, weigh, right = density_parts(
         grams, flat, weight, din, gather, integers, sine, inverse, onto
     )
     rows = exchanged(coarse, "band")
-    msg = exchanged(hartree_shares(rows, vectors, green, over_x, over_y, edges), "dom")
+    msg = exchanged(hartree_shares(rows, vectors, mine, weigh, right, over_x, over_y, edges), "dom")
     dens, hart = final_parts(sides, msg, own, vectors)
     orbitals_out = jnp.transpose(points.reshape(PLANES, GG, NB), (2, 0, 1)).reshape(1, NB, PLANES, GG)
     density = jnp.transpose(dens, (1, 0, 2))

time: 66 us -> 65.9 us (level)
  no operation moved by 1% of the time
where the time goes in v8:
time: 65.9 us; the launch traced here: 65.7 us
  blocking collectives  57.9 us (88%)
  Pallas kernels  5.94 us (9%)
  local copies, waits for them, and re-layouts  1.04 us (2%)
  between operations  0.78 us (1%)
    all_to_all x4, blocking collectives, exchanged(): return lax.all_to_all(x, axis, split_axis=0, concat_axis=0, tiled=True)  57.9 us
    pallas_call x1, Pallas kernels, density_parts(): pl.pallas_call(density_kernel, out_shape=(jax.ShapeDtypeStruct((PLANES *...  2.16 us
    pallas_call x1, Pallas kernels, filtered_shares(): pl.pallas_call(filter_kernel, out_shape=(jax.ShapeDtypeStruct((BANDS, LOC...  1.49 us

profile of v8, /device:TPU:1, one launch (start us, length us, event | category | flops | bytes accessed | tf_op | source)
XLA Modules:
  0.0 65.7 jit_solution(17549209444051175988)
XLA Ops:
  0.6 0.0 copy-start.7
  0.6 0.0 copy-start
  0.7 0.0 copy-start.12
  0.7 0.2 matrix.1.mat_ref
  0.9 0.0 copy-start.9
  0.9 0.0 copy-start.10
  0.9 0.0 copy-start.11
  0.9 0.6 copy-done.7
  1.5 0.4 copy-done
  1.9 0.0 copy-done.12
  1.9 0.0 copy-done.9
  1.9 0.0 copy-done.10
  1.9 0.0 copy-done.11
  1.9 1.5 %filter.1 = (f32[8,16,1792]{2,1,0:T(8,128)S(1)}, f32[128,256]{1,0:T(8,128)S(1)}, s32[8,128]{1,0:T(8,128)S(1)}) custom-call(f32[16,24,576]{2,1,0:T(8,128)S(1)} %bitcast.21, f32[24,576]{1,0:T(8,128)S(1)} %bitcast.22, bf16[640,640]{1,0:T(8,128)(2,1)S(1)} %matrix.1.mat_ref, f32[1,128]{1,0:T(1,128)S(1)} %bitcast.24, s32[1,32]{1,0:T(1,128)S(1)} %bitcast.25, ...), custom_call_target="tpu_custom_call" | custom-call | tf_op jit(solution)/shard_map/filter/pallas_call | solution.py:156
  3.4 19.3 %all_to_all.20 = f32[8,16,1792]{2,1,0:T(8,128)S(1)} all-to-all(f32[8,16,1792]{2,1,0:T(8,128)S(1)} %get-tuple-element.17), channel_id=1, replica_groups=mesh['dom'=32,'band'=8] {'band'}, dimensions={0} | all-to-all | bytes 1835008 | tf_op jit(solution)/shard_map/all_to_all | solution.py:465
  22.7 0.0 copy-start.1
  22.7 0.6 gram.1
  23.3 0.0 copy-start.2
  23.3 0.0 copy-start.3
  23.3 0.0 copy-start.6
  23.4 0.0 copy-start.8
  23.4 10.7 %all_to_all.21.g_ref = f32[8,72,128]{2,1,0:T(8,128)S(1)} all-to-all(f32[8,72,128]{2,1,0:T(8,128)S(1)} %gram.1), channel_id=1, replica_groups=mesh['dom'=32,'band'=8] {'band'}, dimensions={0} | all-to-all | bytes 589824 | tf_op jit(solution)/shard_map/all_to_all | solution.py:465
  34.0 0.0 copy-done.1
  34.0 0.0 copy-done.2
  34.0 0.0 copy-done.3
  34.0 0.0 copy-done.6
  34.0 0.0 copy-done.8
  34.1 0.0 copy-start.5
  34.1 2.2 %density.1 = (f32[1728,128]{1,0:T(8,128)}, f32[8,8,128]{2,1,0:T(8,128)S(1)}, f32[3,1,576]{2,1,0:T(1,128)S(1)}, f32[8,128]{1,0:T(8,128)S(1)}, f32[8,640]{1,0:T(8,...) custom-call(f32[8,72,128]{2,1,0:T(8,128)S(1)} %all_to_all.21.g_ref, ...), custom_call_target="tpu_custom_call" | custom-call | tf_op jit(solution)/shard_map/density/pallas_call | solution.py:346
  36.2 0.0 copy-start.4
  36.2 7.8 %all_to_all.22.rows_ref = f32[8,8,128]{2,1,0:T(8,128)S(1)} all-to-all(f32[8,8,128]{2,1,0:T(8,128)S(1)} %get-tuple-element.22), channel_id=1, replica_groups=mesh['dom'=32,'band'=8] {'band'}, dimensions={0} | all-to-all | bytes 65536 | tf_op jit(solution)/shard_map/all_to_all | solution.py:465
  44.0 0.0 copy-done.5
  44.0 0.0 copy-done.4
  44.0 0.7 %share.1 = f32[32,8,128]{2,1,0:T(8,128)S(1)} custom-call(f32[8,8,128]{2,1,0:T(8,128)S(1)} %all_to_all.22.rows_ref, f32[8,640]{1,0:T(8,128)S(1)} %get-tuple-element.23.vec_ref, f32[8,192]{1,0:T(8,128)S(1)} %get-tuple-element.24.mine_ref, f32[64,192]{1,0:T(8,128)S(1)} %get-tuple-element.25.weigh_ref, bf16[2,256,192]{2,1,0:T(8,128)(2,1)S(1)} %get-tuple-element.26.right_ref, ...), custom_call_target="tpu_custom_call" | custom-call | tf_op jit(solution)/shard_map/share/pallas_call | solution.py:409
  44.7 20.1 %all_to_all.23.msg_ref = f32[32,8,128]{2,1,0:T(8,128)S(1)} all-to-all(f32[32,8,128]{2,1,0:T(8,128)S(1)} %share.1), channel_id=1, replica_groups=mesh['dom'=32,'band'=8] {'dom'}, dimensions={0} | all-to-all | bytes 262144 | tf_op jit(solution)/shard_map/all_to_all | solution.py:465
  64.9 0.8 %final.1 = (f32[3,1,576]{2,1,0:T(1,128)}, f32[6,1,8]{2,1,0:T(1,128)}) custom-call(f32[2,32,128]{2,1,0:T(8,128)S(1)} %get-tuple-element.21.side_ref, f32[32,8,128]{2,1,0:T(8,128)S(1)} %all_to_all.23.msg_ref, f32[3,1,576]{2,1,0:T(1,128)S(1)} %get-tuple-element.28.own_ref, f32[8,640]{1,0:T(8,128)S(1)} %get-tuple-element.23.vec_ref), custom_call_target="tpu_custom_call" | custom-call | tf_op jit(solution)/shard_map/final/pallas_call | solution.py:452
Async XLA Ops:
  0.6 0.8 %copy-start.7 = (f32[1,24,576]{2,1,0:T(8,128)S(1)}, f32[1,24,576]{2,1,0:T(8,128)}, u32[]{:S(2)}) copy-start(f32[1,24,576]{2,1,0:T(8,128)} %param.14) | copy-start | bytes 165892
  0.6 1.2 %copy-start = (f32[1,16,24,576]{3,2,1,0:T(8,128)S(1)}, f32[1,16,24,576]{3,2,1,0:T(8,128)}, u32[]{:S(2)}) copy-start(f32[1,16,24,576]{3,2,1,0:T(8,128)} %param.13) | copy-start | bytes 2654212
  0.7 1.2 %copy-start.12 = (s32[6]{0:T(128)S(1)}, s32[6]{0:T(128)}, u32[]{:S(2)}) copy-start(s32[6]{0:T(128)} %param.19) | copy-start | bytes 76
  0.9 1.0 %copy-start.9 = (f32[128]{0:T(128)S(1)}, f32[128]{0:T(128)}, u32[]{:S(2)}) copy-start(f32[128]{0:T(128)} %param.16) | copy-start | bytes 1540
  0.9 1.0 %copy-start.10 = (s32[32]{0:T(128)S(1)}, s32[32]{0:T(128)}, u32[]{:S(2)}) copy-start(s32[32]{0:T(128)} %param.17) | copy-start | bytes 388
  0.9 1.0 %copy-start.11 = (s32[2]{0:T(128)S(1)}, s32[2]{0:T(128)}, u32[]{:S(2)}) copy-start(s32[2]{0:T(128)} %param.18) | copy-start | bytes 28
  22.7 11.3 %copy-start.1 = (f32[640,256]{1,0:T(8,128)S(1)}, f32[640,256]{1,0:T(8,128)}, u32[]{:S(2)}) copy-start(f32[640,256]{1,0:T(8,128)} %constant.12.clone.gather_ref) | copy-start | bytes 1966084
  23.3 10.7 %copy-start.2 = (f32[32,8,192]{2,1,0:T(8,128)S(1)}, f32[32,8,192]{2,1,0:T(8,128)}, u32[]{:S(2)}) copy-start(f32[32,8,192]{2,1,0:T(8,128)} %constant.13.clone.sine_ref) | copy-start | bytes 589828
  23.3 10.7 %copy-start.3 = (f32[8,8,192]{2,1,0:T(8,128)S(1)}, f32[8,8,192]{2,1,0:T(8,128)}, u32[]{:S(2)}) copy-start(f32[8,8,192]{2,1,0:T(8,128)} %constant.15.clone.onto_ref) | copy-start | bytes 147460
  23.3 10.7 %copy-start.6 = (f32[64,192]{1,0:T(8,128)S(1)}, f32[64,192]{1,0:T(8,128)}, u32[]{:S(2)}) copy-start(f32[64,192]{1,0:T(8,128)} %constant.14.clone.inverse_ref) | copy-start | bytes 147460
  23.4 10.7 %copy-start.8 = (f32[1,3,576]{2,0,1:T(1,128)S(1)}, f32[1,3,576]{2,0,1:T(1,128)}, u32[]{:S(2)}) copy-start(f32[1,3,576]{2,0,1:T(1,128)} %param.15) | copy-start | bytes 20740
  34.1 10.0 %copy-start.5 = (f32[8,8,256]{2,1,0:T(8,128)S(1)}, f32[8,8,256]{2,1,0:T(8,128)}, u32[]{:S(2)}) copy-start(f32[8,8,256]{2,1,0:T(8,128)} %constant.16.clone.over_x_ref) | copy-start | bytes 196612
  36.2 7.8 %copy-start.4 = (f32[8,8,256]{2,1,0:T(8,128)S(1)}, f32[8,8,256]{2,1,0:T(8,128)}, u32[]{:S(2)}) copy-start(f32[8,8,256]{2,1,0:T(8,128)} %constant.17.clone.over_y_ref) | copy-start | bytes 196612

commit v9 on v8

--- a/solution.py
+++ b/solution.py
@@ -382,20 +382,23 @@
     modes = over_x_ref[0] * cells[0:1]
     for x in range(1, CG):
         modes = modes + over_x_ref[x] * cells[x : x + 1]
-    spectrum = jnp.zeros((8, NZC), F32)
+    parts = []
     for ky in range(CG):
         acc = jnp.zeros((8, NZC), F32)
         for j in range(8):
             at = G * ky + 3 * j
             acc = acc + jnp.broadcast_to(modes[:, at : at + 1], (8, NZC)) * mine_ref[j : j + 1]
         acc = acc * weigh_ref[8 * ky : 8 * ky + 8]
-        spectrum = spectrum + over_y_ref[ky, :, :NZC] * jnp.sum(acc, axis=0, keepdims=True)
+        parts.append(over_y_ref[ky, :, :NZC] * jnp.sum(acc, axis=0, keepdims=True))
+    while len(parts) > 1:
+        parts = [a + b for a, b in zip(parts[::2], parts[1::2])]
+    spectrum = parts[0]
     high, low = halves(spectrum)
     dot = functools.partial(
         lax.dot_general, dimension_numbers=(((1,), (1,)), ((), ())), preferred_element_type=F32
     )
     cells = dot(high, right_ref[0]) + (dot(high, right_ref[1]) + dot(low, right_ref[0]))
-    turn_ref[...] = jnp.concatenate([cells, jnp.zeros((120, 256), F32)], 0).T
+    turn_ref[:, :8] = cells.T
     line_ref[...] = jnp.zeros_like(line_ref)
     for j in range(CZ):
         line_ref[:, 8 * j : 8 * j + 8] = turn_ref[pl.ds(j, DOMS, stride=8), :][:, :8]

time: 65.9 us -> 65.9 us (level)
  no operation moved by 1% of the time
where the time goes in v9:
time: 65.9 us; the launch traced here: 65.7 us
  blocking collectives  57.9 us (88%)
  Pallas kernels  5.94 us (9%)
  local copies, waits for them, and re-layouts  1.04 us (2%)
  between operations  0.78 us (1%)
    all_to_all x4, blocking collectives, exchanged(): return lax.all_to_all(x, axis, split_axis=0, concat_axis=0, tiled=True)  57.9 us
    pallas_call x1, Pallas kernels, density_parts(): pl.pallas_call(density_kernel, out_shape=(jax.ShapeDtypeStruct((PLANES *...  2.16 us
    pallas_call x1, Pallas kernels, filtered_shares(): pl.pallas_call(filter_kernel, out_shape=(jax.ShapeDtypeStruct((BANDS, LOC...  1.49 us

profile of v9, /device:TPU:1, one launch (start us, length us, event | category | flops | bytes accessed | tf_op | source)
XLA Modules:
  0.0 65.7 jit_solution(4621042617569056006)
XLA Ops:
  0.6 0.0 copy-start.7
  0.6 0.0 copy-start
  0.7 0.0 copy-start.12
  0.7 0.2 matrix.1.mat_ref
  0.9 0.0 copy-start.9
  0.9 0.0 copy-start.10
  0.9 0.0 copy-start.11
  0.9 0.6 copy-done.7
  1.5 0.4 copy-done
  1.9 0.0 copy-done.12
  1.9 0.0 copy-done.9
  1.9 0.0 copy-done.10
  1.9 0.0 copy-done.11
  1.9 1.5 %filter.1 = (f32[8,16,1792]{2,1,0:T(8,128)S(1)}, f32[128,256]{1,0:T(8,128)S(1)}, s32[8,128]{1,0:T(8,128)S(1)}) custom-call(f32[16,24,576]{2,1,0:T(8,128)S(1)} %bitcast.21, f32[24,576]{1,0:T(8,128)S(1)} %bitcast.22, bf16[640,640]{1,0:T(8,128)(2,1)S(1)} %matrix.1.mat_ref, f32[1,128]{1,0:T(1,128)S(1)} %bitcast.24, s32[1,32]{1,0:T(1,128)S(1)} %bitcast.25, ...), custom_call_target="tpu_custom_call" | custom-call | tf_op jit(solution)/shard_map/filter/pallas_call | solution.py:156
  3.4 19.3 %all_to_all.20 = f32[8,16,1792]{2,1,0:T(8,128)S(1)} all-to-all(f32[8,16,1792]{2,1,0:T(8,128)S(1)} %get-tuple-element.17), channel_id=1, replica_groups=mesh['dom'=32,'band'=8] {'band'}, dimensions={0} | all-to-all | bytes 1835008 | tf_op jit(solution)/shard_map/all_to_all | solution.py:468
  22.7 0.0 copy-start.1
  22.7 0.6 gram.1
  23.3 0.0 copy-start.2
  23.3 0.0 copy-start.3
  23.3 0.0 copy-start.6
  23.4 0.0 copy-start.8
  23.4 10.7 %all_to_all.21.g_ref = f32[8,72,128]{2,1,0:T(8,128)S(1)} all-to-all(f32[8,72,128]{2,1,0:T(8,128)S(1)} %gram.1), channel_id=1, replica_groups=mesh['dom'=32,'band'=8] {'band'}, dimensions={0} | all-to-all | bytes 589824 | tf_op jit(solution)/shard_map/all_to_all | solution.py:468
  34.0 0.0 copy-done.1
  34.0 0.0 copy-done.2
  34.0 0.0 copy-done.3
  34.0 0.0 copy-done.6
  34.0 0.0 copy-done.8
  34.1 0.0 copy-start.5
  34.1 2.2 %density.1 = (f32[1728,128]{1,0:T(8,128)}, f32[8,8,128]{2,1,0:T(8,128)S(1)}, f32[3,1,576]{2,1,0:T(1,128)S(1)}, f32[8,128]{1,0:T(8,128)S(1)}, f32[8,640]{1,0:T(8,...) custom-call(f32[8,72,128]{2,1,0:T(8,128)S(1)} %all_to_all.21.g_ref, ...), custom_call_target="tpu_custom_call" | custom-call | tf_op jit(solution)/shard_map/density/pallas_call | solution.py:346
  36.2 0.0 copy-start.4
  36.2 7.8 %all_to_all.22.rows_ref = f32[8,8,128]{2,1,0:T(8,128)S(1)} all-to-all(f32[8,8,128]{2,1,0:T(8,128)S(1)} %get-tuple-element.22), channel_id=1, replica_groups=mesh['dom'=32,'band'=8] {'band'}, dimensions={0} | all-to-all | bytes 65536 | tf_op jit(solution)/shard_map/all_to_all | solution.py:468
  44.0 0.0 copy-done.5
  44.0 0.0 copy-done.4
  44.0 0.7 %share.1 = f32[32,8,128]{2,1,0:T(8,128)S(1)} custom-call(f32[8,8,128]{2,1,0:T(8,128)S(1)} %all_to_all.22.rows_ref, f32[8,640]{1,0:T(8,128)S(1)} %get-tuple-element.23.vec_ref, f32[8,192]{1,0:T(8,128)S(1)} %get-tuple-element.24.mine_ref, f32[64,192]{1,0:T(8,128)S(1)} %get-tuple-element.25.weigh_ref, bf16[2,256,192]{2,1,0:T(8,128)(2,1)S(1)} %get-tuple-element.26.right_ref, ...), custom_call_target="tpu_custom_call" | custom-call | tf_op jit(solution)/shard_map/share/pallas_call | solution.py:412
  44.7 20.1 %all_to_all.23.msg_ref = f32[32,8,128]{2,1,0:T(8,128)S(1)} all-to-all(f32[32,8,128]{2,1,0:T(8,128)S(1)} %share.1), channel_id=1, replica_groups=mesh['dom'=32,'band'=8] {'dom'}, dimensions={0} | all-to-all | bytes 262144 | tf_op jit(solution)/shard_map/all_to_all | solution.py:468
  64.9 0.8 %final.1 = (f32[3,1,576]{2,1,0:T(1,128)}, f32[6,1,8]{2,1,0:T(1,128)}) custom-call(f32[2,32,128]{2,1,0:T(8,128)S(1)} %get-tuple-element.21.side_ref, f32[32,8,128]{2,1,0:T(8,128)S(1)} %all_to_all.23.msg_ref, f32[3,1,576]{2,1,0:T(1,128)S(1)} %get-tuple-element.28.own_ref, f32[8,640]{1,0:T(8,128)S(1)} %get-tuple-element.23.vec_ref), custom_call_target="tpu_custom_call" | custom-call | tf_op jit(solution)/shard_map/final/pallas_call | solution.py:455
Async XLA Ops:
  0.6 0.8 %copy-start.7 = (f32[1,24,576]{2,1,0:T(8,128)S(1)}, f32[1,24,576]{2,1,0:T(8,128)}, u32[]{:S(2)}) copy-start(f32[1,24,576]{2,1,0:T(8,128)} %param.14) | copy-start | bytes 165892
  0.6 1.2 %copy-start = (f32[1,16,24,576]{3,2,1,0:T(8,128)S(1)}, f32[1,16,24,576]{3,2,1,0:T(8,128)}, u32[]{:S(2)}) copy-start(f32[1,16,24,576]{3,2,1,0:T(8,128)} %param.13) | copy-start | bytes 2654212
  0.7 1.2 %copy-start.12 = (s32[6]{0:T(128)S(1)}, s32[6]{0:T(128)}, u32[]{:S(2)}) copy-start(s32[6]{0:T(128)} %param.19) | copy-start | bytes 76
  0.9 1.0 %copy-start.9 = (f32[128]{0:T(128)S(1)}, f32[128]{0:T(128)}, u32[]{:S(2)}) copy-start(f32[128]{0:T(128)} %param.16) | copy-start | bytes 1540
  0.9 1.0 %copy-start.10 = (s32[32]{0:T(128)S(1)}, s32[32]{0:T(128)}, u32[]{:S(2)}) copy-start(s32[32]{0:T(128)} %param.17) | copy-start | bytes 388
  0.9 1.0 %copy-start.11 = (s32[2]{0:T(128)S(1)}, s32[2]{0:T(128)}, u32[]{:S(2)}) copy-start(s32[2]{0:T(128)} %param.18) | copy-start | bytes 28
  22.7 11.3 %copy-start.1 = (f32[640,256]{1,0:T(8,128)S(1)}, f32[640,256]{1,0:T(8,128)}, u32[]{:S(2)}) copy-start(f32[640,256]{1,0:T(8,128)} %constant.12.clone.gather_ref) | copy-start | bytes 1966084
  23.3 10.7 %copy-start.2 = (f32[32,8,192]{2,1,0:T(8,128)S(1)}, f32[32,8,192]{2,1,0:T(8,128)}, u32[]{:S(2)}) copy-start(f32[32,8,192]{2,1,0:T(8,128)} %constant.13.clone.sine_ref) | copy-start | bytes 589828
  23.3 10.7 %copy-start.3 = (f32[8,8,192]{2,1,0:T(8,128)S(1)}, f32[8,8,192]{2,1,0:T(8,128)}, u32[]{:S(2)}) copy-start(f32[8,8,192]{2,1,0:T(8,128)} %constant.15.clone.onto_ref) | copy-start | bytes 147460
  23.3 10.7 %copy-start.6 = (f32[64,192]{1,0:T(8,128)S(1)}, f32[64,192]{1,0:T(8,128)}, u32[]{:S(2)}) copy-start(f32[64,192]{1,0:T(8,128)} %constant.14.clone.inverse_ref) | copy-start | bytes 147460
  23.4 10.7 %copy-start.8 = (f32[1,3,576]{2,0,1:T(1,128)S(1)}, f32[1,3,576]{2,0,1:T(1,128)}, u32[]{:S(2)}) copy-start(f32[1,3,576]{2,0,1:T(1,128)} %param.15) | copy-start | bytes 20740
  34.1 10.0 %copy-start.5 = (f32[8,8,256]{2,1,0:T(8,128)S(1)}, f32[8,8,256]{2,1,0:T(8,128)}, u32[]{:S(2)}) copy-start(f32[8,8,256]{2,1,0:T(8,128)} %constant.16.clone.over_x_ref) | copy-start | bytes 196612
  36.2 7.8 %copy-start.4 = (f32[8,8,256]{2,1,0:T(8,128)S(1)}, f32[8,8,256]{2,1,0:T(8,128)}, u32[]{:S(2)}) copy-start(f32[8,8,256]{2,1,0:T(8,128)} %constant.17.clone.over_y_ref) | copy-start | bytes 196612
